TPU v7x, 32 devices: a whole 2x2x4 slice. The times are simulated.
32 devices in a mesh: dp: 8 (over z, y), seq: 4 (over x, core).
Axes of the slice: x: 2, y: 2, z: 4, core: 2. Of those that a mesh axis runs over, the one named last changes fastest.
Arguments:
- prompt_in: bfloat16 [16, 512, 768], P('dp', 'seq'), may hold values from -6 to 6
- cont_in: bfloat16 [16, 512, 768], P('dp', 'seq'), may hold values from -6 to 6
- enc_out: bfloat16 [16, 256, 768], P('dp', 'seq'), may hold values from -6 to 6
- prefix: int32 [16], P('dp'), may hold values from 128 to 512, as said below
- prompt_cot: bfloat16 [16, 512, 768], P('dp', 'seq'), may hold values from -6 to 6
- cont_cot: bfloat16 [16, 512, 768], P('dp', 'seq'), may hold values from -6 to 6
- self_query: bfloat16 [768, 768], P(('dp', 'seq')), may hold values from -0.21875 to 0.21875
- self_qbias: bfloat16 [768], P(('dp', 'seq')), may hold values from -1.75 to 1.75
- self_key: bfloat16 [768, 768], P(('dp', 'seq')), may hold values from -0.21875 to 0.21875
- self_value: bfloat16 [768, 768], P(('dp', 'seq')), may hold values from -0.21875 to 0.21875
- self_vbias: bfloat16 [768], P(('dp', 'seq')), may hold values from -1.75 to 1.75
- self_out: bfloat16 [768, 768], P(('dp', 'seq')), may hold values from -3.5 to 3.5
- self_obias: bfloat16 [768], P(('dp', 'seq')), may hold values from -1.75 to 1.75
- gain_one: bfloat16 [768], P(('dp', 'seq')), may hold values from 0.5 to 1.5
- shift_one: bfloat16 [768], P(('dp', 'seq')), may hold values from -1.75 to 1.75
- cross_query: bfloat16 [768, 768], P(('dp', 'seq')), may hold values from -0.21875 to 0.21875
- cross_qbias: bfloat16 [768], P(('dp', 'seq')), may hold values from -1.75 to 1.75
- cross_key: bfloat16 [768, 768], P(('dp', 'seq')), may hold values from -0.21875 to 0.21875
- cross_value: bfloat16 [768, 768], P(('dp', 'seq')), may hold values from -0.21875 to 0.21875
- cross_vbias: bfloat16 [768], P(('dp', 'seq')), may hold values from -1.75 to 1.75
- cross_out: bfloat16 [768, 768], P(('dp', 'seq')), may hold values from -3 to 3
- cross_obias: bfloat16 [768], P(('dp', 'seq')), may hold values from -1.75 to 1.75
- gain_two: bfloat16 [768], P(('dp', 'seq')), may hold values from 0.5 to 1.5
- shift_two: bfloat16 [768], P(('dp', 'seq')), may hold values from -1.75 to 1.75
- inner_mat: bfloat16 [768, 3072], P(('dp', 'seq')), may hold values from -0.21875 to 0.21875
- inner_bias: bfloat16 [3072], P(('dp', 'seq')), may hold values from -1.75 to 1.75
- outer_mat: bfloat16 [3072, 768], P(('dp', 'seq')), may hold values from -0.109375 to 0.109375
- outer_bias: bfloat16 [768], P(('dp', 'seq')), may hold values from -1.75 to 1.75
- gain_three: bfloat16 [768], P(('dp', 'seq')), may hold values from 0.5 to 1.5
- shift_three: bfloat16 [768], P(('dp', 'seq')), may hold values from -1.75 to 1.75
Outputs:
- prompt_out: bfloat16 [16, 512, 768], P('dp', 'seq')
- cont_out: bfloat16 [16, 512, 768], P('dp', 'seq')
- prompt_grad: bfloat16 [16, 512, 768], P('dp', 'seq')
- cont_grad: bfloat16 [16, 512, 768], P('dp', 'seq')
- enc_grad: bfloat16 [16, 256, 768], P('dp', 'seq')
- grad_self_query: float32 [768, 768], P(('dp', 'seq'))
- grad_self_qbias: float32 [768], P(('dp', 'seq'))
- grad_self_key: float32 [768, 768], P(('dp', 'seq'))
- grad_self_value: float32 [768, 768], P(('dp', 'seq'))
- grad_self_vbias: float32 [768], P(('dp', 'seq'))
- grad_self_out: float32 [768, 768], P(('dp', 'seq'))
- grad_self_obias: float32 [768], P(('dp', 'seq'))
- grad_gain_one: float32 [768], P(('dp', 'seq'))
- grad_shift_one: float32 [768], P(('dp', 'seq'))
- grad_cross_query: float32 [768, 768], P(('dp', 'seq'))
- grad_cross_qbias: float32 [768], P(('dp', 'seq'))
- grad_cross_key: float32 [768, 768], P(('dp', 'seq'))
- grad_cross_value: float32 [768, 768], P(('dp', 'seq'))
- grad_cross_vbias: float32 [768], P(('dp', 'seq'))
- grad_cross_out: float32 [768, 768], P(('dp', 'seq'))
- grad_cross_obias: float32 [768], P(('dp', 'seq'))
- grad_gain_two: float32 [768], P(('dp', 'seq'))
- grad_shift_two: float32 [768], P(('dp', 'seq'))
- grad_inner_mat: float32 [768, 3072], P(('dp', 'seq'))
- grad_inner_bias: float32 [3072], P(('dp', 'seq'))
- grad_outer_mat: float32 [3072, 768], P(('dp', 'seq'))
- grad_outer_bias: float32 [768], P(('dp', 'seq'))
- grad_gain_three: float32 [768], P(('dp', 'seq'))
- grad_shift_three: float32 [768], P(('dp', 'seq'))
Inputs may be any that keep to these rules, and one draw needn't show every extreme that they name: `prefix`: some group's continuation follows the whole prompt and some other group's follows its first 128 positions.
All inputs are finite; a program needn't handle non-finite values.
Results may differ from a plain program's by a relative error of at most 0.025.
Values may be sent and summed in bfloat16 or wider, within the bound.
No kernel may reach another device: no remote copies, remote signals or barrier semaphores. Data moves between devices by JAX's collectives and lax.ppermute only.
A program may use at most 256 MiB of HBM per device.

v0:
```python
import jax
import jax.numpy as jnp
from jax import lax
from jax.sharding import PartitionSpec as P

H = 12


highest = lax.Precision.HIGHEST


def matmul(left, right):
    return jnp.dot(left, right, preferred_element_type=jnp.float32)


def contract_rows(left, right):
    return lax.dot_general(
        left, right, (((0,), (0,)), ((), ())), preferred_element_type=jnp.float32
    )


def times_transpose(left, right):
    return lax.dot_general(
        left, right, (((1,), (1,)), ((), ())), preferred_element_type=jnp.float32
    )


def exact_rows(left, right):
    return lax.dot_general(
        left, right, (((0,), (0,)), ((), ())), precision=highest, preferred_element_type=jnp.float32
    )


def exact_transpose(left, right):
    return lax.dot_general(
        left, right, (((1,), (1,)), ((), ())), precision=highest, preferred_element_type=jnp.float32
    )


def column_sums(values):
    return jnp.sum(values.astype(jnp.float32), axis=0)


def widen(values):
    return values.astype(jnp.float32)


def normalize(values, gain, shift):
    centred = values - jnp.mean(values, axis=-1, keepdims=True)
    scale = lax.rsqrt(jnp.mean(centred * centred, axis=-1, keepdims=True) + 1e-05)
    return centred * scale * gain + shift


def norm_backward(values, gain, shift, upstream):
    result, pullback = jax.vjp(normalize, values, gain, shift)
    return pullback(upstream)


def gelu_exact(values):
    return jax.nn.gelu(values, approximate=False)


def split_pairs(matrix, heads):
    return matrix.reshape(matrix.shape[0], heads // 2, -1).transpose(1, 0, 2)


def join_pairs(stacked):
    return stacked.transpose(1, 0, 2).reshape(stacked.shape[1], -1)


def pair_heads(matrix):
    return matrix.reshape(matrix.shape[0], 2, matrix.shape[1] // 2)


def pair_scores(query_pair, key_pair, allowed):
    scores = jnp.einsum(
        "rhd,khd->hrk",
        pair_heads(query_pair),
        pair_heads(key_pair),
        preferred_element_type=jnp.float32,
    )
    if allowed is None:
        return scores
    return jnp.where(allowed[None], scores, -1e30)


def attend_forward(queries, keys, values, allowed, heads):

    def one_pair(items):
        query_pair, key_pair, value_pair = items
        scores = pair_scores(query_pair, key_pair, allowed)
        top = jnp.max(scores, axis=-1, keepdims=True)
        total = jnp.sum(jnp.exp(scores - top), axis=-1, keepdims=True)
        logsum = top + jnp.log(total)
        probs = jnp.exp(scores - logsum).astype(jnp.bfloat16)
        mixed = jnp.einsum(
            "hrk,khd->rhd", probs, pair_heads(value_pair), preferred_element_type=jnp.float32
        )
        return (mixed.reshape(mixed.shape[0], -1), logsum[..., 0])

    mixed, logsum = lax.map(
        one_pair,
        (split_pairs(queries, heads), split_pairs(keys, heads), split_pairs(values, heads)),
    )
    return (join_pairs(mixed).astype(jnp.bfloat16), logsum)


def attend_backward(queries, keys, values, allowed, heads, logsum, upstream):

    def one_pair(items):
        query_pair, key_pair, value_pair, logsum_pair, upstream_pair = items
        scores = pair_scores(query_pair, key_pair, allowed)
        probs = jnp.exp(scores - logsum_pair[..., None])
        mix_grad = pair_heads(upstream_pair)
        prob_grad = jnp.einsum(
            "rhd,khd->hrk", mix_grad, pair_heads(value_pair), preferred_element_type=jnp.float32
        )
        value_grad = jnp.einsum(
            "hrk,rhd->khd", probs.astype(jnp.bfloat16), mix_grad, preferred_element_type=jnp.float32
        )
        score_grad = probs * (prob_grad - jnp.sum(probs * prob_grad, axis=-1, keepdims=True))
        score_grad = score_grad.astype(jnp.bfloat16)
        query_grad = jnp.einsum(
            "hrk,khd->rhd", score_grad, pair_heads(key_pair), preferred_element_type=jnp.float32
        )
        key_grad = jnp.einsum(
            "hrk,rhd->khd", score_grad, pair_heads(query_pair), preferred_element_type=jnp.float32
        )
        return (
            query_grad.reshape(query_grad.shape[0], -1),
            key_grad.reshape(key_grad.shape[0], -1),
            value_grad.reshape(value_grad.shape[0], -1),
        )

    query_grad, key_grad, value_grad = lax.map(
        one_pair,
        (
            split_pairs(queries, heads),
            split_pairs(keys, heads),
            split_pairs(values, heads),
            logsum,
            split_pairs(upstream, heads),
        ),
    )
    return (join_pairs(query_grad), join_pairs(key_grad), join_pairs(value_grad))


def forward_pass(weights, tokens, encoder, allowed, prompt_rows, heads):
    (
        self_query,
        self_qbias,
        self_key,
        self_value,
        self_vbias,
        self_out,
        self_obias,
        gain_one,
        shift_one,
        cross_query,
        cross_qbias,
        cross_key,
        cross_value,
        cross_vbias,
        cross_out,
        cross_obias,
        gain_two,
        shift_two,
        inner_mat,
        inner_bias,
        outer_mat,
        outer_bias,
        gain_three,
        shift_three,
    ) = weights
    queries = ((matmul(tokens, self_query) + widen(self_qbias)) * 0.125).astype(jnp.bfloat16)
    keys_own = matmul(tokens, self_key).astype(jnp.bfloat16)
    values_own = (matmul(tokens, self_value) + widen(self_vbias)).astype(jnp.bfloat16)
    prompt_keys, prompt_values, cont_keys, cont_values = (
        lax.all_gather(keys_own[:prompt_rows], "seq", axis=0, tiled=True),
        lax.all_gather(values_own[:prompt_rows], "seq", axis=0, tiled=True),
        lax.all_gather(keys_own[prompt_rows:], "seq", axis=0, tiled=True),
        lax.all_gather(values_own[prompt_rows:], "seq", axis=0, tiled=True),
    )
    all_keys = jnp.concatenate([prompt_keys, cont_keys], axis=0)
    all_values = jnp.concatenate([prompt_values, cont_values], axis=0)
    mixed, logsum = attend_forward(queries, all_keys, all_values, allowed, heads)
    first_pre = widen(tokens) + matmul(mixed, self_out) + widen(self_obias)
    first = normalize(first_pre, widen(gain_one), widen(shift_one))
    first_low = first.astype(jnp.bfloat16)
    cross_queries = ((matmul(first_low, cross_query) + widen(cross_qbias)) * 0.125).astype(
        jnp.bfloat16
    )
    own_keys = matmul(encoder, cross_key).astype(jnp.bfloat16)
    own_values = (matmul(encoder, cross_value) + widen(cross_vbias)).astype(jnp.bfloat16)
    cross_keys, cross_values = (
        lax.all_gather(own_keys, "seq", axis=0, tiled=True),
        lax.all_gather(own_values, "seq", axis=0, tiled=True),
    )
    cross_mixed, cross_logsum = attend_forward(cross_queries, cross_keys, cross_values, None, heads)
    second_pre = first + matmul(cross_mixed, cross_out) + widen(cross_obias)
    second = normalize(second_pre, widen(gain_two), widen(shift_two))
    second_low = second.astype(jnp.bfloat16)
    inner = matmul(second_low, inner_mat) + widen(inner_bias)
    active = gelu_exact(inner).astype(jnp.bfloat16)
    third_pre = second + matmul(active, outer_mat) + widen(outer_bias)
    result = normalize(third_pre, widen(gain_three), widen(shift_three))
    saved = (
        queries,
        all_keys,
        all_values,
        logsum,
        mixed,
        first_pre,
        first_low,
        cross_queries,
        cross_keys,
        cross_values,
        cross_logsum,
        cross_mixed,
        second_pre,
        second_low,
        inner,
        active,
        third_pre,
        tokens,
        encoder,
    )
    return (result, saved)


def backward_pass(weights, tokens, encoder, allowed, prompt_len, heads, saved, upstream):
    (
        self_query,
        self_qbias,
        self_key,
        self_value,
        self_vbias,
        self_out,
        self_obias,
        gain_one,
        shift_one,
        cross_query,
        cross_qbias,
        cross_key,
        cross_value,
        cross_vbias,
        cross_out,
        cross_obias,
        gain_two,
        shift_two,
        inner_mat,
        inner_bias,
        outer_mat,
        outer_bias,
        gain_three,
        shift_three,
    ) = weights
    (
        queries,
        all_keys,
        all_values,
        logsum,
        mixed,
        first_pre,
        first_low,
        cross_queries,
        cross_keys,
        cross_values,
        cross_logsum,
        cross_mixed,
        second_pre,
        second_low,
        inner,
        active,
        third_pre,
        all_tokens,
        enc_rows,
    ) = saved
    third_up, gain_three_grad, shift_three_grad = norm_backward(
        third_pre, widen(gain_three), widen(shift_three), upstream
    )
    ffn_low = third_up.astype(jnp.bfloat16)
    outer_mat_grad = contract_rows(active, ffn_low)
    outer_bias_grad = column_sums(ffn_low)
    active_grad = times_transpose(ffn_low, outer_mat)
    unused, gelu_back = jax.vjp(gelu_exact, inner)
    inner_low = gelu_back(active_grad)[0].astype(jnp.bfloat16)
    inner_mat_grad = contract_rows(second_low, inner_low)
    inner_bias_grad = column_sums(inner_low)
    second_up = third_up + times_transpose(inner_low, inner_mat)
    second_grad, gain_two_grad, shift_two_grad = norm_backward(
        second_pre, widen(gain_two), widen(shift_two), second_up
    )
    cross_low = second_grad.astype(jnp.bfloat16)
    cross_out_grad = contract_rows(cross_mixed, cross_low)
    cross_obias_grad = column_sums(cross_low)
    cross_mix_grad = times_transpose(cross_low, cross_out).astype(jnp.bfloat16)
    cross_query_part, cross_key_part, cross_value_part = attend_backward(
        cross_queries, cross_keys, cross_values, None, heads, cross_logsum, cross_mix_grad
    )
    cross_key_own, cross_value_own = (
        lax.psum_scatter(
            cross_key_part.astype(jnp.bfloat16), "seq", scatter_dimension=0, tiled=True
        ).astype(jnp.float32),
        lax.psum_scatter(
            cross_value_part.astype(jnp.bfloat16), "seq", scatter_dimension=0, tiled=True
        ).astype(jnp.float32),
    )
    wide_rows = widen(encoder)
    cross_key_grad = exact_rows(wide_rows, cross_key_own)
    cross_value_grad = exact_rows(wide_rows, cross_value_own)
    cross_vbias_grad = jnp.sum(cross_value_own, axis=0)
    encoder_grad = (
        exact_transpose(cross_key_own, widen(cross_key))
        + exact_transpose(cross_value_own, widen(cross_value))
    ).astype(jnp.bfloat16)
    cross_query_low = cross_query_part.astype(jnp.bfloat16)
    cross_query_grad = contract_rows(first_low, cross_query_low) * 0.125
    cross_qbias_grad = column_sums(cross_query_low) * 0.125
    first_up = second_grad + times_transpose(cross_query_low, cross_query) * 0.125
    first_grad, gain_one_grad, shift_one_grad = norm_backward(
        first_pre, widen(gain_one), widen(shift_one), first_up
    )
    self_low = first_grad.astype(jnp.bfloat16)
    self_out_grad = contract_rows(mixed, self_low)
    self_obias_grad = column_sums(self_low)
    mix_grad = times_transpose(self_low, self_out).astype(jnp.bfloat16)
    query_part, key_part, value_part = attend_backward(
        queries, all_keys, all_values, allowed, heads, logsum, mix_grad
    )
    prompt_key_own, prompt_value_own, cont_key_own, cont_value_own = (
        lax.psum_scatter(
            key_part[:prompt_len].astype(jnp.bfloat16), "seq", scatter_dimension=0, tiled=True
        ).astype(jnp.float32),
        lax.psum_scatter(
            value_part[:prompt_len].astype(jnp.bfloat16), "seq", scatter_dimension=0, tiled=True
        ).astype(jnp.float32),
        lax.psum_scatter(
            key_part[prompt_len:].astype(jnp.bfloat16), "seq", scatter_dimension=0, tiled=True
        ).astype(jnp.float32),
        lax.psum_scatter(
            value_part[prompt_len:].astype(jnp.bfloat16), "seq", scatter_dimension=0, tiled=True
        ).astype(jnp.float32),
    )
    key_own = jnp.concatenate([prompt_key_own, cont_key_own], axis=0)
    value_own = jnp.concatenate([prompt_value_own, cont_value_own], axis=0)
    wide_tokens = widen(tokens)
    self_key_grad = exact_rows(wide_tokens, key_own)
    self_value_grad = exact_rows(wide_tokens, value_own)
    self_vbias_grad = jnp.sum(value_own, axis=0)
    key_side = exact_transpose(key_own, widen(self_key)) + exact_transpose(
        value_own, widen(self_value)
    )
    query_low = query_part.astype(jnp.bfloat16)
    self_query_grad = contract_rows(tokens, query_low) * 0.125
    self_qbias_grad = column_sums(query_low) * 0.125
    token_grad = first_grad + times_transpose(query_low, self_query) * 0.125 + key_side
    grads = (
        self_query_grad,
        self_qbias_grad,
        self_key_grad,
        self_value_grad,
        self_vbias_grad,
        self_out_grad,
        self_obias_grad,
        gain_one_grad,
        shift_one_grad,
        cross_query_grad,
        cross_qbias_grad,
        cross_key_grad,
        cross_value_grad,
        cross_vbias_grad,
        cross_out_grad,
        cross_obias_grad,
        gain_two_grad,
        shift_two_grad,
        inner_mat_grad,
        inner_bias_grad,
        outer_mat_grad,
        outer_bias_grad,
        gain_three_grad,
        shift_three_grad,
    )
    return (token_grad.astype(jnp.bfloat16), encoder_grad, grads)


def body(
    prompt_in,
    cont_in,
    enc_out,
    prefix,
    prompt_cot,
    cont_cot,
    self_query,
    self_qbias,
    self_key,
    self_value,
    self_vbias,
    self_out,
    self_obias,
    gain_one,
    shift_one,
    cross_query,
    cross_qbias,
    cross_key,
    cross_value,
    cross_vbias,
    cross_out,
    cross_obias,
    gain_two,
    shift_two,
    inner_mat,
    inner_bias,
    outer_mat,
    outer_bias,
    gain_three,
    shift_three,
):
    heads = H
    seq_index = lax.axis_index("seq")
    parts = lax.axis_size("seq")
    blocks = lax.axis_size("dp")
    prompt_rows = prompt_in.shape[1]
    cont_rows = cont_in.shape[1]
    prompt_len = prompt_rows * parts
    cont_len = cont_rows * parts
    row_ids = jnp.arange(prompt_rows + cont_rows, dtype=jnp.int32)
    is_prompt = row_ids < prompt_rows
    position = jnp.where(
        is_prompt, seq_index * prompt_rows + row_ids, seq_index * cont_rows + row_ids - prompt_rows
    )
    key_ids = jnp.arange(prompt_len + cont_len, dtype=jnp.int32)
    key_prompt = key_ids < prompt_len
    key_position = jnp.where(key_prompt, key_ids, key_ids - prompt_len)
    causal = key_position[None, :] <= position[:, None]
    prompt_outs, cont_outs, prompt_grads, cont_grads, enc_grads = ([], [], [], [], [])
    totals = None
    for group in range(prompt_in.shape[0]):
        gathered = (
            lax.all_gather(self_query, ("dp", "seq"), axis=0, tiled=True),
            lax.all_gather(self_qbias, ("dp", "seq"), axis=0, tiled=True),
            lax.all_gather(self_key, ("dp", "seq"), axis=0, tiled=True),
            lax.all_gather(self_value, ("dp", "seq"), axis=0, tiled=True),
            lax.all_gather(self_vbias, ("dp", "seq"), axis=0, tiled=True),
            lax.all_gather(self_out, ("dp", "seq"), axis=0, tiled=True),
            lax.all_gather(self_obias, ("dp", "seq"), axis=0, tiled=True),
            lax.all_gather(gain_one, ("dp", "seq"), axis=0, tiled=True),
            lax.all_gather(shift_one, ("dp", "seq"), axis=0, tiled=True),
            lax.all_gather(cross_query, ("dp", "seq"), axis=0, tiled=True),
            lax.all_gather(cross_qbias, ("dp", "seq"), axis=0, tiled=True),
            lax.all_gather(cross_key, ("dp", "seq"), axis=0, tiled=True),
            lax.all_gather(cross_value, ("dp", "seq"), axis=0, tiled=True),
            lax.all_gather(cross_vbias, ("dp", "seq"), axis=0, tiled=True),
            lax.all_gather(cross_out, ("dp", "seq"), axis=0, tiled=True),
            lax.all_gather(cross_obias, ("dp", "seq"), axis=0, tiled=True),
            lax.all_gather(gain_two, ("dp", "seq"), axis=0, tiled=True),
            lax.all_gather(shift_two, ("dp", "seq"), axis=0, tiled=True),
            lax.all_gather(inner_mat, ("dp", "seq"), axis=0, tiled=True),
            lax.all_gather(inner_bias, ("dp", "seq"), axis=0, tiled=True),
            lax.all_gather(outer_mat, ("dp", "seq"), axis=0, tiled=True),
            lax.all_gather(outer_bias, ("dp", "seq"), axis=0, tiled=True),
            lax.all_gather(gain_three, ("dp", "seq"), axis=0, tiled=True),
            lax.all_gather(shift_three, ("dp", "seq"), axis=0, tiled=True),
        )
        tokens = jnp.concatenate([prompt_in[group], cont_in[group]], axis=0)
        encoder = enc_out[group]
        offset = prefix[group]
        allowed = jnp.where(
            is_prompt[:, None],
            key_prompt[None, :] & causal,
            key_prompt[None, :] & (key_ids[None, :] < offset)
            | jnp.logical_not(key_prompt)[None, :] & causal,
        )
        result, saved = forward_pass(gathered, tokens, encoder, allowed, prompt_rows, heads)
        prompt_outs.append(result[:prompt_rows].astype(jnp.bfloat16))
        cont_outs.append(result[prompt_rows:].astype(jnp.bfloat16))
        gathered = (
            lax.all_gather(self_query, ("dp", "seq"), axis=0, tiled=True),
            lax.all_gather(self_qbias, ("dp", "seq"), axis=0, tiled=True),
            lax.all_gather(self_key, ("dp", "seq"), axis=0, tiled=True),
            lax.all_gather(self_value, ("dp", "seq"), axis=0, tiled=True),
            lax.all_gather(self_vbias, ("dp", "seq"), axis=0, tiled=True),
            lax.all_gather(self_out, ("dp", "seq"), axis=0, tiled=True),
            lax.all_gather(self_obias, ("dp", "seq"), axis=0, tiled=True),
            lax.all_gather(gain_one, ("dp", "seq"), axis=0, tiled=True),
            lax.all_gather(shift_one, ("dp", "seq"), axis=0, tiled=True),
            lax.all_gather(cross_query, ("dp", "seq"), axis=0, tiled=True),
            lax.all_gather(cross_qbias, ("dp", "seq"), axis=0, tiled=True),
            lax.all_gather(cross_key, ("dp", "seq"), axis=0, tiled=True),
            lax.all_gather(cross_value, ("dp", "seq"), axis=0, tiled=True),
            lax.all_gather(cross_vbias, ("dp", "seq"), axis=0, tiled=True),
            lax.all_gather(cross_out, ("dp", "seq"), axis=0, tiled=True),
            lax.all_gather(cross_obias, ("dp", "seq"), axis=0, tiled=True),
            lax.all_gather(gain_two, ("dp", "seq"), axis=0, tiled=True),
            lax.all_gather(shift_two, ("dp", "seq"), axis=0, tiled=True),
            lax.all_gather(inner_mat, ("dp", "seq"), axis=0, tiled=True),
            lax.all_gather(inner_bias, ("dp", "seq"), axis=0, tiled=True),
            lax.all_gather(outer_mat, ("dp", "seq"), axis=0, tiled=True),
            lax.all_gather(outer_bias, ("dp", "seq"), axis=0, tiled=True),
            lax.all_gather(gain_three, ("dp", "seq"), axis=0, tiled=True),
            lax.all_gather(shift_three, ("dp", "seq"), axis=0, tiled=True),
        )
        upstream = jnp.concatenate([prompt_cot[group], cont_cot[group]], axis=0).astype(jnp.float32)
        token_grad, encoder_grad, grads = backward_pass(
            gathered, tokens, encoder, allowed, prompt_len, heads, saved, upstream
        )
        prompt_grads.append(token_grad[:prompt_rows])
        cont_grads.append(token_grad[prompt_rows:])
        enc_grads.append(encoder_grad)
        if totals is None:
            totals = grads
        else:
            totals = tuple((first + second for first, second in zip(totals, grads)))
    pieces = [item.reshape(blocks, parts, item.shape[0] // (blocks * parts), -1) for item in totals]
    swapped = (
        lax.all_to_all(
            pieces[0].astype(jnp.bfloat16), "seq", split_axis=1, concat_axis=1, tiled=True
        ).astype(jnp.float32),
        lax.all_to_all(
            pieces[1].astype(jnp.bfloat16), "seq", split_axis=1, concat_axis=1, tiled=True
        ).astype(jnp.float32),
        lax.all_to_all(
            pieces[2].astype(jnp.bfloat16), "seq", split_axis=1, concat_axis=1, tiled=True
        ).astype(jnp.float32),
        lax.all_to_all(
            pieces[3].astype(jnp.bfloat16), "seq", split_axis=1, concat_axis=1, tiled=True
        ).astype(jnp.float32),
        lax.all_to_all(
            pieces[4].astype(jnp.bfloat16), "seq", split_axis=1, concat_axis=1, tiled=True
        ).astype(jnp.float32),
        lax.all_to_all(
            pieces[5].astype(jnp.bfloat16), "seq", split_axis=1, concat_axis=1, tiled=True
        ).astype(jnp.float32),
        lax.all_to_all(
            pieces[6].astype(jnp.bfloat16), "seq", split_axis=1, concat_axis=1, tiled=True
        ).astype(jnp.float32),
        lax.all_to_all(
            pieces[7].astype(jnp.bfloat16), "seq", split_axis=1, concat_axis=1, tiled=True
        ).astype(jnp.float32),
        lax.all_to_all(
            pieces[8].astype(jnp.bfloat16), "seq", split_axis=1, concat_axis=1, tiled=True
        ).astype(jnp.float32),
        lax.all_to_all(
            pieces[9].astype(jnp.bfloat16), "seq", split_axis=1, concat_axis=1, tiled=True
        ).astype(jnp.float32),
        lax.all_to_all(
            pieces[10].astype(jnp.bfloat16), "seq", split_axis=1, concat_axis=1, tiled=True
        ).astype(jnp.float32),
        lax.all_to_all(
            pieces[11].astype(jnp.bfloat16), "seq", split_axis=1, concat_axis=1, tiled=True
        ).astype(jnp.float32),
        lax.all_to_all(
            pieces[12].astype(jnp.bfloat16), "seq", split_axis=1, concat_axis=1, tiled=True
        ).astype(jnp.float32),
        lax.all_to_all(
            pieces[13].astype(jnp.bfloat16), "seq", split_axis=1, concat_axis=1, tiled=True
        ).astype(jnp.float32),
        lax.all_to_all(
            pieces[14].astype(jnp.bfloat16), "seq", split_axis=1, concat_axis=1, tiled=True
        ).astype(jnp.float32),
        lax.all_to_all(
            pieces[15].astype(jnp.bfloat16), "seq", split_axis=1, concat_axis=1, tiled=True
        ).astype(jnp.float32),
        lax.all_to_all(
            pieces[16].astype(jnp.bfloat16), "seq", split_axis=1, concat_axis=1, tiled=True
        ).astype(jnp.float32),
        lax.all_to_all(
            pieces[17].astype(jnp.bfloat16), "seq", split_axis=1, concat_axis=1, tiled=True
        ).astype(jnp.float32),
        lax.all_to_all(
            pieces[18].astype(jnp.bfloat16), "seq", split_axis=1, concat_axis=1, tiled=True
        ).astype(jnp.float32),
        lax.all_to_all(
            pieces[19].astype(jnp.bfloat16), "seq", split_axis=1, concat_axis=1, tiled=True
        ).astype(jnp.float32),
        lax.all_to_all(
            pieces[20].astype(jnp.bfloat16), "seq", split_axis=1, concat_axis=1, tiled=True
        ).astype(jnp.float32),
        lax.all_to_all(
            pieces[21].astype(jnp.bfloat16), "seq", split_axis=1, concat_axis=1, tiled=True
        ).astype(jnp.float32),
        lax.all_to_all(
            pieces[22].astype(jnp.bfloat16), "seq", split_axis=1, concat_axis=1, tiled=True
        ).astype(jnp.float32),
        lax.all_to_all(
            pieces[23].astype(jnp.bfloat16), "seq", split_axis=1, concat_axis=1, tiled=True
        ).astype(jnp.float32),
    )
    partial_value = [jnp.sum(item, axis=1) for item in swapped]
    reduced = (
        lax.psum_scatter(partial_value[0], "dp", scatter_dimension=0, tiled=True),
        lax.psum_scatter(partial_value[1], "dp", scatter_dimension=0, tiled=True),
        lax.psum_scatter(partial_value[2], "dp", scatter_dimension=0, tiled=True),
        lax.psum_scatter(partial_value[3], "dp", scatter_dimension=0, tiled=True),
        lax.psum_scatter(partial_value[4], "dp", scatter_dimension=0, tiled=True),
        lax.psum_scatter(partial_value[5], "dp", scatter_dimension=0, tiled=True),
        lax.psum_scatter(partial_value[6], "dp", scatter_dimension=0, tiled=True),
        lax.psum_scatter(partial_value[7], "dp", scatter_dimension=0, tiled=True),
        lax.psum_scatter(partial_value[8], "dp", scatter_dimension=0, tiled=True),
        lax.psum_scatter(partial_value[9], "dp", scatter_dimension=0, tiled=True),
        lax.psum_scatter(partial_value[10], "dp", scatter_dimension=0, tiled=True),
        lax.psum_scatter(partial_value[11], "dp", scatter_dimension=0, tiled=True),
        lax.psum_scatter(partial_value[12], "dp", scatter_dimension=0, tiled=True),
        lax.psum_scatter(partial_value[13], "dp", scatter_dimension=0, tiled=True),
        lax.psum_scatter(partial_value[14], "dp", scatter_dimension=0, tiled=True),
        lax.psum_scatter(partial_value[15], "dp", scatter_dimension=0, tiled=True),
        lax.psum_scatter(partial_value[16], "dp", scatter_dimension=0, tiled=True),
        lax.psum_scatter(partial_value[17], "dp", scatter_dimension=0, tiled=True),
        lax.psum_scatter(partial_value[18], "dp", scatter_dimension=0, tiled=True),
        lax.psum_scatter(partial_value[19], "dp", scatter_dimension=0, tiled=True),
        lax.psum_scatter(partial_value[20], "dp", scatter_dimension=0, tiled=True),
        lax.psum_scatter(partial_value[21], "dp", scatter_dimension=0, tiled=True),
        lax.psum_scatter(partial_value[22], "dp", scatter_dimension=0, tiled=True),
        lax.psum_scatter(partial_value[23], "dp", scatter_dimension=0, tiled=True),
    )
    owned = tuple((piece.reshape((-1,) + whole.shape[1:]) for piece, whole in zip(reduced, totals)))
    return (
        jnp.stack(prompt_outs),
        jnp.stack(cont_outs),
        jnp.stack(prompt_grads),
        jnp.stack(cont_grads),
        jnp.stack(enc_grads),
    ) + owned


def solution(mesh):
    in_specs = (
        P("dp", "seq", None),
        P("dp", "seq", None),
        P("dp", "seq", None),
        P("dp"),
        P("dp", "seq", None),
        P("dp", "seq", None),
        P(("dp", "seq"), None),
        P(("dp", "seq")),
        P(("dp", "seq"), None),
        P(("dp", "seq"), None),
        P(("dp", "seq")),
        P(("dp", "seq"), None),
        P(("dp", "seq")),
        P(("dp", "seq")),
        P(("dp", "seq")),
        P(("dp", "seq"), None),
        P(("dp", "seq")),
        P(("dp", "seq"), None),
        P(("dp", "seq"), None),
        P(("dp", "seq")),
        P(("dp", "seq"), None),
        P(("dp", "seq")),
        P(("dp", "seq")),
        P(("dp", "seq")),
        P(("dp", "seq"), None),
        P(("dp", "seq")),
        P(("dp", "seq"), None),
        P(("dp", "seq")),
        P(("dp", "seq")),
        P(("dp", "seq")),
    )
    out_specs = (
        P("dp", "seq", None),
        P("dp", "seq", None),
        P("dp", "seq", None),
        P("dp", "seq", None),
        P("dp", "seq", None),
        P(("dp", "seq"), None),
        P(("dp", "seq")),
        P(("dp", "seq"), None),
        P(("dp", "seq"), None),
        P(("dp", "seq")),
        P(("dp", "seq"), None),
        P(("dp", "seq")),
        P(("dp", "seq")),
        P(("dp", "seq")),
        P(("dp", "seq"), None),
        P(("dp", "seq")),
        P(("dp", "seq"), None),
        P(("dp", "seq"), None),
        P(("dp", "seq")),
        P(("dp", "seq"), None),
        P(("dp", "seq")),
        P(("dp", "seq")),
        P(("dp", "seq")),
        P(("dp", "seq"), None),
        P(("dp", "seq")),
        P(("dp", "seq"), None),
        P(("dp", "seq")),
        P(("dp", "seq")),
        P(("dp", "seq")),
    )
    return jax.shard_map(body, mesh=mesh, in_specs=in_specs, out_specs=out_specs, check_vma=False)
```

profile of v0, /device:TPU:0, one launch (start us, length us, event | category | flops | bytes accessed | tf_op | source)
XLA Modules:
  0.0 1722.2 jit_solution(10651931851820663047)
XLA Ops:
  26.3 42.6 %all-reduce.29 = (bf16[3072]{0:T(1024)(128)(2,1)S(1)}, bf16[768]{0:T(1024)(128)(2,1)S(1)}, bf16[768]{0:T(1024)(128)(2,1)S(1)}, bf16[768]{0:T(1024)(128)(2,1)S(1)...) all-reduce(bf16[3072]{0:T(1024)(128)(2,1)S(1)} %dynamic-update-slic, ...), channel_id=1, replica_groups=mesh['dp'=8,'seq'=4] {'dp','seq'}, use_global_device_ids=true, to_apply=%add.10 | all-reduce | flops 13056 | bytes 52224
  83.8 7.2 all_gather.173
  91.9 31.8 %all-gather.11.cloned.1.call-done = bf16[768,768]{1,0:T(8,128)(2,1)} async-done(((bf16[24,768]{1,0:T(8,128)(2,1)}), bf16[768,768]{1,0:T(8,128)(2,1)}) %all-gather.11.cloned.1.call-update) | async-done | bytes 1179664 | tf_op jit(solution)/shard_map/all_gather | solution.py:443
  125.6 8.6 all_gather.75
  134.2 8.7 all_gather.74
  143.8 35.9 %all-gather.13.cloned.1.call-done = bf16[768,768]{1,0:T(8,128)(2,1)} async-done(((bf16[24,768]{1,0:T(8,128)(2,1)}), bf16[768,768]{1,0:T(8,128)(2,1)}) %all-gather.13.cloned.1.call-update) | async-done | bytes 1179664 | tf_op jit(solution)/shard_map/all_gather | solution.py:440
  182.5 52.9 %all-gather.15.cloned.1.call-done = bf16[768,768]{1,0:T(8,128)(2,1)} async-done(((bf16[24,768]{1,0:T(8,128)(2,1)}), bf16[768,768]{1,0:T(8,128)(2,1)}) %all-gather.15.cloned.1.call-update) | async-done | bytes 1179664 | tf_op jit(solution)/shard_map/all_gather | solution.py:442
  237.2 8.6 all_gather.80
  245.9 9.0 all_gather.79
  259.2 30.2 %while.112 = (s32[]{:T(128)}, bf16[6,256,128]{1,2,0:T(8,128)(2,1)}, f32[6,2,256]{2,1,0:T(2,128)}, bf16[6,1024,128]{1,2,0:T(8,128)(2,1)S(1)}, bf16[6,256,128]{1,2...) while((s32[]{:T(128)}, bf16[6,256,128]{1,2,0:T(8,128)(2,1)}, ...), condition=%wide.region_3.4_spmd.clone, body=%wide.region_0.3_spmd.clone.sunk | while | flops 139722240 | bytes 9331093 | solution.py:101
  294.1 52.8 %all-gather.21.cloned.1.call-done = bf16[768,768]{1,0:T(8,128)(2,1)} async-done(((bf16[24,768]{1,0:T(8,128)(2,1)}), bf16[768,768]{1,0:T(8,128)(2,1)}) %all-gather.21.cloned.1.call-update) | async-done | bytes 1179664 | tf_op jit(solution)/shard_map/all_gather | solution.py:449
  349.7 53.1 %all-gather.23.cloned.1.call-done = bf16[768,768]{1,0:T(8,128)(2,1)} async-done(((bf16[24,768]{1,0:T(8,128)(2,1)}), bf16[768,768]{1,0:T(8,128)(2,1)}) %all-gather.23.cloned.1.call-update) | async-done | bytes 1179664 | tf_op jit(solution)/shard_map/all_gather | solution.py:451
  404.5 6.5 all_gather.177
  411.9 14.3 while.108
  426.3 32.5 %all-gather.25.cloned.1.call-done = bf16[768,768]{1,0:T(8,128)(2,1)} async-done(((bf16[24,768]{1,0:T(8,128)(2,1)}), bf16[768,768]{1,0:T(8,128)(2,1)}) %all-gather.25.cloned.1.call-update) | async-done | bytes 1179664 | tf_op jit(solution)/shard_map/all_gather | solution.py:454
  462.6 6.5 all_gather.192
  471.2 8.7 all_gather.189
  480.0 8.7 all_gather.188
  497.9 9.7 all_gather.191
  507.6 12.7 all_gather.190
  525.5 35.8 %while.113 = (s32[]{:T(128)}, bf16[6,256,128]{1,2,0:T(8,128)(2,1)}, f32[6,2,256]{2,1,0:T(2,128)}, bf16[6,1024,128]{1,2,0:T(8,128)(2,1)S(1)}, bf16[6,256,128]{1,2...) while((s32[]{:T(128)}, bf16[6,256,128]{1,2,0:T(8,128)(2,1)}, ...), condition=%wide.region_17.18_spmd.clone, body=%wide.region_14.17_spmd.clone.sunk | while | flops 139722240 | bytes 9331093 | solution.py:101
  570.2 6.7 all_gather.193
  579.2 14.3 while.109
  598.1 11.8 multiply_convert_fusion.5
  614.7 8.1 multiply_convert_fusion.4
  658.1 39.6 %while.110 = (s32[]{:T(128)}, bf16[6,256,128]{1,2,0:T(8,128)(2,1)}, bf16[6,256,128]{1,2,0:T(8,128)(2,1)}, bf16[6,256,128]{1,2,0:T(8,128)(2,1)}, bf16[6,256,128]{...) while((s32[]{:T(128)}, bf16[6,256,128]{1,2,0:T(8,128)(2,1)}, ...), condition=%wide.region_34.35_spmd, body=%wide.region_32.34_spmd.sunk | while | flops 84803072 | bytes 5515401 | solution.py:135
  702.0 39.7 %while.111 = (s32[]{:T(128)}, bf16[6,256,128]{1,2,0:T(8,128)(2,1)}, bf16[6,256,128]{1,2,0:T(8,128)(2,1)}, bf16[6,256,128]{1,2,0:T(8,128)(2,1)}, bf16[6,256,128]{...) while((s32[]{:T(128)}, bf16[6,256,128]{1,2,0:T(8,128)(2,1)}, ...), condition=%wide.region_50.51_spmd, body=%wide.region_48.50_spmd.sunk | while | flops 84803072 | bytes 5515401 | solution.py:135
  764.7 53.7 %while.115 = (s32[]{:T(128)}, bf16[6,256,128]{1,2,0:T(8,128)(2,1)}, bf16[6,1024,128]{1,2,0:T(8,128)(2,1)}, bf16[6,1024,128]{1,2,0:T(8,128)(2,1)}, bf16[6,1024,12...) while((s32[]{:T(128)}, bf16[6,256,128]{1,2,0:T(8,128)(2,1)}, ...), condition=%wide.region_55.56_spmd.clone, body=%wide.region_53.55_spmd.clone.sunk | while | flops 341048832 | bytes 20405744 | solution.py:135
  832.1 49.7 %while.114 = (s32[]{:T(128)}, bf16[6,256,128]{1,2,0:T(8,128)(2,1)S(1)}, bf16[6,1024,128]{1,2,0:T(8,128)(2,1)}, bf16[6,1024,128]{1,2,0:T(8,128)(2,1)}, bf16[6,102...) while((s32[]{:T(128)}, ...), condition=%wide.region_39.40_spmd.clone, body=%wide.region_37.39_spmd.clone.sunk | while | flops 341048832 | bytes 20400568 | solution.py:135
  986.5 12.7 all-to-all-done
  1008.4 15.2 all-to-all-done.5
  1034.7 13.2 all-to-all-done.9
  1056.1 12.0 all-to-all-done.14
  1078.7 9.6 all-to-all-done.11
  1101.6 6.1 all-to-all-done.12
  1139.8 8.5 all-to-all-done.3
  1148.3 4.9 all-to-all-start.18
  1161.4 5.1 fusion.203
  1166.5 40.6 %all-to-all-done.18 = bf16[8,4,24,3072]{3,2,0,1:T(8,128)(2,1)} async-done(((bf16[8,4,24,3072]{3,2,0,1:T(8,128)(2,1)}), bf16[8,4,24,3072]{3,2,0,1:T(8,128)(2,1)}, u32[]{:S(2)}, u32[]{:S(2)}) %all-to-all-start.18) | async-done | bytes 4718624 | tf_op jit(solution)/shard_map/all_to_all | solution.py:570
  1226.2 5.1 add_convert_fusion
  1233.9 5.1 all-to-all-start.20
  1257.6 35.2 %all-to-all-done.20 = bf16[8,4,96,768]{3,2,0,1:T(8,128)(2,1)} async-done(((bf16[8,4,96,768]{3,2,0,1:T(8,128)(2,1)}), bf16[8,4,96,768]{3,2,0,1:T(8,128)(2,1)}, u32[]{:S(2)}, u32[]{:S(2)}) %all-to-all-start.20) | async-done | bytes 4718624 | tf_op jit(solution)/shard_map/all_to_all | solution.py:576
  1323.1 37.2 %all-reduce.28 = (f32[8,24,1]{1,2,0:T(1,128)S(1)}, f32[8,24,1]{1,2,0:T(1,128)S(1)}, f32[8,24,1]{1,2,0:T(1,128)S(1)}, f32[8,24,1]{1,2,0:T(1,128)S(1)}, f32[8,24,1...) all-reduce(f32[8,24,1]{1,2,0:T(1,128)S(1)} %bitcast.771, ...), channel_id=15, replica_groups=mesh['dp'=8,'seq'=4] {'dp'}, use_global_device_ids=true, to_apply=%region_69.70.clone | all-reduce | flops 3264 | bytes 26112
  1376.3 64.2 %reduce-scatter.59.cloned.1.call-done = f32[1,24,768]{2,1,0:T(8,128)} async-done(((f32[8,24,768]{2,1,0:T(8,128)}), f32[1,24,768]{2,1,0:T(8,128)}) %reduce-scatter.59.cloned.1.call-update) | async-done | bytes 73744 | tf_op jit(solution)/shard_map/reduce_scatter | solution.py:603
  1440.4 65.1 %reduce-scatter.49.cloned.1.call-done = f32[1,24,768]{2,1,0:T(8,128)} async-done(((f32[8,24,768]{2,1,0:T(8,128)}), f32[1,24,768]{2,1,0:T(8,128)}) %reduce-scatter.49.cloned.1.call-update) | async-done | bytes 73744 | tf_op jit(solution)/shard_map/reduce_scatter | solution.py:593
  1505.5 65.3 %reduce-scatter.51.cloned.1.call-done = f32[1,24,768]{2,1,0:T(8,128)} async-done(((f32[8,24,768]{2,1,0:T(8,128)}), f32[1,24,768]{2,1,0:T(8,128)}) %reduce-scatter.51.cloned.1.call-update) | async-done | bytes 73744 | tf_op jit(solution)/shard_map/reduce_scatter | solution.py:594
  1570.8 72.4 %reduce-scatter.63.cloned.1.call-done = f32[1,24,3072]{2,1,0:T(8,128)} async-done(((f32[8,24,3072]{2,1,0:T(8,128)}), f32[1,24,3072]{2,1,0:T(8,128)}) %reduce-scatter.63.cloned.1.call-update) | async-done | bytes 294928 | tf_op jit(solution)/shard_map/reduce_scatter | solution.py:609
  1643.1 72.3 %reduce-scatter.65.cloned.1.call-done = f32[1,96,768]{2,1,0:T(8,128)} async-done(((f32[8,96,768]{2,1,0:T(8,128)}), f32[1,96,768]{2,1,0:T(8,128)}) %reduce-scatter.65.cloned.1.call-update) | async-done | bytes 294928 | tf_op jit(solution)/shard_map/reduce_scatter | solution.py:611
  (1328 shorter events, 730.4 us)
Async XLA Ops:
  7.2 74.9 %all-gather.19.cloned.1.call-start = ((), (), s32[]{:S(2)}) async-start(), calls=%async_computation.50 | async-start | bytes 1216512 | tf_op jit(solution)/shard_map/all_gather | solution.py:452
  8.0 115.8 %all-gather.11.cloned.1.call-start = ((), (), s32[]{:S(2)}) async-start(), calls=%async_computation.46 | async-start | bytes 1216512 | tf_op jit(solution)/shard_map/all_gather | solution.py:443
  8.7 170.9 %all-gather.13.cloned.1.call-start = ((), (), s32[]{:S(2)}) async-start(), calls=%async_computation.47 | async-start | bytes 1216512 | tf_op jit(solution)/shard_map/all_gather | solution.py:440
  9.5 226.0 %all-gather.15.cloned.1.call-start = ((), (), s32[]{:S(2)}) async-start(), calls=%async_computation.48 | async-start | bytes 1216512 | tf_op jit(solution)/shard_map/all_gather | solution.py:442
  10.0 281.2 %all-gather.17.cloned.1.call-start = ((), (), s32[]{:S(2)}) async-start(), calls=%async_computation.49 | async-start | bytes 1216512 | tf_op jit(solution)/shard_map/all_gather | solution.py:445
  10.6 336.3 %all-gather.21.cloned.1.call-start = ((), (), s32[]{:S(2)}) async-start(), calls=%async_computation.51 | async-start | bytes 1216512 | tf_op jit(solution)/shard_map/all_gather | solution.py:449
  11.2 391.6 %all-gather.23.cloned.1.call-start = ((), (), s32[]{:S(2)}) async-start(), calls=%async_computation.52 | async-start | bytes 1216512 | tf_op jit(solution)/shard_map/all_gather | solution.py:451
  11.9 446.8 %all-gather.25.cloned.1.call-start = ((), (), s32[]{:S(2)}) async-start(), calls=%async_computation.53 | async-start | bytes 1216512 | tf_op jit(solution)/shard_map/all_gather | solution.py:454
  12.7 585.4 %all-gather.27.cloned.1.call-start = ((), (), s32[]{:S(2)}) async-start(), calls=%async_computation.54 | async-start | bytes 4866048 | tf_op jit(solution)/shard_map/all_gather | solution.py:458
  13.4 596.4 %all-gather.29.cloned.1.call-start = ((), (), s32[]{:S(2)}) async-start(), calls=%async_computation.55 | async-start | bytes 4866048 | tf_op jit(solution)/shard_map/all_gather | solution.py:460
  14.0 1038.2 %reduce-scatter.83.cloned.1.call-start = ((), (), s32[]{:S(2)}) async-start(), calls=%async_computation.74 | async-start | bytes 491520
  699.6 354.0 %reduce-scatter.87.cloned.1.call-start = ((), (), s32[]{:S(2)}) async-start(), calls=%async_computation.76 | async-start | bytes 491520
  745.7 329.0 %reduce-scatter.85.cloned.1.call-start = ((), (), s32[]{:S(2)}) async-start(), calls=%async_computation.75 | async-start | bytes 491520
  751.6 324.6 %reduce-scatter.89.cloned.1.call-start = ((), (), s32[]{:S(2)}) async-start(), calls=%async_computation.77 | async-start | bytes 491520
  761.1 333.4 %reduce-scatter.77.cloned.1.call-start = ((), (), s32[]{:S(2)}) async-start(), calls=%async_computation.71 | async-start | bytes 983040
  823.3 272.4 %reduce-scatter.75.cloned.1.call-start = ((), (), s32[]{:S(2)}) async-start(), calls=%async_computation.70 | async-start | bytes 983040
  829.3 267.6 %reduce-scatter.69.cloned.1.call-start = ((), (), s32[]{:S(2)}) async-start(), calls=%async_computation.67 | async-start | bytes 983040
  887.0 211.1 %reduce-scatter.67.cloned.1.call-start = ((), (), s32[]{:S(2)}) async-start(), calls=%async_computation.66 | async-start | bytes 983040
  889.3 222.7 %reduce-scatter.81.cloned.1.call-start = ((), (), s32[]{:S(2)}) async-start(), calls=%async_computation.73 | async-start | bytes 983040
  894.4 218.8 %reduce-scatter.79.cloned.1.call-start = ((), (), s32[]{:S(2)}) async-start(), calls=%async_computation.72 | async-start | bytes 983040
  904.0 12.7 all-to-all-start.1
  908.4 206.1 %reduce-scatter.73.cloned.1.call-start = ((), (), s32[]{:S(2)}) async-start(), calls=%async_computation.69 | async-start | bytes 983040
  955.3 8.9 all-to-all-start.16
  959.2 157.1 %reduce-scatter.71.cloned.1.call-start = ((), (), s32[]{:S(2)}) async-start(), calls=%async_computation.68 | async-start | bytes 983040
  979.0 20.2 %all-to-all-start = ((bf16[8,4,24,768]{3,2,0,1:T(8,128)(2,1)}), bf16[8,4,24,768]{3,2,0,1:T(8,128)(2,1)}, u32[]{:S(2)}, u32[]{:S(2)}) async-start(bf16[8,4,24,768]{3,2,0,1:T(8,128)(2,1)} %copy.177), calls=%async_computation | async-start | bytes 2359296 | tf_op jit(solution)/shard_map/all_to_all | solution.py:516
  999.2 24.4 %all-to-all-start.5 = ((bf16[8,4,24,768]{3,2,0,1:T(8,128)(2,1)}), bf16[8,4,24,768]{3,2,0,1:T(8,128)(2,1)}, u32[]{:S(2)}, u32[]{:S(2)}) async-start(bf16[8,4,24,768]{3,2,0,1:T(8,128)(2,1)} %copy.182), calls=%async_computation.8 | async-start | bytes 2359296 | tf_op jit(solution)/shard_map/all_to_all | solution.py:531
  1003.5 372.7 %reduce-scatter.47.cloned.1.call-start = ((), (), s32[]{:S(2)}) async-start(), calls=%async_computation.56 | async-start | bytes 663552 | tf_op jit(solution)/shard_map/reduce_scatter | solution.py:591
  1023.6 24.2 %all-to-all-start.9 = ((bf16[8,4,24,768]{3,2,0,1:T(8,128)(2,1)}), bf16[8,4,24,768]{3,2,0,1:T(8,128)(2,1)}, u32[]{:S(2)}, u32[]{:S(2)}) async-start(bf16[8,4,24,768]{3,2,0,1:T(8,128)(2,1)} %copy.186), calls=%async_computation.13 | async-start | bytes 2359296 | tf_op jit(solution)/shard_map/all_to_all | solution.py:543
  1027.9 348.3 %reduce-scatter.53.cloned.1.call-start = ((), (), s32[]{:S(2)}) async-start(), calls=%async_computation.59 | async-start | bytes 663552 | tf_op jit(solution)/shard_map/reduce_scatter | solution.py:596
  1047.8 20.2 %all-to-all-start.14 = ((bf16[8,4,24,768]{3,2,0,1:T(8,128)(2,1)}), bf16[8,4,24,768]{3,2,0,1:T(8,128)(2,1)}, u32[]{:S(2)}, u32[]{:S(2)}) async-start(bf16[8,4,24,768]{3,2,0,1:T(8,128)(2,1)} %copy.191), calls=%async_computation.21 | async-start | bytes 2359296 | tf_op jit(solution)/shard_map/all_to_all | solution.py:558
  1068.1 20.2 %all-to-all-start.11 = ((bf16[8,4,24,768]{3,2,0,1:T(8,128)(2,1)}), bf16[8,4,24,768]{3,2,0,1:T(8,128)(2,1)}, u32[]{:S(2)}, u32[]{:S(2)}) async-start(bf16[8,4,24,768]{3,2,0,1:T(8,128)(2,1)} %copy.188), calls=%async_computation.16 | async-start | bytes 2359296 | tf_op jit(solution)/shard_map/all_to_all | solution.py:549
  1072.4 303.9 %reduce-scatter.55.cloned.1.call-start = ((), (), s32[]{:S(2)}) async-start(), calls=%async_computation.60 | async-start | bytes 663552 | tf_op jit(solution)/shard_map/reduce_scatter | solution.py:600
  1088.3 19.4 %all-to-all-start.12 = ((bf16[8,4,24,768]{3,2,0,1:T(8,128)(2,1)}), bf16[8,4,24,768]{3,2,0,1:T(8,128)(2,1)S(1)}, u32[]{:S(2)}, u32[]{:S(2)}) async-start(bf16[8,4,24,768]{3,2,0,1:T(8,128)(2,1)} %copy.189), calls=%async_computation.18 | async-start | bytes 2359296 | tf_op jit(solution)/shard_map/all_to_all | solution.py:552
  1091.8 284.4 %reduce-scatter.61.cloned.1.call-start = ((), (), s32[]{:S(2)}) async-start(), calls=%async_computation.63 | async-start | bytes 663552 | tf_op jit(solution)/shard_map/reduce_scatter | solution.py:605
  1107.7 20.5 %all-to-all-start.2 = ((bf16[8,4,24,768]{3,2,0,1:T(8,128)(2,1)}), bf16[8,4,24,768]{3,2,0,1:T(8,128)(2,1)}, u32[]{:S(2)}, u32[]{:S(2)}) async-start(bf16[8,4,24,768]{3,2,0,1:T(8,128)(2,1)} %copy.179), calls=%async_computation.3 | async-start | bytes 2359296 | tf_op jit(solution)/shard_map/all_to_all | solution.py:522
  1111.9 264.3 %reduce-scatter.57.cloned.1.call-start = ((), (), s32[]{:S(2)}) async-start(), calls=%async_computation.61 | async-start | bytes 663552 | tf_op jit(solution)/shard_map/reduce_scatter | solution.py:602
  1128.1 20.2 %all-to-all-start.3 = ((bf16[8,4,24,768]{3,2,0,1:T(8,128)(2,1)}), bf16[8,4,24,768]{3,2,0,1:T(8,128)(2,1)}, u32[]{:S(2)}, u32[]{:S(2)}) async-start(bf16[8,4,24,768]{3,2,0,1:T(8,128)(2,1)} %copy.180), calls=%async_computation.5 | async-start | bytes 2359296 | tf_op jit(solution)/shard_map/all_to_all | solution.py:525
  1148.3 58.8 %all-to-all-start.18 = ((bf16[8,4,24,3072]{3,2,0,1:T(8,128)(2,1)}), bf16[8,4,24,3072]{3,2,0,1:T(8,128)(2,1)}, u32[]{:S(2)}, u32[]{:S(2)}) async-start(bf16[8,4,24,3072]{3,2,0,1:T(8,128)(2,1)} %copy.195), calls=%async_computation.26 | async-start | bytes 9437184 | tf_op jit(solution)/shard_map/all_to_all | solution.py:570
  1153.3 287.2 %reduce-scatter.59.cloned.1.call-start = ((), (), s32[]{:S(2)}) async-start(), calls=%async_computation.62 | async-start | bytes 663552 | tf_op jit(solution)/shard_map/reduce_scatter | solution.py:603
  1154.4 351.1 %reduce-scatter.49.cloned.1.call-start = ((), (), s32[]{:S(2)}) async-start(), calls=%async_computation.57 | async-start | bytes 663552 | tf_op jit(solution)/shard_map/reduce_scatter | solution.py:593
  1157.0 413.8 %reduce-scatter.51.cloned.1.call-start = ((), (), s32[]{:S(2)}) async-start(), calls=%async_computation.58 | async-start | bytes 663552 | tf_op jit(solution)/shard_map/reduce_scatter | solution.py:594
  1207.1 8.6 all-to-all-start.22
  1210.4 432.8 %reduce-scatter.63.cloned.1.call-start = ((), (), s32[]{:S(2)}) async-start(), calls=%async_computation.64 | async-start | bytes 2654208 | tf_op jit(solution)/shard_map/reduce_scatter | solution.py:609
  1222.9 11.0 all-to-all-start.19
  1233.9 59.0 %all-to-all-start.20 = ((bf16[8,4,96,768]{3,2,0,1:T(8,128)(2,1)}), bf16[8,4,96,768]{3,2,0,1:T(8,128)(2,1)}, u32[]{:S(2)}, u32[]{:S(2)}) async-start(bf16[8,4,96,768]{3,2,0,1:T(8,128)(2,1)} %copy.197), calls=%async_computation.29 | async-start | bytes 9437184 | tf_op jit(solution)/shard_map/all_to_all | solution.py:576
  1292.8 12.2 all-to-all-start.13
  1296.1 419.4 %reduce-scatter.65.cloned.1.call-start = ((), (), s32[]{:S(2)}) async-start(), calls=%async_computation.65 | async-start | bytes 2654208 | tf_op jit(solution)/shard_map/reduce_scatter | solution.py:611
  1310.6 12.4 all-to-all-start.4
  (193 other events, 2877.2 us)
Sparse Core Ops, SparseCore 0:
  11.0 56.8 all-gather.18
  70.8 52.8 all-gather.10
  126.7 52.9 all-gather.12
  182.4 52.9 all-gather.14
  238.2 53.0 all-gather.16
  294.0 52.9 all-gather.20
  349.8 52.9 all-gather.22
  405.7 53.0 all-gather.24
  461.7 66.7 all-gather.26
  531.2 62.5 all-gather.28
  699.8 19.9 reduce-scatter.82
  745.8 19.9 reduce-scatter.86
  768.3 20.8 reduce-scatter.84
  791.5 20.8 reduce-scatter.88
  823.4 22.3 reduce-scatter.76
  848.4 23.2 reduce-scatter.74
  887.1 22.3 reduce-scatter.68
  912.1 23.3 reduce-scatter.66
  938.0 23.1 reduce-scatter.80
  963.8 23.2 reduce-scatter.78
  989.6 29.5 reduce-scatter.72
  1021.9 26.9 reduce-scatter.70
  1052.8 61.7 reduce-scatter.46
  1118.7 61.0 reduce-scatter.52
  1183.7 61.1 reduce-scatter.54
  1248.9 61.1 reduce-scatter.60
  1313.8 61.2 reduce-scatter.56
  1379.3 61.1 reduce-scatter.58
  1444.3 61.1 reduce-scatter.48
  1509.6 61.1 reduce-scatter.50
  1574.8 68.2 reduce-scatter.62
  1647.2 68.2 reduce-scatter.64
where the time goes:
time: 1740 us; the launch traced here: 1720 us
  waiting for transfers between devices  772 us (44%)
  local copies, waits for them, and re-layouts  333 us (19%)
  matrix products  191 us (11%)
  blocking collectives  182 us (10%)
  other arithmetic  130 us (7%)
  starting transfers between devices  97.1 us (6%)
    dynamic_slice x144, local copies, waits for them, and re-layouts, attend_forward(): lax.map(one_pair, (split_pairs(queries, heads), split_pairs(keys, heads),...  121 us
    unnamed x2, blocking collectives  79.9 us
    reduce_scatter x1, waiting for transfers between devices, body(): lax.psum_scatter(partial_value[18], 'dp', scatter_dimension=0, tiled=True)  72.4 us
    reduce_scatter x1, waiting for transfers between devices, body(): lax.psum_scatter(partial_value[20], 'dp', scatter_dimension=0, tiled=True)  72.3 us
    reduce_scatter x1, waiting for transfers between devices, body(): lax.psum_scatter(partial_value[3], 'dp', scatter_dimension=0, tiled=True)  65.3 us
    reduce_scatter x1, waiting for transfers between devices, body(): lax.psum_scatter(partial_value[2], 'dp', scatter_dimension=0, tiled=True)  65.1 us
    reduce_scatter x1, waiting for transfers between devices, body(): lax.psum_scatter(partial_value[12], 'dp', scatter_dimension=0, tiled=True)  64.2 us
    unnamed x397, local copies, waits for them, and re-layouts  61 us
  transfers between devices with their start and end apart: 56, of which 29 were waited for; matrix products, arithmetic and copies ran while one was open for 32% of the time, Pallas kernels for 0%

commit v1 on v0

v1 whole, which is shorter than its diff:
```python
import jax
import jax.numpy as jnp
from jax import lax
from jax.experimental import pallas as pl
from jax.experimental.pallas import tpu as pltpu
from jax.sharding import PartitionSpec as P

HEADS = 12
VMEM_LIMIT = 60 * 1024 * 1024
NEG = -1e30


def matmul(left, right):
    return jnp.dot(left, right, preferred_element_type=jnp.float32)


def contract_rows(left, right):
    return lax.dot_general(
        left, right, (((0,), (0,)), ((), ())), preferred_element_type=jnp.float32
    )


def times_transpose(left, right):
    return lax.dot_general(
        left, right, (((1,), (1,)), ((), ())), preferred_element_type=jnp.float32
    )


def widen(values):
    return values.astype(jnp.float32)


def low(values):
    return values.astype(jnp.bfloat16)


def normalize(values, gain, shift):
    centred = values - jnp.mean(values, axis=-1, keepdims=True)
    scale = lax.rsqrt(jnp.mean(centred * centred, axis=-1, keepdims=True) + 1e-05)
    return centred * scale * gain + shift


def norm_backward(values, gain, upstream):
    centred = values - jnp.mean(values, axis=-1, keepdims=True)
    scale = lax.rsqrt(jnp.mean(centred * centred, axis=-1, keepdims=True) + 1e-05)
    normed = centred * scale
    scaled = upstream * gain
    result = scale * (
        scaled
        - jnp.mean(scaled, axis=-1, keepdims=True)
        - normed * jnp.mean(scaled * normed, axis=-1, keepdims=True)
    )
    return (
        result,
        jnp.sum(upstream * normed, axis=0, keepdims=True),
        jnp.sum(upstream, axis=0, keepdims=True),
    )


(
    SELF_Q,
    SELF_V,
    SELF_O,
    GAIN_ONE,
    SHIFT_ONE,
    CROSS_Q,
    CROSS_V,
    CROSS_O,
    GAIN_TWO,
    SHIFT_TWO,
    OUTER_B,
    GAIN_THREE,
    SHIFT_THREE,
    INNER_B,
) = range(14)


def pack_vectors(vectors, width):
    def kernel(*refs):
        out_ref = refs[-1]
        out_ref[...] = jnp.zeros_like(out_ref)
        for i, ref in enumerate(refs[:-1]):
            size = ref.shape[1]
            at = 128 * (i // 8)
            out_ref[i % 8 : i % 8 + 1, at : at + size] = ref[...]

    return pl.pallas_call(
        kernel,
        out_shape=jax.ShapeDtypeStruct((8, width), vectors[0].dtype),
        name="pack_vectors",
    )(*[v[None, :] for v in vectors])


class Call:
    def __init__(self, name, grid):
        self.name, self.grid = name, grid
        self.ins, self.in_specs, self.out_shapes, self.out_specs = [], [], [], []
        self.flops, self.bytes, self.exps = 0, 0, 0

    def whole(self, array):
        zeros = (0,) * array.ndim
        self.blocked(array, array.shape, lambda *g: zeros, buffers=1)

    def blocked(self, array, block, index, buffers=2):
        mode = {} if buffers == 2 else {"pipeline_mode": pl.Buffered(buffers)}
        self.ins.append(array)
        self.in_specs.append(pl.BlockSpec(block, index, **mode))
        self.bytes += array.size * array.dtype.itemsize

    def scalars(self, array):
        self.ins.append(array)
        self.in_specs.append(pl.BlockSpec(memory_space=pltpu.SMEM))

    def weight(self, weight):
        array, block, index = weight
        self.ins.append(array)
        self.in_specs.append(pl.BlockSpec(block, lambda *g: index, pipeline_mode=pl.Buffered(1)))
        self.bytes += array.shape[-1] ** 2 * 2

    def out(self, shape, dtype, block=None, index=None):
        zeros = (0,) * len(shape)
        self.out_shapes.append(jax.ShapeDtypeStruct(shape, dtype))
        self.out_specs.append(pl.BlockSpec(block or shape, index or (lambda *g: zeros)))
        size = 1
        for n in shape:
            size *= n
        self.bytes += size * jnp.dtype(dtype).itemsize

    def run(self, kernel, scratch=()):
        return pl.pallas_call(
            kernel,
            grid=self.grid,
            in_specs=self.in_specs,
            out_specs=self.out_specs,
            out_shape=self.out_shapes,
            scratch_shapes=list(scratch),
            compiler_params=pltpu.CompilerParams(vmem_limit_bytes=VMEM_LIMIT),
            cost_estimate=pl.CostEstimate(
                flops=int(self.flops), bytes_accessed=int(self.bytes), transcendentals=int(self.exps)
            ),
            name=self.name,
        )(*self.ins)


class Halves:
    def __init__(self, call, count, owners, owned_rows, width, heads=None, index=None):
        self.owned_rows = owned_rows
        self.even = owned_rows % 8 == 0
        if self.even:
            shape, outs = (owners // 2, count, owned_rows, width), 2
            block = (heads or owners // 2, 1 if index else count, owned_rows, width)
        else:
            shape, outs = (count, owners * owned_rows, width), 1
            block = (1 if index else count, 2 * (heads or owners // 2) * owned_rows, width)
        for _ in range(outs):
            if index is None:
                call.out(shape, jnp.bfloat16)
            elif self.even:
                call.out(shape, jnp.bfloat16, block, lambda *g: index(*g) + (0, 0))
            else:
                call.out(shape, jnp.bfloat16, block, lambda *g: index(*g)[::-1] + (0,))
        self.outs = outs

    def store(self, refs, at, value, mine):
        if not self.even:
            refs[0][at] = low(value)
            return
        parts = value.reshape(-1, 2, self.owned_rows, value.shape[-1])
        first, second = low(parts[:, 0]), low(parts[:, 1])
        refs[0][:, at] = jnp.where(mine == 0, first, second)
        refs[1][:, at] = jnp.where(mine == 0, second, first)

    def pair(self, results, mine):
        if self.even:
            return tuple(results)
        whole = results[0]
        parts = whole.reshape(whole.shape[0], -1, 2, self.owned_rows, whole.shape[-1])
        return tuple(
            lax.dynamic_index_in_dim(parts, which, 2, keepdims=False).transpose(1, 0, 2, 3)
            for which in (mine, 1 - mine)
        )


def load(ref):
    value = ref[...]
    return value.reshape(-1, value.shape[-1])


def row(vecs_ref, index):
    return vecs_ref[index : index + 1, :]


def fill_bias(bias_ref, chunk, rows, ids_ref):
    half, block = rows // 2, rows // 4
    key = lax.broadcasted_iota(jnp.int32, (rows, rows), 0)
    query = lax.broadcasted_iota(jnp.int32, (rows, rows), 1)
    key_block = jnp.where(
        lax.rem(key, half) < block, ids_ref[2 * chunk], ids_ref[2 * chunk + 1]
    )
    query_block = jnp.where(lax.rem(query, half) < block, ids_ref[0], ids_ref[1])
    key_place = key_block * block + lax.rem(key, block)
    query_place = query_block * block + lax.rem(query, block)
    causal = key_place <= query_place
    prompt_key = key < half
    prompt_query = query < half
    allowed = (prompt_key & prompt_query & causal) | (
        jnp.logical_not(prompt_query)
        & ((prompt_key & (key_place < ids_ref[4])) | (jnp.logical_not(prompt_key) & causal))
    )
    bias_ref[chunk] = jnp.where(allowed, 0.0, NEG)


def lane_masks(values):
    lane = lax.broadcasted_iota(jnp.int32, values.shape, 1)
    zero = jnp.zeros_like(values)
    first = lane < values.shape[1] // 2
    return jnp.where(first, values, zero), jnp.where(first, zero, values)


def attend_pair(queries, keys, values, bias_ref, log_ref):
    queries = lane_masks(queries)
    outs = []
    for head in range(2):
        scores = []
        for chunk in range(2):
            part = times_transpose(keys[chunk], queries[head])
            scores.append(part if bias_ref is None else part + bias_ref[chunk])
        top = jnp.maximum(
            scores[0].max(axis=0, keepdims=True), scores[1].max(axis=0, keepdims=True)
        )
        total, mixed = 0.0, 0.0
        for chunk in range(2):
            weights = jnp.exp(scores[chunk] - top)
            total = total + weights.sum(axis=0, keepdims=True)
            mixed = mixed + contract_rows(values[chunk], low(weights))
        outs.append(mixed * (1.0 / total))
        log_ref[0, head : head + 1, :] = top + jnp.log(total)
    lane = lax.broadcasted_iota(jnp.int32, outs[0].shape, 0)
    return low(jnp.where(lane < outs[0].shape[0] // 2, outs[0], outs[1]).T)


def attend_pair_backward(queries, keys, values, bias_ref, log_ref, mixed, upstream):
    queries = lane_masks(queries)
    ups = lane_masks(upstream)
    product = widen(mixed) * widen(upstream)
    high = low(product)
    rest = low(product - widen(high))
    pair = product.shape[1]
    lane = lax.broadcasted_iota(jnp.int32, (8, pair), 1)
    line = lax.broadcasted_iota(jnp.int32, (8, pair), 0)
    pick = jnp.where(
        ((lane < pair // 2) & (line == 0)) | ((lane >= pair // 2) & (line == 1)), 1.0, 0.0
    ).astype(jnp.bfloat16)
    delta = times_transpose(pick, high) + times_transpose(pick, rest)
    dq = 0.0
    dk = [0.0, 0.0]
    dv = [0.0, 0.0]
    for head in range(2):
        for chunk in range(2):
            part = times_transpose(keys[chunk], queries[head])
            if bias_ref is not None:
                part = part + bias_ref[chunk]
            probs = jnp.exp(part - log_ref[0, head : head + 1, :])
            prob_grad = times_transpose(values[chunk], ups[head])
            score_grad = low(probs * (prob_grad - delta[head : head + 1, :]))
            dv[chunk] = dv[chunk] + matmul(low(probs), ups[head])
            dk[chunk] = dk[chunk] + matmul(score_grad, queries[head])
            dq = dq + contract_rows(lane_masks(keys[chunk])[head], score_grad)
    return low(dq.T), dk, dv


def project_kernel(scaled, x_ref, *refs):
    vecs_ref = refs[-3] if scaled else refs[-2]
    values = x_ref[...]
    if scaled:
        wq_ref, wk_ref, wv_ref = refs[:3]
        q_ref, kv_ref = refs[-2:]
        q_ref[...] = low((matmul(values, load(wq_ref)) + row(vecs_ref, SELF_Q)) * 0.125)
        bias = row(vecs_ref, SELF_V)
    else:
        wk_ref, wv_ref = refs[:2]
        kv_ref = refs[-1]
        bias = row(vecs_ref, CROSS_V)
    kv_ref[0] = low(matmul(values, load(wk_ref)))
    kv_ref[1] = low(matmul(values, load(wv_ref)) + bias)


def project(tokens, weights, vecs):
    rows, width = tokens.shape
    scaled = len(weights) == 3
    call = Call("project", (1,))
    call.whole(tokens)
    for weight in weights:
        call.weight(weight)
    call.whole(vecs)
    if scaled:
        call.out((rows, width), jnp.bfloat16)
    call.out((2, rows, width), jnp.bfloat16)
    call.flops = 2 * len(weights) * rows * width * width

    def kernel(*refs):
        project_kernel(scaled, *refs)

    return call.run(kernel)


def lanes_of(width):
    lanes = 2 * (width // HEADS)

    def at(h):
        return pl.ds(pl.multiple_of(h * lanes, lanes), lanes)

    return lanes, at


def self_attend(ids, queries, own, other):
    rows, width = queries.shape
    pairs = HEADS // 2
    lanes, _ = lanes_of(width)
    call = Call("self_attend", (pairs,))
    call.scalars(ids)
    call.blocked(queries, (rows, lanes), lambda h: (0, h))
    for array in (own, other):
        call.blocked(array, (2, rows, lanes), lambda h: (0, 0, h))
    call.out((rows, width), jnp.bfloat16, (rows, lanes), lambda h: (0, h))
    call.out((pairs, 2, rows), jnp.float32, (1, 2, rows), lambda h: (h, 0, 0))
    call.flops = 16 * rows * rows * width
    call.exps = 2 * rows * rows * HEADS

    def kernel(ids_ref, q_ref, own_ref, other_ref, mixed_ref, log_ref, bias_ref):
        @pl.when(pl.program_id(0) == 0)
        def _():
            for chunk in range(2):
                fill_bias(bias_ref, chunk, rows, ids_ref)

        keys, values = (own_ref[0], other_ref[0]), (own_ref[1], other_ref[1])
        mixed_ref[...] = attend_pair(q_ref[...], keys, values, bias_ref, log_ref)

    return call.run(kernel, [pltpu.VMEM((2, rows, rows), jnp.float32)])


def self_finish(tokens, mixed, out_weight, query_weight, vecs):
    rows, width = tokens.shape
    call = Call("self_finish", (1,))
    call.whole(tokens)
    call.whole(mixed)
    call.weight(out_weight)
    call.weight(query_weight)
    call.whole(vecs)
    call.out((rows, width), jnp.float32)
    call.out((rows, width), jnp.bfloat16)
    call.out((rows, width), jnp.bfloat16)
    call.flops = 4 * rows * width * width

    def kernel(x_ref, mixed_ref, wo_ref, wq_ref, vecs_ref, pre_ref, low_ref, next_ref):
        pre = widen(x_ref[...]) + matmul(mixed_ref[...], load(wo_ref)) + row(vecs_ref, SELF_O)
        pre_ref[...] = pre
        first = low(normalize(pre, row(vecs_ref, GAIN_ONE), row(vecs_ref, SHIFT_ONE)))
        low_ref[...] = first
        next_ref[...] = low((matmul(first, load(wq_ref)) + row(vecs_ref, CROSS_Q)) * 0.125)

    return call.run(kernel)


def cross_attend(queries, own, other, first_pre, out_weight, vecs):
    rows, width = queries.shape
    key_rows = own.shape[1]
    pairs = HEADS // 2
    lanes, at = lanes_of(width)
    call = Call("cross_attend", (pairs,))
    call.blocked(queries, (rows, lanes), lambda h: (0, h))
    for array in (own, other):
        call.blocked(array, (2, key_rows, lanes), lambda h: (0, 0, h))
    call.whole(first_pre)
    call.weight(out_weight)
    call.whole(vecs)
    call.out((rows, width), jnp.bfloat16)
    call.out((pairs, 2, rows), jnp.float32, (1, 2, rows), lambda h: (h, 0, 0))
    call.out((rows, width), jnp.float32)
    call.out((rows, width), jnp.bfloat16)
    call.flops = 16 * rows * key_rows * width + 2 * rows * width * width
    call.exps = 2 * rows * key_rows * HEADS

    def kernel(
        q_ref, own_ref, other_ref, first_ref, wo_ref, vecs_ref, mixed_ref, log_ref, pre_ref, low_ref
    ):
        step = pl.program_id(0)
        keys, values = (own_ref[0], other_ref[0]), (own_ref[1], other_ref[1])
        mixed_ref[:, at(step)] = attend_pair(q_ref[...], keys, values, None, log_ref)

        @pl.when(step == pairs - 1)
        def _():
            first = normalize(first_ref[...], row(vecs_ref, GAIN_ONE), row(vecs_ref, SHIFT_ONE))
            pre = first + matmul(mixed_ref[...], load(wo_ref)) + row(vecs_ref, CROSS_O)
            pre_ref[...] = pre
            low_ref[...] = low(normalize(pre, row(vecs_ref, GAIN_TWO), row(vecs_ref, SHIFT_TWO)))

    return call.run(kernel)


def feed_blocks(call, feed, width, chunks, owned_rows):
    owners = feed.shape[0]
    hidden_rows = chunks * owned_rows
    if owned_rows % 8 == 0:
        call.blocked(feed, (owners, owned_rows, width), lambda i: (0, chunks + i, 0))
        call.blocked(feed, (owners // chunks, hidden_rows, width), lambda i: (i, 0, 0))
    else:
        parts = [
            feed[:, hidden_rows + i * owned_rows : hidden_rows + (i + 1) * owned_rows]
            for i in range(chunks)
        ]
        parts = [p.reshape(-1, width) for p in parts]
        call.blocked(jnp.concatenate(parts, axis=1), (width, width), lambda i: (0, i))
        call.blocked(feed[:, :hidden_rows].reshape(-1, width), (width, width), lambda i: (i, 0))


def feed_forward(second_pre, second_low, feed, vecs, chunks, owned_rows):
    rows, width = second_low.shape
    hidden = chunks * width
    call = Call("feed_forward", (chunks,))
    call.whole(second_pre)
    call.whole(second_low)
    feed_blocks(call, feed, width, chunks, owned_rows)
    call.whole(vecs)
    call.out((rows, hidden), jnp.bfloat16, (rows, width), lambda i: (0, i))
    call.out((rows, hidden), jnp.bfloat16, (rows, width), lambda i: (0, i))
    call.out((rows, width), jnp.float32)
    call.out((rows, width), jnp.bfloat16)
    call.flops = 4 * rows * hidden * width
    call.exps = 2 * rows * hidden

    def kernel(
        pre_ref, low_ref, inner_ref, outer_ref, vecs_ref, active_ref, slope_ref, third_ref, out_ref
    ):
        step = pl.program_id(0)

        @pl.when(step == 0)
        def _():
            second = normalize(pre_ref[...], row(vecs_ref, GAIN_TWO), row(vecs_ref, SHIFT_TWO))
            third_ref[...] = second + row(vecs_ref, OUTER_B)

        inner = matmul(low_ref[...], load(inner_ref)) + vecs_ref[pl.ds(INNER_B + step, 1), :]
        bell = 0.5 * (1.0 + lax.erf(inner * 0.7071067811865476))
        active = low(inner * bell)
        active_ref[...] = active
        density = jnp.exp(-0.5 * inner * inner) * 0.3989422804014327
        slope_ref[...] = low(bell + inner * density)
        third_ref[...] += matmul(active, load(outer_ref))

        @pl.when(step == chunks - 1)
        def _():
            out_ref[...] = low(
                normalize(third_ref[...], row(vecs_ref, GAIN_THREE), row(vecs_ref, SHIFT_THREE))
            )

    return call.run(kernel)


def feed_backward(
    ids, upstream, third_pre, second_pre, second_low, active, slope, cross_mixed, feed, out_weight, vecs,
    chunks, owned_rows,
):
    rows, width = second_low.shape
    hidden = chunks * width
    owners = width // owned_rows
    call = Call("feed_backward", (chunks,))
    call.scalars(ids)
    call.whole(upstream)
    call.whole(third_pre)
    call.whole(second_pre)
    call.whole(second_low)
    call.blocked(active, (rows, width), lambda i: (0, i))
    call.blocked(slope, (rows, width), lambda i: (0, i))
    call.whole(cross_mixed)
    feed_blocks(call, feed, width, chunks, owned_rows)
    call.weight(out_weight)
    call.whole(vecs)
    inner_half = Halves(
        call, chunks, owners, owned_rows, width, owners // 2, lambda i: (0, i)
    )
    outer_half = Halves(
        call, 1, owners, chunks * owned_rows, width, owners // 2 // chunks, lambda i: (i, 0)
    )
    out_half = Halves(call, 1, owners, owned_rows, width)
    call.out((rows, width), jnp.float32)
    call.out((rows, width), jnp.bfloat16)
    call.out((16, width), jnp.float32)
    n_in, n_half, n_outer = len(call.ins), inner_half.outs, outer_half.outs
    call.flops = 8 * rows * hidden * width + 4 * rows * width * width

    def kernel(*refs):
        (
            ids_ref, up_ref, third_ref, second_ref, low_ref, active_ref, slope_ref, mixed_ref, inner_ref,
            outer_ref, wo_ref, vecs_ref,
        ) = refs[:n_in]
        inner_grads = refs[n_in : n_in + n_half]
        outer_grads = refs[n_in + n_half : n_in + n_half + n_outer]
        out_grads = refs[n_in + n_half + n_outer : -5]
        second_grad_ref, mix_ref, sums_ref, third_low_ref, total_ref = refs[-5:]
        step = pl.program_id(0)
        mine = ids_ref[5]

        @pl.when(step == 0)
        def _():
            grad, gain_sum, shift_sum = norm_backward(
                third_ref[...], row(vecs_ref, GAIN_THREE), widen(up_ref[...])
            )
            total_ref[...] = grad
            third_low_ref[...] = low(grad)
            sums_ref[0:1, :] = gain_sum
            sums_ref[1:2, :] = shift_sum
            sums_ref[2:3, :] = jnp.sum(widen(low(grad)), axis=0, keepdims=True)

        third_low = third_low_ref[...]
        inner_low = low(times_transpose(third_low, load(outer_ref)) * widen(slope_ref[...]))
        total_ref[...] += times_transpose(inner_low, load(inner_ref))
        outer_half.store(outer_grads, 0, contract_rows(active_ref[...], third_low), mine)
        inner_half.store(inner_grads, 0, contract_rows(low_ref[...], inner_low), mine)
        sums_ref[pl.ds(8 + step, 1), :] = jnp.sum(widen(inner_low), axis=0, keepdims=True)

        @pl.when(step == chunks - 1)
        def _():
            grad, gain_sum, shift_sum = norm_backward(
                second_ref[...], row(vecs_ref, GAIN_TWO), total_ref[...]
            )
            second_grad_ref[...] = grad
            cross_low = low(grad)
            sums_ref[3:4, :] = gain_sum
            sums_ref[4:5, :] = shift_sum
            sums_ref[5:6, :] = jnp.sum(widen(cross_low), axis=0, keepdims=True)
            mix_ref[...] = low(times_transpose(cross_low, load(wo_ref)))
            out_half.store(out_grads, 0, contract_rows(mixed_ref[...], cross_low), mine)

    results = call.run(
        kernel, [pltpu.VMEM((rows, width), jnp.bfloat16), pltpu.VMEM((rows, width), jnp.float32)]
    )
    core = ids[5]
    return (
        inner_half.pair(results[:n_half], core),
        outer_half.pair(results[n_half : n_half + n_outer], core),
        out_half.pair(results[n_half + n_outer : -3], core),
    ) + tuple(results[-3:])


def cross_backward(
    ids, queries, own, other, mixed, upstream, logsum, first_low, first_pre, second_grad, self_mixed,
    query_weight, out_weight, vecs, owned_rows,
):
    rows, width = queries.shape
    key_rows = own.shape[1]
    pairs = HEADS // 2
    lanes, at = lanes_of(width)
    call = Call("cross_backward", (pairs,))
    call.scalars(ids)
    for array in (queries, mixed, upstream):
        call.blocked(array, (rows, lanes), lambda h: (0, h))
    call.blocked(logsum, (1, 2, rows), lambda h: (h, 0, 0))
    for array in (own, other):
        call.blocked(array, (2, key_rows, lanes), lambda h: (0, 0, h))
    for array in (first_low, first_pre, second_grad, self_mixed):
        call.whole(array)
    call.weight(query_weight)
    call.weight(out_weight)
    call.whole(vecs)
    for _ in range(2):
        call.out((2, key_rows, width), jnp.bfloat16, (2, key_rows, lanes), lambda h: (0, 0, h))
    call.out((rows, width), jnp.float32)
    call.out((rows, width), jnp.bfloat16)
    call.out((8, width), jnp.float32)
    half = Halves(call, 2, width // owned_rows, owned_rows, width)
    call.flops = 40 * rows * key_rows * width + 8 * rows * width * width
    call.exps = 2 * rows * key_rows * HEADS

    def kernel(
        ids_ref, q_ref, mixed_ref, up_ref, log_ref, own_ref, other_ref, low_ref, pre_ref, grad_ref,
        self_mixed_ref, wq_ref, wo_ref, vecs_ref, own_out_ref, other_out_ref, first_ref, mix_ref,
        sums_ref, *rest,
    ):
        step = pl.program_id(0)
        weights_refs, dq_ref = rest[:-1], rest[-1]
        keys, values = (own_ref[0], other_ref[0]), (own_ref[1], other_ref[1])
        dq, dk, dv = attend_pair_backward(
            q_ref[...], keys, values, None, log_ref, mixed_ref[...], up_ref[...]
        )
        dq_ref[:, at(step)] = dq
        for chunk, out in enumerate((own_out_ref, other_out_ref)):
            out[0] = low(dk[chunk])
            out[1] = low(dv[chunk])

        @pl.when(step == pairs - 1)
        def _():
            query_low = dq_ref[...]
            half.store(weights_refs, 0, contract_rows(low_ref[...], query_low) * 0.125, ids_ref[5])
            total = grad_ref[...] + times_transpose(query_low, load(wq_ref)) * 0.125
            grad, gain_sum, shift_sum = norm_backward(pre_ref[...], row(vecs_ref, GAIN_ONE), total)
            first_ref[...] = grad
            self_low = low(grad)
            mix_ref[...] = low(times_transpose(self_low, load(wo_ref)))
            half.store(weights_refs, 1, contract_rows(self_mixed_ref[...], self_low), ids_ref[5])
            sums_ref[0:1, :] = gain_sum
            sums_ref[1:2, :] = shift_sum
            sums_ref[2:3, :] = jnp.sum(widen(self_low), axis=0, keepdims=True)
            sums_ref[3:4, :] = jnp.sum(widen(query_low), axis=0, keepdims=True) * 0.125

    results = call.run(kernel, [pltpu.VMEM((rows, width), jnp.bfloat16)])
    return tuple(results[:5]) + (half.pair(results[5:], ids[5]),)


def self_backward(
    ids, queries, own, other, mixed, upstream, logsum, tokens, first_grad, query_weight, owned_rows
):
    rows, width = queries.shape
    pairs = HEADS // 2
    lanes, at = lanes_of(width)
    call = Call("self_backward", (pairs,))
    call.scalars(ids)
    for array in (queries, mixed, upstream):
        call.blocked(array, (rows, lanes), lambda h: (0, h))
    call.blocked(logsum, (1, 2, rows), lambda h: (h, 0, 0))
    for array in (own, other):
        call.blocked(array, (2, rows, lanes), lambda h: (0, 0, h))
    for array in (tokens, first_grad):
        call.whole(array)
    call.weight(query_weight)
    for _ in range(2):
        call.out((2, rows, width), jnp.bfloat16, (2, rows, lanes), lambda h: (0, 0, h))
    call.out((rows, width), jnp.float32)
    call.out((8, width), jnp.float32)
    half = Halves(call, 1, width // owned_rows, owned_rows, width)
    call.flops = 40 * rows * rows * width + 4 * rows * width * width
    call.exps = 2 * rows * rows * HEADS

    def kernel(
        ids_ref, q_ref, mixed_ref, up_ref, log_ref, own_ref, other_ref, x_ref, grad_ref, wq_ref,
        own_out_ref, other_out_ref, part_ref, sums_ref, *rest,
    ):
        weights_refs, (bias_ref, dq_ref) = rest[:-2], rest[-2:]
        step = pl.program_id(0)

        @pl.when(step == 0)
        def _():
            for chunk in range(2):
                fill_bias(bias_ref, chunk, rows, ids_ref)

        keys, values = (own_ref[0], other_ref[0]), (own_ref[1], other_ref[1])
        dq, dk, dv = attend_pair_backward(
            q_ref[...], keys, values, bias_ref, log_ref, mixed_ref[...], up_ref[...]
        )
        dq_ref[:, at(step)] = dq
        for chunk, out in enumerate((own_out_ref, other_out_ref)):
            out[0] = low(dk[chunk])
            out[1] = low(dv[chunk])

        @pl.when(step == pairs - 1)
        def _():
            query_low = dq_ref[...]
            half.store(weights_refs, 0, contract_rows(x_ref[...], query_low) * 0.125, ids_ref[5])
            part_ref[...] = grad_ref[...] + times_transpose(query_low, load(wq_ref)) * 0.125
            sums_ref[0:1, :] = jnp.sum(widen(query_low), axis=0, keepdims=True) * 0.125

    results = call.run(
        kernel,
        [pltpu.VMEM((2, rows, rows), jnp.float32), pltpu.VMEM((rows, width), jnp.bfloat16)],
    )
    return tuple(results[:4]) + (half.pair(results[4:], ids[5]),)


def key_backward(ids, tokens, mine, got, part, key_weight, value_weight, owned_rows):
    rows, width = tokens.shape
    call = Call("key_backward", (1,))
    call.scalars(ids)
    for array in (tokens, mine, got) + (() if part is None else (part,)):
        call.whole(array)
    call.weight(key_weight)
    call.weight(value_weight)
    call.out((rows, width), jnp.bfloat16)
    call.out((8, width), jnp.float32)
    half = Halves(call, 2, width // owned_rows, owned_rows, width)
    call.flops = 8 * rows * width * width

    def kernel(ids_ref, x_ref, mine_ref, got_ref, *refs):
        if part is not None:
            total, refs = refs[0][...], refs[1:]
        else:
            total = 0.0
        wk_ref, wv_ref, out_ref, sums_ref = refs[:4]
        weights_refs = refs[4:]
        values = x_ref[...]
        dk = low(widen(mine_ref[0]) + widen(got_ref[0]))
        dv = low(widen(mine_ref[1]) + widen(got_ref[1]))
        half.store(weights_refs, 0, contract_rows(values, dk), ids_ref[5])
        half.store(weights_refs, 1, contract_rows(values, dv), ids_ref[5])
        out_ref[...] = low(
            total + times_transpose(dk, load(wk_ref)) + times_transpose(dv, load(wv_ref))
        )
        sums_ref[0:1, :] = jnp.sum(widen(dv), axis=0, keepdims=True)

    results = call.run(kernel)
    return tuple(results[:2]) + (half.pair(results[2:], ids[5]),)


def flip(size, bit):
    return [(i, i ^ bit) for i in range(size)]


def swap_seq(values, bits):
    return lax.ppermute(values, "seq", flip(lax.axis_size("seq"), bits))


def tie(*values):
    return lax.optimization_barrier(values)


def bit_order(dp_size, seq_size):
    return [("dp", b) for b in range(dp_size.bit_length() - 1)][::-1] + [
        ("seq", b) for b in range(seq_size.bit_length() - 1)
    ][::-1]


class Moves:
    def __init__(self):
        self.spots = {name: lax.axis_index(name) for name in ("dp", "seq")}
        self.sizes = {name: lax.axis_size(name) for name in ("dp", "seq")}
        self.canonical = bit_order(self.sizes["dp"], self.sizes["seq"])

    def mine(self, step):
        return (self.spots[step[0]] >> step[1]) & 1

    def send(self, values, step):
        name, bit = step
        return lax.ppermute(values, name, flip(self.sizes[name], 1 << bit))


def split_sum(keep, got, at, mine):
    total = low(widen(keep) + widen(got))
    return [
        lax.dynamic_index_in_dim(total, which, at, keepdims=False) for which in (mine, 1 - mine)
    ]


def merge(keep, got, at, mine):
    shape = keep.shape
    before, after = 1, shape[-2]
    for n in shape[:at]:
        before *= n
    for n in shape[at + 1 : -2]:
        after *= n
    width = shape[-1]
    left = tuple(shape[:at] + shape[at + 1 :])
    if shape[-2] % 8:
        return split_sum(keep, got, at, mine)
    view = (before, 2, after, width)
    rows, heads = after, 1
    while rows > 256 and rows % 16 == 0:
        rows //= 2
    while heads * rows < 128 and before % (2 * heads) == 0:
        heads *= 2
    block = (heads, None, rows, width)

    def stay(i, j, mine_ref):
        return (i, mine_ref[0], j, 0)

    def go(i, j, mine_ref):
        return (i, 1 - mine_ref[0], j, 0)

    def kernel(mine_ref, keep_a, keep_b, got_a, got_b, stay_ref, go_ref):
        stay_ref[...] = low(widen(keep_a[...]) + widen(got_a[...]))
        go_ref[...] = low(widen(keep_b[...]) + widen(got_b[...]))

    size = before * after * width
    out = pl.BlockSpec((heads, rows, width), lambda i, j, mine_ref: (i, j, 0))
    keep, got = keep.reshape(view), got.reshape(view)
    results = pl.pallas_call(
        kernel,
        grid_spec=pltpu.PrefetchScalarGridSpec(
            num_scalar_prefetch=1,
            grid=(before // heads, after // rows),
            in_specs=[pl.BlockSpec(block, m) for m in (stay, go, stay, go)],
            out_specs=[out, out],
        ),
        out_shape=[jax.ShapeDtypeStruct((before, after, width), jnp.bfloat16)] * 2,
        compiler_params=pltpu.CompilerParams(vmem_limit_bytes=VMEM_LIMIT),
        cost_estimate=pl.CostEstimate(flops=2 * size, bytes_accessed=12 * size, transcendentals=0),
        name="merge",
    )(mine.reshape(1).astype(jnp.int32), keep, keep, got, got)
    return [r.reshape(left) for r in results]


class Scatter:
    def __init__(self, moves, pairs, order):
        self.moves = moves
        self.dims = [step for step in moves.canonical if step != order[0]]
        self.order = list(order)
        pieces = (2,) * len(self.dims)

        def join(arrays):
            arrays = [a.reshape(pieces + (-1, a.shape[-1])) for a in arrays]
            return arrays[0] if len(arrays) == 1 else jnp.concatenate(arrays, axis=-2)

        self.keep = join([k for k, _ in pairs])
        self.away = join([a for _, a in pairs])
        self.got = None

    def ship(self):
        self.got = self.moves.send(self.away, self.order.pop(0))
        self.away = None

    def take(self):
        got, self.got = self.got, None
        if self.order:
            step = self.order[0]
            at = self.dims.index(step)
            split = merge if self.keep.size > 2**18 else split_sum
            self.keep, self.away = split(self.keep, got, at, self.moves.mine(step))
            self.dims.pop(at)
        else:
            self.held = widen(self.keep) + widen(got)

    def total(self):
        return low(widen(self.keep) + widen(self.got))


def joined(chains):
    first = chains[0]
    chain = object.__new__(Scatter)
    chain.moves, chain.dims, chain.order, chain.got = first.moves, first.dims, first.order, None
    chain.keep = jnp.concatenate([c.keep for c in chains], axis=-2)
    chain.away = jnp.concatenate([c.away for c in chains], axis=-2)
    return chain


def receive(chains, *values):
    tied = tie(*[c.got for c in chains], *values)
    for chain, got in zip(chains, tied):
        chain.got = got
        chain.take()
    values = tied[len(chains) :]
    return values[0] if len(values) == 1 else values


def depart(chains, *values):
    tied = tie(*[c.away for c in chains], *values)
    for chain, away in zip(chains, tied):
        chain.away = away
        chain.ship()
    values = tied[len(chains) :]
    return values[0] if len(values) == 1 else values


def advance(chains, *values):
    values = receive(chains, *values)
    return depart(chains, *(values if isinstance(values, (list, tuple)) else (values,)))


class Gather:
    def __init__(self, moves, held, order, dims=()):
        self.moves, self.held, self.order, self.dims = moves, held, list(order), list(dims)

    def ship(self):
        self.got = self.moves.send(self.held, self.order[0])

    def take(self):
        step = self.order.pop(0)
        mine = self.moves.mine(step)
        first = jnp.where(mine == 0, self.held, self.got)
        second = jnp.where(mine == 0, self.got, self.held)
        self.held = jnp.stack([first, second], axis=0)
        self.dims.insert(0, step)

    def part(self, first, last, order):
        return Gather(self.moves, self.held[..., first:last, :], order, self.dims)

    def result(self):
        order = [self.dims.index(step) for step in self.moves.canonical]
        count = len(order)
        held = self.held.transpose(order + [count, count + 1])
        return held.reshape((-1,) + held.shape[-2:])


def pump(taking, shipping, *values):
    tied = tie(*[g.got for g in taking], *values)
    for gather, got in zip(taking, tied):
        gather.got = got
        gather.take()
    tied = tie(*[g.held for g in shipping], *tied[len(taking) :])
    for gather, held in zip(shipping, tied):
        gather.held = held
        gather.ship()
    values = tied[len(shipping) :]
    return values[0] if len(values) == 1 else values


def body(
    prompt_in,
    cont_in,
    enc_out,
    prefix,
    prompt_cot,
    cont_cot,
    self_query,
    self_qbias,
    self_key,
    self_value,
    self_vbias,
    self_out,
    self_obias,
    gain_one,
    shift_one,
    cross_query,
    cross_qbias,
    cross_key,
    cross_value,
    cross_vbias,
    cross_out,
    cross_obias,
    gain_two,
    shift_two,
    inner_mat,
    inner_bias,
    outer_mat,
    outer_bias,
    gain_three,
    shift_three,
):
    seq = lax.axis_index("seq")
    parts, blocks = lax.axis_size("seq"), lax.axis_size("dp")
    rows = prompt_in.shape[1]
    width = prompt_in.shape[2]
    owned_rows = self_query.shape[0]
    group = seq // 2
    ids = jnp.stack([seq, 3 - seq, seq ^ 1, 3 - (seq ^ 1), prefix[group], seq & 1]).astype(jnp.int32)

    def pick(array, index):
        return lax.dynamic_index_in_dim(array, index, 0, keepdims=False)

    vectors = [
        self_qbias,
        self_vbias,
        self_obias,
        gain_one,
        shift_one,
        cross_qbias,
        cross_vbias,
        cross_obias,
        gain_two,
        shift_two,
        outer_bias,
        gain_three,
        shift_three,
    ]
    hidden_rows = outer_mat.shape[0]
    chunks = hidden_rows // owned_rows
    tail = pack_vectors(vectors + [inner_bias], width)
    moves = Moves()
    bits = moves.canonical
    dp_bits, hi, lo = bits[:-2], bits[-2], bits[-1]
    line, near = dp_bits[:-1], dp_bits[-1]
    cut = 2 * owned_rows
    first_part = jnp.concatenate([self_query, self_key, self_value, tail], axis=0)
    feed = jnp.concatenate(
        [outer_mat]
        + [inner_mat[:, i * width : (i + 1) * width] for i in range(chunks)]
        + [self_out, cross_query, cross_key, cross_value, cross_out],
        axis=0,
    )
    one = Gather(moves, first_part, line)
    one.ship()
    first_part, feed, sent = tie(
        first_part,
        feed,
        jnp.concatenate([pick(v, 1 - group) for v in (prompt_in, cont_in, enc_out)], axis=0),
    )
    feed = lax.all_gather(feed, ("dp", "seq"), axis=0, tiled=False)
    got = swap_seq(sent, 3)
    pump([one], [one])
    while len(one.order) > 1:
        pump([one], [one])
    got = pump([one], [], got)
    one_parts = [
        one.part(0, cut, [near, hi, lo]),
        one.part(cut, first_part.shape[0], [hi, near, lo]),
    ]
    got = pump([], one_parts, got)
    got = pump(one_parts, one_parts, got)
    got = pump(one_parts, one_parts, got)
    got = pump(one_parts, [], got)

    tokens = jnp.concatenate(
        [pick(prompt_in, group), got[:rows], pick(cont_in, group), got[rows : 2 * rows]], axis=0
    )
    encoder = jnp.concatenate([pick(enc_out, group), got[2 * rows :]], axis=0)

    def square(array, index):
        if owned_rows % 8 == 0:
            return array, (array.shape[0], owned_rows, width), (0, index, 0)
        part = array[:, index * owned_rows : (index + 1) * owned_rows].reshape(-1, width)
        return part, part.shape, (0, 0)

    front, back = [g.result() for g in one_parts]
    self_query, self_key, self_value = square(front, 0), square(front, 1), square(back, 0)
    tail = back[:, owned_rows:]
    owners = parts * blocks
    slots = tail.reshape(owners, 8, -1, 128)[:, :, :2, :owned_rows]
    vecs = slots.transpose(2, 1, 0, 3).reshape(16, width)[:13]
    biases = tail[:, 5, 128 : 128 + hidden_rows].reshape(chunks, width)
    vecs = widen(jnp.concatenate([vecs, biases], axis=0))

    queries, own = project(tokens, [self_query, self_key, self_value], vecs)
    other = swap_seq(own, 1)
    cot_sent = jnp.concatenate([pick(v, 1 - group) for v in (prompt_cot, cont_cot)], axis=0)
    cot_sent, other = tie(cot_sent, other)
    cot_got = swap_seq(cot_sent, 3)
    mixed, logsum = self_attend(ids, queries, own, other)
    mixed, cot_got = tie(mixed, cot_got)
    base = 2 * chunks
    self_out, cross_query, cross_key, cross_value, cross_out = [
        square(feed, base + i) for i in range(5)
    ]
    (cross_own,) = project(encoder, [cross_key, cross_value], vecs)
    cross_other = swap_seq(cross_own, 1)
    first_pre, first_low, cross_queries = self_finish(tokens, mixed, self_out, cross_query, vecs)
    cross_mixed, cross_logsum, second_pre, second_low = cross_attend(
        cross_queries, cross_own, cross_other, first_pre, cross_out, vecs
    )
    upstream = jnp.concatenate(
        [pick(prompt_cot, group), cot_got[:rows], pick(cont_cot, group), cot_got[rows:]], axis=0
    )
    active, slope, third_pre, result = feed_forward(
        second_pre, second_low, feed, vecs, chunks, owned_rows
    )

    def send_back(own, *values):
        away = jnp.concatenate([own[rows : 2 * rows], own[3 * rows :]], axis=0)
        tied = tie(away, *values)
        return (own, swap_seq(tied[0], 3)) + tuple(tied[1:])

    def place(own, back):
        kept = (own[:rows], own[2 * rows : 3 * rows])
        back = (back[:rows], back[rows:])
        return [
            jnp.where(group == 0, jnp.stack([a, b]), jnp.stack([b, a])) for a, b in zip(kept, back)
        ]

    result, result_back, third_pre = send_back(result, third_pre)

    bits = dp_bits[::-1]
    x_first = [lo, hi] + bits
    y_first = [lo, bits[0], hi] + bits[1:]
    inner_pair, outer_pair, cross_out_pair, second_grad, cross_mix, feed_sums = feed_backward(
        ids, upstream, third_pre, second_pre, second_low, active, slope, cross_mixed, feed, cross_out,
        vecs, chunks, owned_rows,
    )
    cross_mix, result_back = tie(cross_mix, result_back)
    prompt_out, cont_out = place(result, result_back)
    outer_chain = Scatter(moves, [outer_pair], x_first)
    inner_chain = Scatter(moves, [inner_pair], y_first)
    feed_chains = [outer_chain, inner_chain]
    cross_mix = depart(feed_chains, cross_mix)
    cross_mix = advance(feed_chains, cross_mix)
    own_back, other_back, first_grad, mix, cross_sums, query_pair = cross_backward(
        ids, cross_queries, cross_own, cross_other, cross_mixed, cross_mix, cross_logsum, first_low,
        first_pre, second_grad, mixed, cross_query, self_out, vecs, owned_rows,
    )
    mix, other_back = receive(feed_chains, mix, other_back)
    got_back = swap_seq(other_back, 1)
    got_back = depart(feed_chains, got_back)
    enc_back, key_sums, key_pair = key_backward(
        ids, encoder, own_back, got_back, None, cross_key, cross_value, owned_rows
    )
    cross_chains = [
        Scatter(moves, [query_pair, cross_out_pair], x_first),
        Scatter(moves, [key_pair], y_first),
    ]
    outer_chain.got, inner_chain.got, enc_back, mix = tie(
        outer_chain.got, inner_chain.got, enc_back, mix
    )
    mix = depart(cross_chains, mix)
    rest = jnp.concatenate([c.total() for c in feed_chains], axis=-2)
    rest, mix = tie(rest, mix)
    rest = rest.reshape((-1,) + rest.shape[-2:])
    lines = [[i for i in range(blocks) if i % 2 == side] for side in range(2)]
    rest = lax.psum_scatter(
        rest, "dp", scatter_dimension=0, axis_index_groups=lines, tiled=True
    )[0]
    mix = advance(cross_chains, mix)
    self_own, self_other, part, self_sums, self_query_pair = self_backward(
        ids, queries, own, other, mixed, mix, logsum, tokens, first_grad, self_query, owned_rows
    )
    self_other = receive(cross_chains, self_other)
    self_got = swap_seq(self_other, 1)
    self_got = depart(cross_chains, self_got)
    token_grad, self_key_sums, self_key_pair = key_backward(
        ids, tokens, self_own, self_got, part, self_key, self_value, owned_rows
    )
    token_grad = receive(cross_chains, token_grad)
    sums = jnp.concatenate(
        [
            self_sums[0:1],
            self_key_sums[0:1],
            cross_sums[2:3],
            cross_sums[0:2],
            cross_sums[3:4],
            key_sums[0:1],
            feed_sums[5:6],
            feed_sums[3:5],
            feed_sums[2:3],
            feed_sums[0:2],
        ],
        axis=0,
    )
    slots = jnp.pad(sums.reshape(13, owners, owned_rows), ((0, 3), (0, 0), (0, 128 - owned_rows)))
    slots = slots.reshape(2, 8, owners, 128).transpose(2, 1, 0, 3)
    bias_sums = feed_sums[8 : 8 + chunks].reshape(owners, hidden_rows)
    slots = slots.at[:, 5, 1, :hidden_rows].set(bias_sums)
    sums = jnp.pad(low(slots).reshape(owners, 8, 256), ((0, 0), (0, 0), (0, width - 256)))
    sums = sums.reshape(-1, 2, 8, width)
    sums_pair = (
        lax.dynamic_index_in_dim(sums, seq & 1, 1, keepdims=False),
        lax.dynamic_index_in_dim(sums, 1 - (seq & 1), 1, keepdims=False),
    )
    even_chain = Scatter(moves, [self_key_pair], x_first)
    odd_chain = Scatter(moves, [self_query_pair, sums_pair], y_first)
    last = [even_chain, odd_chain]
    token_grad, token_back = send_back(token_grad)
    depart(last)
    advance(last)
    advance(last)
    receive(last)
    tail_chain = joined(last + cross_chains)
    tail_chain.ship()
    while tail_chain.got is not None:
        receive([tail_chain])
        if tail_chain.order and tail_chain.away is not None:
            tail_chain.ship()
    ends, at = [], 0
    for size, extra in ((2, 0), (1, 8), (3, 0), (2, 0)):
        ends.append((at, at + size * owned_rows))
        at += size * owned_rows + extra
    self_key_grads, self_query_grad, cross_grads, cross_key_grads = [
        tail_chain.held[a:b].reshape(-1, owned_rows, width) for a, b in ends
    ]
    vec = tail_chain.held[ends[1][1] : ends[1][1] + 8].reshape(8, -1, 128)
    prompt_grad, cont_grad = place(token_grad, token_back)
    enc_rows = enc_out.shape[1]
    enc_got = swap_seq(enc_back[enc_rows:], 3)
    enc_grad = jnp.where(
        group == 0,
        jnp.stack([enc_back[:enc_rows], enc_got]),
        jnp.stack([enc_got, enc_back[:enc_rows]]),
    )

    rest = widen(rest)
    outer_mat_grad = rest[:hidden_rows]
    inner_mat_grad = jnp.concatenate(
        [rest[hidden_rows + i * owned_rows : hidden_rows + (i + 1) * owned_rows] for i in range(chunks)],
        axis=1,
    )
    vec_out = [vec[i % 8, i // 8, :owned_rows] for i in range(13)]
    inner_bias_out = vec[5, 1, :hidden_rows]
    return (
        prompt_out,
        cont_out,
        prompt_grad,
        cont_grad,
        enc_grad,
        self_query_grad[0],
        vec_out[0],
        self_key_grads[0],
        self_key_grads[1],
        vec_out[1],
        cross_grads[1],
        vec_out[2],
        vec_out[3],
        vec_out[4],
        cross_grads[0],
        vec_out[5],
        cross_key_grads[0],
        cross_key_grads[1],
        vec_out[6],
        cross_grads[2],
        vec_out[7],
        vec_out[8],
        vec_out[9],
        inner_mat_grad,
        inner_bias_out,
        outer_mat_grad,
        vec_out[10],
        vec_out[11],
        vec_out[12],
    )


def solution(mesh):
    rows_spec = P("dp", "seq", None)
    mat, vec = P(("dp", "seq"), None), P(("dp", "seq"))
    weights = (
        mat,
        vec,
        mat,
        mat,
        vec,
        mat,
        vec,
        vec,
        vec,
        mat,
        vec,
        mat,
        mat,
        vec,
        mat,
        vec,
        vec,
        vec,
        mat,
        vec,
        mat,
        vec,
        vec,
        vec,
    )
    in_specs = (rows_spec, rows_spec, rows_spec, P("dp"), rows_spec, rows_spec) + weights
    out_specs = (rows_spec,) * 5 + weights
    return jax.shard_map(body, mesh=mesh, in_specs=in_specs, out_specs=out_specs, check_vma=False)
```

time: 1740 us -> 438 us (0.25)
  waiting for transfers between devices: 772 us -> 158 us
  local copies, waits for them, and re-layouts: 333 us -> 36.2 us
  matrix products: 191 us -> 0 us
  blocking collectives: 182 us -> 0 us
  Pallas kernels: 0 us -> 164 us
  other arithmetic: 130 us -> 23.4 us
  starting transfers between devices: 97.1 us -> 34.6 us
    reduce_scatter x10 -> x1, waiting for transfers between devices: 339 us -> 2.87 us  [body(): lax.psum_scatter(rest, 'dp', scatter_dimension=0, axis_index_groups=lines...]
    all_gather x10 -> x1, waiting for transfers between devices: 261 us -> 37 us  [body(): feed = lax.all_gather(feed, ('dp', 'seq'), axis=0, tiled=False)]
    dot_general x228 -> x0, matrix products: 191 us -> none  [the longest x20 53.3 us: matmul(): return jnp.dot(left, right, preferred_element_type=jnp.float32)]
    all_to_all x24 -> x0, waiting for transfers between devices: 165 us -> none  [the longest x1 40.6 us: body(): lax.all_to_all(pieces[18].astype(jnp.bfloat16), 'seq', split_axis=1, conc...]
    pallas_call x0 -> x24, Pallas kernels: none -> 164 us  [the longest x11 128 us: run(): pl.pallas_call(kernel, grid=self.grid, in_specs=self.in_specs, out_specs=...]
    dynamic_slice x144 -> x2, local copies, waits for them, and re-layouts: 121 us -> 0.62 us  [the longest x1 0.58 us: body(): prefix[group]]
    ppermute x0 -> x37, waiting for transfers between devices: none -> 118 us  [the longest x28 113 us: send(): return lax.ppermute(values, name, flip(self.sizes[name], 1 << bit))]
    all_gather x12 -> x0, blocking collectives: 102 us -> none  [the longest x2 21.7 us: forward_pass(): lax.all_gather(keys_own[:prompt_rows], 'seq', axis=0, tiled=True)]
  transfers between devices with their start and end apart: 56 -> 39, of which waited for: 29 -> 25; matrix products, arithmetic and copies ran while one was open for 32% -> 8% of each run, Pallas kernels for 0% -> 27%
where the time goes in v1:
time: 438 us; the launch traced here: 432 us
  Pallas kernels  164 us (37%)
  waiting for transfers between devices  158 us (36%)
  local copies, waits for them, and re-layouts  36.2 us (8%)
  starting transfers between devices  34.6 us (8%)
  other arithmetic  23.4 us (5%)
  between operations  15.6 us (4%)
    pallas_call x11, Pallas kernels, run(): pl.pallas_call(kernel, grid=self.grid, in_specs=self.in_specs, out_specs=...  128 us
    ppermute x28, waiting for transfers between devices, send(): return lax.ppermute(values, name, flip(self.sizes[name], 1 << bit))  113 us
    all_gather x1, waiting for transfers between devices, body(): feed = lax.all_gather(feed, ('dp', 'seq'), axis=0, tiled=False)  37 us
    pallas_call x12, Pallas kernels, merge(): pl.pallas_call(kernel, grid_spec=pltpu.PrefetchScalarGridSpec(num_scalar_...  34.9 us
    ppermute x28, starting transfers between devices, send(): return lax.ppermute(values, name, flip(self.sizes[name], 1 << bit))  29.4 us
    unnamed x140, local copies, waits for them, and re-layouts  15.8 us
  transfers between devices with their start and end apart: 39, of which 25 were waited for; matrix products, arithmetic and copies ran while one was open for 8% of the time, Pallas kernels for 27%

profile of v1, /device:TPU:0, one launch (start us, length us, event | category | flops | bytes accessed | tf_op | source)
XLA Modules:
  0.0 432.0 jit_solution(5233803486910926510)
XLA Ops:
  16.8 4.1 collective-permute-start
  21.5 5.3 %collective-permute-done = bf16[80,768]{1,0:T(8,128)(2,1)S(1)} collective-permute-done((bf16[80,768]{1,0:T(8,128)(2,1)S(1)}, bf16[80,768]{1,0:T(8,128)(2,1)S(1)}, u32[]{:S(2)}, u32[]{:S(2)}) %collective-permute-start) | collective-permute-done | bytes 122912 | tf_op jit(solution)/shard_map/ppermute | solution.py:731
  28.4 12.2 %collective-permute-done.1 = bf16[2,80,768]{2,1,0:T(8,128)(2,1)S(1)} collective-permute-done((bf16[2,80,768]{2,1,0:T(8,128)(2,1)S(1)}, bf16[2,80,768]{2,1,0:T(8,128)(2,1)S(1)}, u32[]{:S(2)}, u32[]{:S(2)}) %collective-permute-start.1) | collective-permute-done | bytes 245792 | tf_op jit(solution)/shard_map/ppermute | solution.py:731
  44.2 4.4 %collective-permute-done.4 = bf16[2,2,32,768]{3,2,1,0:T(8,128)(2,1)S(1)} collective-permute-done((bf16[2,2,32,768]{3,2,1,0:T(8,128)(2,1)S(1)}, bf16[2,2,32,768]{3,2,1,0:T(8,128)(2,1)S(1)}, u32[]{:S(2)}, u32[]{:S(2)}) %collective-permute-start.4) | collective-permute-done | bytes 196640 | tf_op jit(solution)/shard_map/ppermute | solution.py:731
  48.7 2.5 collective-permute-start.5
  51.3 14.4 %collective-permute-done.6 = bf16[2,2,2,32,768]{4,3,2,1,0:T(8,128)(2,1)S(1)} collective-permute-done((bf16[2,2,2,32,768]{4,3,2,1,0:T(8,128)(2,1)S(1)}, bf16[2,2,2,32,768]{4,3,2,1,0:T(8,128)(2,1)S(1)}, u32[]{:S(2)}, u32[]{:S(2)}) %collective-permute-start.6) | collective-permute-done | bytes 393248 | tf_op jit(solution)/shard_map/ppermute | solution.py:731
  65.7 6.8 %collective-permute-done.5 = bf16[2,2,2,48,768]{4,3,2,1,0:T(8,128)(2,1)S(1)} collective-permute-done((bf16[2,2,2,48,768]{4,3,2,1,0:T(8,128)(2,1)S(1)}, bf16[2,2,2,48,768]{4,3,2,1,0:T(8,128)(2,1)S(1)}, u32[]{:S(2)}, u32[]{:S(2)}) %collective-permute-start.5) | collective-permute-done | bytes 589856 | tf_op jit(solution)/shard_map/ppermute | solution.py:731
  73.5 3.6 collective-permute-done.8
  84.6 5.5 %project.2 = (bf16[512,768]{1,0:T(8,128)(2,1)}, bf16[2,512,768]{2,1,0:T(8,128)(2,1)}) custom-call(bf16[512,768]{1,0:T(8,128)(2,1)} %pad_maximum_fusion.5.refs_0_.x_ref, bf16[32,48,768]{2,1,0:T(8,128)(2,1)} %bitcast.284, bf16[32,48,768]{2,1,0:T(8,128)(2,1)} %bitcast.285, bf16[32,32,768]{2,1,0:T(8,128)(2,1)} %bitcast.290, ...), custom_call_target="tpu_custom_call" | custom-call | flops 1811939328 | bytes 6736896 | tf_op jit(solution)/shard_map/project/pallas_call | solution.py:130
  93.7 2.2 collective-permute-start.10
  96.6 14.8 %self_attend.1 = (bf16[512,768]{1,0:T(8,128)(2,1)}, f32[6,2,512]{2,1,0:T(2,128)}) custom-call(s32[6]{0:T(128)} %stack.183.ids_ref.refs_0_, bf16[512,768]{1,0:T(8,128)(2,1)} %get-tuple-element.213.q_ref, bf16[2,512,768]{2,1,0:T(8,128)(2,1)} %get-tuple-element.214.own_ref, bf16[2,512,768]{2,1,0:T(8,128)(2,1)} %copy-done.61), custom_call_target="tpu_custom_call" | custom-call | flops 3221225472 | bytes 4743168 | tf_op jit(solution)/shard_map/self_attend/pallas_call | solution.py:130
  111.4 2.4 collective-permute-done.10
  113.8 37.0 %all-gather.3.cloned.1.call-done = bf16[9984,768]{1,0:T(8,128)(2,1)} async-done(((bf16[312,768]{1,0:T(8,128)(2,1)}), bf16[9984,768]{1,0:T(8,128)(2,1)}) %all-gather.3.cloned.1.call-update) | async-done | bytes 15335440 | tf_op jit(solution)/shard_map/all_gather | solution.py:973
  150.8 3.0 project.3.own_ref
  155.0 5.1 %self_finish.1 = (f32[512,768]{1,0:T(8,128)}, bf16[512,768]{1,0:T(8,128)(2,1)}, bf16[512,768]{1,0:T(8,128)(2,1)}) custom-call(bf16[512,768]{1,0:T(8,128)(2,1)} %pad_maximum_fusion.5.refs_0_.x_ref, bf16[512,768]{1,0:T(8,128)(2,1)} %get-tuple-element.218.mixed_ref.self_mixed_ref, bf16[32,312,768]{2,1,0:T(8,128)(2,1)} %bitcast.272, ...), custom_call_target="tpu_custom_call" | custom-call | flops 1207959552 | bytes 7130112 | tf_op jit(solution)/shard_map/self_finish/pallas_call | solution.py:130
  160.9 10.9 %cross_attend.1 = (bf16[512,768]{1,0:T(8,128)(2,1)}, f32[6,2,512]{2,1,0:T(2,128)}, f32[512,768]{1,0:T(8,128)}, bf16[512,768]{1,0:T(8,128)(2,1)}) custom-call(bf16[512,768]{1,0:T(8,128)(2,1)} %get-tuple-element.220.q_ref, bf16[2,128,768]{2,1,0:T(8,128)(2,1)} %project.3.own_ref, bf16[2,128,768]{2,1,0:T(8,128)(2,1)} %copy-done.12, ...), custom_call_target="tpu_custom_call" | custom-call | flops 1409286144 | bytes 7547904 | tf_op jit(solution)/shard_map/cross_attend/pallas_call | solution.py:130
  171.9 13.3 %feed_forward.1 = (bf16[512,3072]{1,0:T(8,128)(2,1)}, bf16[512,3072]{1,0:T(8,128)(2,1)}, f32[512,768]{1,0:T(8,128)}, bf16[512,768]{1,0:T(8,128)(2,1)}) custom-call(f32[512,768]{1,0:T(8,128)} %get-tuple-element.222.pre_ref.refs_3_, bf16[512,768]{1,0:T(8,128)(2,1)} %get-tuple-element.223.low_ref.refs_4_, bf16[32,312,768]{2,1,0:T(8,128)(2,1)} %bitcast.275, ...), custom_call_target="tpu_custom_call" | custom-call | flops 4831838208 | bytes 41733120 | tf_op jit(solution)/shard_map/feed_forward/pallas_call | solution.py:130
  185.2 2.0 slice_bitcast_fusion.7
  187.7 21.9 %feed_backward.1 = (bf16[16,4,24,768]{3,2,1,0:T(8,128)(2,1)}, bf16[16,4,24,768]{3,2,1,0:T(8,128)(2,1)}, bf16[16,1,96,768]{3,2,1,0:T(8,128)(2,1)}, bf16[16,1,96,7...) custom-call(s32[6]{0:T(128)} %stack.183.ids_ref.refs_0_, ...), custom_call_target="tpu_custom_call" | custom-call | flops 10871635968 | bytes 56724480 | tf_op jit(solution)/shard_map/feed_backward/pallas_call | solution.py:130
  210.9 5.1 %collective-permute-done.13 = bf16[2,2,2,2,96,768]{5,4,3,2,1,0:T(8,128)(2,1)S(1)} collective-permute-done((bf16[2,2,2,2,96,768]{5,4,3,2,1,0:T(8,128)(2,1)}, bf16[2,2,2,2,96,768]{5,4,3,2,1,0:T(8,128)(2,1)S(1)}, u32[]{:S(2)}, u32[]{:S(2)}) %collective-permute-start.13) | collective-permute-done | bytes 2359328 | tf_op jit(solution)/shard_map/ppermute | solution.py:731
  216.0 2.6 collective-permute-done.14
  218.6 4.3 merge.13
  222.9 4.5 %merge.12 = (bf16[8,96,768]{2,1,0:T(8,128)(2,1)}, bf16[8,96,768]{2,1,0:T(8,128)(2,1)}) custom-call(s32[1]{0:T(128)} %bitcast.57.mine_ref, bf16[8,2,96,768]{3,2,1,0:T(8,128)(2,1)} %bitcast.292, bf16[8,2,96,768]{3,2,1,0:T(8,128)(2,1)} %bitcast.293, bf16[8,2,96,768]{3,2,1,0:T(8,128)(2,1)} %bitcast.296, bf16[8,2,96,768]{3,2,1,0:T(8,128)(2,1)} %bitcast.297), custom_call_target="tpu_custom_call" | custom-call | flops 1179648 | bytes 7077888 | tf_op jit(solution)/shard_map/merge/pallas_call | solution.py:773
  230.3 17.2 %cross_backward.1 = (bf16[2,128,768]{2,1,0:T(8,128)(2,1)}, bf16[2,128,768]{2,1,0:T(8,128)(2,1)}, f32[512,768]{1,0:T(8,128)}, bf16[512,768]{1,0:T(8,128)(2,1)}, f...) custom-call(s32[6]{0:T(128)} %stack.183.ids_ref.refs_0_, ...), custom_call_target="tpu_custom_call" | custom-call | flops 4429185024 | bytes 15830016 | tf_op jit(solution)/shard_map/cross_backward/pallas_call | solution.py:130
  247.5 8.2 %collective-permute-done.15 = bf16[2,2,2,96,768]{4,3,2,1,0:T(8,128)(2,1)S(1)} collective-permute-done((bf16[2,2,2,96,768]{4,3,2,1,0:T(8,128)(2,1)}, bf16[2,2,2,96,768]{4,3,2,1,0:T(8,128)(2,1)S(1)}, u32[]{:S(2)}, u32[]{:S(2)}) %collective-permute-start.15) | collective-permute-done | bytes 1179680 | tf_op jit(solution)/shard_map/ppermute | solution.py:731
  257.8 2.5 merge.15
  260.3 2.9 merge.14
  267.4 4.6 %key_backward.2 = (bf16[128,768]{1,0:T(8,128)(2,1)}, f32[8,768]{1,0:T(8,128)}, bf16[16,2,24,768]{3,2,1,0:T(8,128)(2,1)}, bf16[16,2,24,768]{3,2,1,0:T(8,128)(2,1)}) custom-call(s32[6]{0:T(128)} %stack.183.ids_ref.refs_0_, bf16[128,768]{1,0:T(8,128)(2,1)} %pad_maximum_fusion.19.refs_0_.x_ref, bf16[2,128,768]{2,1,0:T(8,128)(2,1)} %get-tuple-element.255.mine_ref, ...), custom_call_target="tpu_custom_call" | custom-call | flops 603979776 | bytes 5922816 | tf_op jit(solution)/shard_map/key_backward/pallas_call | solution.py:130
  271.9 6.9 %collective-permute-done.18 = bf16[2,2,96,768]{3,2,1,0:T(8,128)(2,1)S(1)} collective-permute-done((bf16[2,2,96,768]{3,2,1,0:T(8,128)(2,1)}, bf16[2,2,96,768]{3,2,1,0:T(8,128)(2,1)S(1)}, u32[]{:S(2)}, u32[]{:S(2)}) %collective-permute-start.18) | collective-permute-done | bytes 589856 | tf_op jit(solution)/shard_map/ppermute | solution.py:731
  281.4 2.5 pad_maximum_fusion.keep_a.keep_b
  287.5 2.5 merge.17
  290.0 4.2 merge.16
  295.3 24.4 %self_backward.1 = (bf16[2,512,768]{2,1,0:T(8,128)(2,1)}, bf16[2,512,768]{2,1,0:T(8,128)(2,1)}, f32[512,768]{1,0:T(8,128)}, f32[8,768]{1,0:T(8,128)}, bf16[16,1,...) custom-call(s32[6]{0:T(128)} %stack.183.ids_ref.refs_0_, bf16[512,768]{1,0:T(8,128)(2,1)} %get-tuple-element.213.q_ref, ...), custom_call_target="tpu_custom_call" | custom-call | flops 9261023232 | bytes 14991360 | tf_op jit(solution)/shard_map/self_backward/pallas_call | solution.py:130
  323.1 2.1 merge.19
  325.3 2.4 merge.18
  328.8 7.2 %key_backward.3 = (bf16[512,768]{1,0:T(8,128)(2,1)}, f32[8,768]{1,0:T(8,128)}, bf16[16,2,24,768]{3,2,1,0:T(8,128)(2,1)}, bf16[16,2,24,768]{3,2,1,0:T(8,128)(2,1)}) custom-call(s32[6]{0:T(128)} %stack.183.ids_ref.refs_0_, bf16[512,768]{1,0:T(8,128)(2,1)} %pad_maximum_fusion.5.refs_0_.x_ref, bf16[2,512,768]{2,1,0:T(8,128)(2,1)} %get-tuple-element.303.mine_ref, ...), custom_call_target="tpu_custom_call" | custom-call | flops 2415919104 | bytes 11034624 | tf_op jit(solution)/shard_map/key_backward/pallas_call | solution.py:130
  345.7 2.9 reduce-scatter.2.cloned.1.call-done
  353.8 5.4 %collective-permute-done.26 = bf16[2,2,48,768]{3,2,0,1:T(8,128)(2,1)S(1)} collective-permute-done((bf16[2,2,48,768]{3,2,0,1:T(8,128)(2,1)S(1)}, bf16[2,2,48,768]{3,2,0,1:T(8,128)(2,1)S(1)}, u32[]{:S(2)}, u32[]{:S(2)}) %collective-permute-start.26) | collective-permute-done | bytes 294944 | tf_op jit(solution)/shard_map/ppermute | solution.py:731
  360.2 2.6 merge.21
  362.9 2.7 merge.20
  369.9 5.5 %collective-permute-done.32 = bf16[2,2,2,32,768]{4,3,0,1,2:T(8,128)(2,1)S(1)} collective-permute-done((bf16[2,2,2,32,768]{4,3,0,1,2:T(8,128)(2,1)S(1)}, bf16[2,2,2,32,768]{4,3,0,1,2:T(8,128)(2,1)S(1)}, u32[]{:S(2)}, u32[]{:S(2)}) %collective-permute-start.32) | collective-permute-done | bytes 393248 | tf_op jit(solution)/shard_map/ppermute | solution.py:731
  375.4 8.2 %collective-permute-done.31 = bf16[2,2,2,48,768]{4,3,2,1,0:T(8,128)(2,1)S(1)} collective-permute-done((bf16[2,2,2,48,768]{4,3,2,1,0:T(8,128)(2,1)}, bf16[2,2,2,48,768]{4,3,2,1,0:T(8,128)(2,1)S(1)}, u32[]{:S(2)}, u32[]{:S(2)}) %collective-permute-start.31) | collective-permute-done | bytes 589856 | tf_op jit(solution)/shard_map/ppermute | solution.py:731
  384.5 2.1 merge.22
  389.9 4.1 collective-permute-done.34
  397.8 9.3 %collective-permute-done.35 = bf16[2,200,768]{2,1,0:T(8,128)(2,1)S(1)} collective-permute-done((bf16[2,200,768]{2,1,0:T(8,128)(2,1)S(1)}, bf16[2,200,768]{2,1,0:T(8,128)(2,1)S(1)}, u32[]{:S(2)}, u32[]{:S(2)}) %collective-permute-start.35) | collective-permute-done | bytes 614432 | tf_op jit(solution)/shard_map/ppermute | solution.py:731
  407.9 2.1 merge.23
  410.1 2.2 collective-permute-start.36
  413.9 8.8 %collective-permute-done.36 = bf16[200,768]{1,0:T(8,128)(2,1)S(1)} collective-permute-done((bf16[200,768]{1,0:T(8,128)(2,1)}, bf16[200,768]{1,0:T(8,128)(2,1)S(1)}, u32[]{:S(2)}, u32[]{:S(2)}) %collective-permute-start.36) | collective-permute-done | bytes 307232 | tf_op jit(solution)/shard_map/ppermute | solution.py:731
  (297 shorter events, 85.0 us)
Async XLA Ops:
  7.2 7.1 %copy-start.59 = (bf16[24,768]{1,0:T(8,128)(2,1)S(1)}, bf16[24,768]{1,0:T(8,128)(2,1)}, u32[]{:S(2)}) copy-start(bf16[24,768]{1,0:T(8,128)(2,1)} %param.52) | copy-start | bytes 110596
  7.3 143.6 %all-gather.3.cloned.1.call-start = ((), (), s32[]{:S(2)}) async-start(), calls=%async_computation.2 | async-start | bytes 15814656 | tf_op jit(solution)/shard_map/all_gather | solution.py:973
  16.7 331.9 %reduce-scatter.2.cloned.1.call-start = ((), (), s32[]{:S(2)}) async-start(), calls=%async_computation.1 | async-start | bytes 1474560 | tf_op jit(solution)/shard_map/reduce_scatter | solution.py:1082
  16.8 10.1 %collective-permute-start = (bf16[80,768]{1,0:T(8,128)(2,1)S(1)}, bf16[80,768]{1,0:T(8,128)(2,1)S(1)}, u32[]{:S(2)}, u32[]{:S(2)}) collective-permute-start(bf16[80,768]{1,0:T(8,128)(2,1)S(1)} %pad_maximum_fusion.20), channel_id=1, source_target_pairs={{0,16},{4,20},{8,24},{12,28},{16,0},{20,4},{24,8},{28,12},{1,17},{... | collective-permute-start | bytes 368648 | tf_op jit(solution)/shard_map/ppermute | solution.py:731
  20.9 19.7 %collective-permute-start.2 = (bf16[320,768]{1,0:T(8,128)(2,1)S(1)}, bf16[320,768]{1,0:T(8,128)(2,1)S(1)}, u32[]{:S(2)}, u32[]{:S(2)}) collective-permute-start(bf16[320,768]{1,0:T(8,128)(2,1)S(1)} %pad_maximum_fusion.11), channel_id=1, source_target_pairs={{0,3},{1,2},{2,1},{3,0},{4,7},{5,6},{6,5},{7,4},{8,11},{9,10},{10,... | collective-permute-start | bytes 1474568 | tf_op jit(solution)/shard_map/ppermute | solution.py:707
  27.6 13.0 %collective-permute-start.1 = (bf16[2,80,768]{2,1,0:T(8,128)(2,1)S(1)}, bf16[2,80,768]{2,1,0:T(8,128)(2,1)S(1)}, u32[]{:S(2)}, u32[]{:S(2)}) collective-permute-start(bf16[2,80,768]{2,1,0:T(8,128)(2,1)S(1)} %pad_maximum_fusion.17), channel_id=1, source_target_pairs={{0,8},{4,12},{8,0},{12,4},{16,24},{20,28},{24,16},{28,20},{1,9},{5... | collective-permute-start | bytes 737288 | tf_op jit(solution)/shard_map/ppermute | solution.py:731
  41.4 7.1 %collective-permute-start.3 = (bf16[2,2,48,768]{3,2,1,0:T(8,128)(2,1)S(1)}, bf16[2,2,48,768]{3,2,1,0:T(8,128)(2,1)S(1)}, u32[]{:S(2)}, u32[]{:S(2)}) collective-permute-start(bf16[2,2,48,768]{3,2,1,0:T(8,128)(2,1)S(1)} %fusion.7), channel_id=1, source_target_pairs={{0,4},{4,0},{8,12},{12,8},{16,20},{20,16},{24,28},{28,24},{1,5},{5... | collective-permute-start | bytes 884744 | tf_op jit(solution)/shard_map/ppermute | solution.py:731
  42.5 6.0 %collective-permute-start.4 = (bf16[2,2,32,768]{3,2,1,0:T(8,128)(2,1)S(1)}, bf16[2,2,32,768]{3,2,1,0:T(8,128)(2,1)S(1)}, u32[]{:S(2)}, u32[]{:S(2)}) collective-permute-start(bf16[2,2,32,768]{3,2,1,0:T(8,128)(2,1)S(1)} %pad_maximum_fusion.18), channel_id=1, source_target_pairs={{0,2},{1,3},{2,0},{3,1},{4,6},{5,7},{6,4},{7,5},{8,10},{9,11},{10,... | collective-permute-start | bytes 589832 | tf_op jit(solution)/shard_map/ppermute | solution.py:731
  48.7 23.8 %collective-permute-start.5 = (bf16[2,2,2,48,768]{4,3,2,1,0:T(8,128)(2,1)S(1)}, bf16[2,2,2,48,768]{4,3,2,1,0:T(8,128)(2,1)S(1)}, u32[]{:S(2)}, u32[]{:S(2)}) collective-permute-start(bf16[2,2,2,48,768]{4,3,2,1,0:T(8,128)(2,1)S(1)} %pad_maximum_fusion.10), channel_id=1, source_target_pairs={{0,2},{1,3},{2,0},{3,1},{4,6},{5,7},{6,4},{7,5},{8,10},{9,11},{10,... | collective-permute-start | bytes 1769480 | tf_op jit(solution)/shard_map/ppermute | solution.py:731
  51.3 14.5 %collective-permute-start.6 = (bf16[2,2,2,32,768]{4,3,2,1,0:T(8,128)(2,1)S(1)}, bf16[2,2,2,32,768]{4,3,2,1,0:T(8,128)(2,1)S(1)}, u32[]{:S(2)}, u32[]{:S(2)}) collective-permute-start(bf16[2,2,2,32,768]{4,3,2,1,0:T(8,128)(2,1)S(1)} %pad_maximum_fusion.12), channel_id=1, source_target_pairs={{0,4},{4,0},{8,12},{12,8},{16,20},{20,16},{24,28},{28,24},{1,5},{5... | collective-permute-start | bytes 1179656 | tf_op jit(solution)/shard_map/ppermute | solution.py:731
  72.9 4.2 collective-permute-start.7
  73.0 4.1 collective-permute-start.8
  84.6 7.4 %copy-start.38 = (bf16[2,128,768]{2,1,0:T(8,128)(2,1)S(1)}, bf16[2,128,768]{2,1,0:T(8,128)(2,1)}, u32[]{:S(2)}) copy-start(bf16[2,128,768]{2,1,0:T(8,128)(2,1)} %param.37) | copy-start | bytes 1179652
  84.6 7.4 %copy-start.39 = (bf16[2,128,768]{2,1,0:T(8,128)(2,1)S(1)}, bf16[2,128,768]{2,1,0:T(8,128)(2,1)}, u32[]{:S(2)}) copy-start(bf16[2,128,768]{2,1,0:T(8,128)(2,1)} %param.36) | copy-start | bytes 1179652
  90.1 3.6 collective-permute-start.9
  93.7 20.1 %collective-permute-start.10 = (bf16[256,768]{1,0:T(8,128)(2,1)S(1)}, bf16[256,768]{1,0:T(8,128)(2,1)S(1)}, u32[]{:S(2)}, u32[]{:S(2)}) collective-permute-start(bf16[256,768]{1,0:T(8,128)(2,1)S(1)} %pad_maximum_fusion.13), channel_id=1, source_target_pairs={{0,3},{1,2},{2,1},{3,0},{4,7},{5,6},{6,5},{7,4},{8,11},{9,10},{10,... | collective-permute-start | bytes 1179656 | tf_op jit(solution)/shard_map/ppermute | solution.py:707
  153.8 6.4 %collective-permute-start.11 = (bf16[2,128,768]{2,1,0:T(8,128)(2,1)}, bf16[2,128,768]{2,1,0:T(8,128)(2,1)S(1)}, u32[]{:S(2)}, u32[]{:S(2)}) collective-permute-start(bf16[2,128,768]{2,1,0:T(8,128)(2,1)} %project.3.own_ref), channel_id=1, source_target_pairs={{0,1},{1,0},{2,3},{3,2},{4,5},{5,4},{6,7},{7,6},{8,9},{9,8},{10,11... | collective-permute-start | bytes 1179656 | tf_op jit(solution)/shard_map/ppermute | solution.py:707
  187.2 22.4 %collective-permute-start.12 = (bf16[256,768]{1,0:T(8,128)(2,1)S(1)}, bf16[256,768]{1,0:T(8,128)(2,1)S(1)}, u32[]{:S(2)}, u32[]{:S(2)}) collective-permute-start(bf16[256,768]{1,0:T(8,128)(2,1)S(1)} %pad_maximum_fusion.14), channel_id=1, source_target_pairs={{0,3},{1,2},{2,1},{3,0},{4,7},{5,6},{6,5},{7,4},{8,11},{9,10},{10,... | collective-permute-start | bytes 1179656 | tf_op jit(solution)/shard_map/ppermute | solution.py:707
  210.4 5.6 %collective-permute-start.13 = (bf16[2,2,2,2,96,768]{5,4,3,2,1,0:T(8,128)(2,1)}, bf16[2,2,2,2,96,768]{5,4,3,2,1,0:T(8,128)(2,1)S(1)}, u32[]{:S(2)}, u32[]{:S(2)}) collective-permute-start(bf16[2,2,2,2,96,768]{5,4,3,2,1,0:T(8,128)(2,1)} %bitcast.376), channel_id=1, source_target_pairs={{0,1},{1,0},{2,3},{3,2},{4,5},{5,4},{6,7},{7,6},{8,9},{9,8},{10,11... | collective-permute-start | bytes 7077896 | tf_op jit(solution)/shard_map/ppermute | solution.py:731
  210.6 8.0 %collective-permute-start.14 = (bf16[2,2,2,2,96,768]{5,4,3,2,1,0:T(8,128)(2,1)}, bf16[2,2,2,2,96,768]{5,4,3,2,1,0:T(8,128)(2,1)}, u32[]{:S(2)}, u32[]{:S(2)}) collective-permute-start(bf16[2,2,2,2,96,768]{5,4,3,2,1,0:T(8,128)(2,1)} %bitcast.375), channel_id=1, source_target_pairs={{0,1},{1,0},{2,3},{3,2},{4,5},{5,4},{6,7},{7,6},{8,9},{9,8},{10,11... | collective-permute-start | bytes 7077896 | tf_op jit(solution)/shard_map/ppermute | solution.py:731
  227.4 28.3 %collective-permute-start.15 = (bf16[2,2,2,96,768]{4,3,2,1,0:T(8,128)(2,1)}, bf16[2,2,2,96,768]{4,3,2,1,0:T(8,128)(2,1)S(1)}, u32[]{:S(2)}, u32[]{:S(2)}) collective-permute-start(bf16[2,2,2,96,768]{4,3,2,1,0:T(8,128)(2,1)} %bitcast.380), channel_id=1, source_target_pairs={{0,2},{1,3},{2,0},{3,1},{4,6},{5,7},{6,4},{7,5},{8,10},{9,11},{10,... | collective-permute-start | bytes 3538952 | tf_op jit(solution)/shard_map/ppermute | solution.py:731
  228.8 27.9 %collective-permute-start.16 = (bf16[2,2,2,96,768]{4,3,2,1,0:T(8,128)(2,1)S(1)}, bf16[2,2,2,96,768]{4,3,2,1,0:T(8,128)(2,1)S(1)}, u32[]{:S(2)}, u32[]{:S(2)}) collective-permute-start(bf16[2,2,2,96,768]{4,3,2,1,0:T(8,128)(2,1)S(1)} %bitcast.378), channel_id=1, source_target_pairs={{0,4},{4,0},{8,12},{12,8},{16,20},{20,16},{24,28},{28,24},{1,5},{5... | collective-permute-start | bytes 3538952 | tf_op jit(solution)/shard_map/ppermute | solution.py:731
  256.7 6.5 %collective-permute-start.17 = (bf16[2,128,768]{2,1,0:T(8,128)(2,1)}, bf16[2,128,768]{2,1,0:T(8,128)(2,1)S(1)}, u32[]{:S(2)}, u32[]{:S(2)}) collective-permute-start(bf16[2,128,768]{2,1,0:T(8,128)(2,1)} %get-tuple-element.266), channel_id=1, source_target_pairs={{0,1},{1,0},{2,3},{3,2},{4,5},{5,4},{6,7},{7,6},{8,9},{9,8},{10,11... | collective-permute-start | bytes 1179656 | tf_op jit(solution)/shard_map/ppermute | solution.py:707
  263.9 14.9 %collective-permute-start.18 = (bf16[2,2,96,768]{3,2,1,0:T(8,128)(2,1)}, bf16[2,2,96,768]{3,2,1,0:T(8,128)(2,1)S(1)}, u32[]{:S(2)}, u32[]{:S(2)}) collective-permute-start(bf16[2,2,96,768]{3,2,1,0:T(8,128)(2,1)} %bitcast.384), channel_id=1, source_target_pairs={{0,4},{4,0},{8,12},{12,8},{16,20},{20,16},{24,28},{28,24},{1,5},{5... | collective-permute-start | bytes 1769480 | tf_op jit(solution)/shard_map/ppermute | solution.py:731
  265.4 14.6 %collective-permute-start.19 = (bf16[2,2,96,768]{3,2,1,0:T(8,128)(2,1)}, bf16[2,2,96,768]{3,2,1,0:T(8,128)(2,1)S(1)}, u32[]{:S(2)}, u32[]{:S(2)}) collective-permute-start(bf16[2,2,96,768]{3,2,1,0:T(8,128)(2,1)} %bitcast.75), channel_id=1, source_target_pairs={{0,2},{1,3},{2,0},{3,1},{4,6},{5,7},{6,4},{7,5},{8,10},{9,11},{10,... | collective-permute-start | bytes 1769480 | tf_op jit(solution)/shard_map/ppermute | solution.py:731
  267.4 14.0 %copy-start.14 = (bf16[16,2,24,768]{3,2,1,0:T(8,128)(2,1)S(1)}, bf16[16,2,24,768]{3,2,1,0:T(8,128)(2,1)}, u32[]{:S(2)}) copy-start(bf16[16,2,24,768]{3,2,1,0:T(8,128)(2,1)} %get-tuple-element.251) | copy-start | bytes 3538948
  280.9 5.6 %collective-permute-start.20 = (bf16[2,2,2,2,72,768]{5,4,3,2,1,0:T(8,128)(2,1)}, bf16[2,2,2,2,72,768]{5,4,3,2,1,0:T(8,128)(2,1)S(1)}, u32[]{:S(2)}, u32[]{:S(2)}) collective-permute-start(bf16[2,2,2,2,72,768]{5,4,3,2,1,0:T(8,128)(2,1)} %pad_maximum_fusion.1), channel_id=1, source_target_pairs={{0,1},{1,0},{2,3},{3,2},{4,5},{5,4},{6,7},{7,6},{8,9},{9,8},{10,11... | collective-permute-start | bytes 5308424 | tf_op jit(solution)/shard_map/ppermute | solution.py:731
  280.9 5.6 %collective-permute-start.21 = (bf16[2,2,2,2,48,768]{5,4,3,2,1,0:T(8,128)(2,1)}, bf16[2,2,2,2,48,768]{5,4,3,2,1,0:T(8,128)(2,1)S(1)}, u32[]{:S(2)}, u32[]{:S(2)}) collective-permute-start(bf16[2,2,2,2,48,768]{5,4,3,2,1,0:T(8,128)(2,1)} %bitcast.379), channel_id=1, source_target_pairs={{0,1},{1,0},{2,3},{3,2},{4,5},{5,4},{6,7},{7,6},{8,9},{9,8},{10,11... | collective-permute-start | bytes 3538952 | tf_op jit(solution)/shard_map/ppermute | solution.py:731
  294.2 25.6 %collective-permute-start.22 = (bf16[2,2,2,72,768]{4,3,2,1,0:T(8,128)(2,1)}, bf16[2,2,2,72,768]{4,3,2,1,0:T(8,128)(2,1)S(1)}, u32[]{:S(2)}, u32[]{:S(2)}) collective-permute-start(bf16[2,2,2,72,768]{4,3,2,1,0:T(8,128)(2,1)} %bitcast.381), channel_id=1, source_target_pairs={{0,2},{1,3},{2,0},{3,1},{4,6},{5,7},{6,4},{7,5},{8,10},{9,11},{10,... | collective-permute-start | bytes 2654216 | tf_op jit(solution)/shard_map/ppermute | solution.py:731
  294.8 25.0 %collective-permute-start.23 = (bf16[2,2,2,48,768]{4,3,2,1,0:T(8,128)(2,1)S(1)}, bf16[2,2,2,48,768]{4,3,2,1,0:T(8,128)(2,1)S(1)}, u32[]{:S(2)}, u32[]{:S(2)}) collective-permute-start(bf16[2,2,2,48,768]{4,3,2,1,0:T(8,128)(2,1)S(1)} %bitcast.383), channel_id=1, source_target_pairs={{0,4},{4,0},{8,12},{12,8},{16,20},{20,16},{24,28},{28,24},{1,5},{5... | collective-permute-start | bytes 1769480 | tf_op jit(solution)/shard_map/ppermute | solution.py:731
  295.3 24.6 %copy-start.60 = (f32[16,768]{1,0:T(8,128)S(1)}, f32[16,768]{1,0:T(8,128)}, u32[]{:S(2)}) copy-start(f32[16,768]{1,0:T(8,128)} %get-tuple-element.316) | copy-start | bytes 147460
  319.8 7.9 %collective-permute-start.24 = (bf16[2,512,768]{2,1,0:T(8,128)(2,1)}, bf16[2,512,768]{2,1,0:T(8,128)(2,1)S(1)}, u32[]{:S(2)}, u32[]{:S(2)}) collective-permute-start(bf16[2,512,768]{2,1,0:T(8,128)(2,1)} %get-tuple-element.300), channel_id=1, source_target_pairs={{0,1},{1,0},{2,3},{3,2},{4,5},{5,4},{6,7},{7,6},{8,9},{9,8},{10,11... | collective-permute-start | bytes 4718600 | tf_op jit(solution)/shard_map/ppermute | solution.py:707
  338.0 21.2 %collective-permute-start.29 = (bf16[2,2,2,2,48,768]{5,4,3,2,1,0:T(8,128)(2,1)}, bf16[2,2,2,2,48,768]{5,4,3,2,1,0:T(8,128)(2,1)S(1)}, u32[]{:S(2)}, u32[]{:S(2)}) collective-permute-start(bf16[2,2,2,2,48,768]{5,4,3,2,1,0:T(8,128)(2,1)} %bitcast.377), channel_id=1, source_target_pairs={{0,1},{1,0},{2,3},{3,2},{4,5},{5,4},{6,7},{7,6},{8,9},{9,8},{10,11... | collective-permute-start | bytes 3538952 | tf_op jit(solution)/shard_map/ppermute | solution.py:731
  339.6 19.6 %collective-permute-start.30 = (bf16[2,2,2,2,32,768]{5,4,3,2,1,0:T(8,128)(2,1)S(1)}, bf16[2,2,2,2,32,768]{5,4,3,2,1,0:T(8,128)(2,1)S(1)}, u32[]{:S(2)}, u32[]{:S(2)}) collective-permute-start(bf16[2,2,2,2,32,768]{5,4,3,2,1,0:T(8,128)(2,1)S(1)} %pad_maximum_fusion.7), channel_id=1, source_target_pairs={{0,1},{1,0},{2,3},{3,2},{4,5},{5,4},{6,7},{7,6},{8,9},{9,8},{10,11... | collective-permute-start | bytes 2359304 | tf_op jit(solution)/shard_map/ppermute | solution.py:731
  340.1 4.9 %collective-permute-start.28 = (bf16[64,768]{1,0:T(8,128)(2,1)S(1)}, bf16[64,768]{1,0:T(8,128)(2,1)S(1)}, u32[]{:S(2)}, u32[]{:S(2)}) collective-permute-start(bf16[64,768]{1,0:T(8,128)(2,1)S(1)} %get-tuple-element.406), channel_id=1, source_target_pairs={{0,3},{1,2},{2,1},{3,0},{4,7},{5,6},{6,5},{7,4},{8,11},{9,10},{10,... | collective-permute-start | bytes 294920 | tf_op jit(solution)/shard_map/ppermute | solution.py:707
  342.1 10.7 %copy-start.21 = (bf16[16,1,24,768]{3,2,1,0:T(8,128)(2,1)S(1)}, bf16[16,1,24,768]{3,2,1,0:T(8,128)(2,1)}, u32[]{:S(2)}) copy-start(bf16[16,1,24,768]{3,2,1,0:T(8,128)(2,1)} %get-tuple-element.322) | copy-start | bytes 1769476
  342.9 16.3 %collective-permute-start.25 = (bf16[2,2,72,768]{3,2,0,1:T(8,128)(2,1)}, bf16[2,2,72,768]{3,2,0,1:T(8,128)(2,1)}, u32[]{:S(2)}, u32[]{:S(2)}) collective-permute-start(bf16[2,2,72,768]{3,2,0,1:T(8,128)(2,1)} %copy.88), channel_id=1, source_target_pairs={{0,4},{4,0},{8,12},{12,8},{16,20},{20,16},{24,28},{28,24},{1,5},{5... | collective-permute-start | bytes 1327112 | tf_op jit(solution)/shard_map/ppermute | solution.py:731
  350.6 8.6 %collective-permute-start.26 = (bf16[2,2,48,768]{3,2,0,1:T(8,128)(2,1)S(1)}, bf16[2,2,48,768]{3,2,0,1:T(8,128)(2,1)S(1)}, u32[]{:S(2)}, u32[]{:S(2)}) collective-permute-start(bf16[2,2,48,768]{3,2,0,1:T(8,128)(2,1)S(1)} %copy.89), channel_id=1, source_target_pairs={{0,2},{1,3},{2,0},{3,1},{4,6},{5,7},{6,4},{7,5},{8,10},{9,11},{10,... | collective-permute-start | bytes 884744 | tf_op jit(solution)/shard_map/ppermute | solution.py:731
  365.6 18.0 %copy-start.40 = (bf16[4,64,768]{2,1,0:T(8,128)(2,1)S(1)}, bf16[4,64,768]{2,1,0:T(8,128)(2,1)}, u32[]{:S(2)}) copy-start(bf16[4,64,768]{2,1,0:T(8,128)(2,1)} %get-tuple-element.330) | copy-start | bytes 1179652
  365.6 9.8 %collective-permute-start.32 = (bf16[2,2,2,32,768]{4,3,0,1,2:T(8,128)(2,1)S(1)}, bf16[2,2,2,32,768]{4,3,0,1,2:T(8,128)(2,1)S(1)}, u32[]{:S(2)}, u32[]{:S(2)}) collective-permute-start(bf16[2,2,2,32,768]{4,3,0,1,2:T(8,128)(2,1)S(1)} %copy.92), channel_id=1, source_target_pairs={{0,4},{4,0},{8,12},{12,8},{16,20},{20,16},{24,28},{28,24},{1,5},{5... | collective-permute-start | bytes 1179656 | tf_op jit(solution)/shard_map/ppermute | solution.py:731
  367.1 16.5 %collective-permute-start.31 = (bf16[2,2,2,48,768]{4,3,2,1,0:T(8,128)(2,1)}, bf16[2,2,2,48,768]{4,3,2,1,0:T(8,128)(2,1)S(1)}, u32[]{:S(2)}, u32[]{:S(2)}) collective-permute-start(bf16[2,2,2,48,768]{4,3,2,1,0:T(8,128)(2,1)} %bitcast.382), channel_id=1, source_target_pairs={{0,2},{1,3},{2,0},{3,1},{4,6},{5,7},{6,4},{7,5},{8,10},{9,11},{10,... | collective-permute-start | bytes 1769480 | tf_op jit(solution)/shard_map/ppermute | solution.py:731
  368.7 43.6 %collective-permute-start.27 = (bf16[256,768]{1,0:T(8,128)(2,1)S(1)}, bf16[256,768]{1,0:T(8,128)(2,1)S(1)}, u32[]{:S(2)}, u32[]{:S(2)}) collective-permute-start(bf16[256,768]{1,0:T(8,128)(2,1)S(1)} %pad_maximum_fusion.15), channel_id=1, source_target_pairs={{0,3},{1,2},{2,1},{3,0},{4,7},{5,6},{6,5},{7,4},{8,11},{9,10},{10,... | collective-permute-start | bytes 1179656 | tf_op jit(solution)/shard_map/ppermute | solution.py:707
  386.6 7.8 %copy-start.50 = (bf16[4,48,768]{2,1,0:T(8,128)(2,1)S(1)}, bf16[4,48,768]{2,1,0:T(8,128)(2,1)}, u32[]{:S(2)}) copy-start(bf16[4,48,768]{2,1,0:T(8,128)(2,1)} %get-tuple-element.328) | copy-start | bytes 884740
  387.6 6.8 %collective-permute-start.33 = (bf16[2,2,48,768]{3,2,0,1:T(8,128)(2,1)S(1)}, bf16[2,2,48,768]{3,2,0,1:T(8,128)(2,1)S(1)}, u32[]{:S(2)}, u32[]{:S(2)}) collective-permute-start(bf16[2,2,48,768]{3,2,0,1:T(8,128)(2,1)S(1)} %copy.94), channel_id=1, source_target_pairs={{0,4},{4,0},{8,12},{12,8},{16,20},{20,16},{24,28},{28,24},{1,5},{5... | collective-permute-start | bytes 884744 | tf_op jit(solution)/shard_map/ppermute | solution.py:731
  388.3 5.7 %collective-permute-start.34 = (bf16[2,2,32,768]{3,2,0,1:T(8,128)(2,1)S(1)}, bf16[2,2,32,768]{3,2,0,1:T(8,128)(2,1)S(1)}, u32[]{:S(2)}, u32[]{:S(2)}) collective-permute-start(bf16[2,2,32,768]{3,2,0,1:T(8,128)(2,1)S(1)} %dynamic-slice_bitcast_fusion.2), channel_id=1, source_target_pairs={{0,2},{1,3},{2,0},{3,1},{4,6},{5,7},{6,4},{7,5},{8,10},{9,11},{10,... | collective-permute-start | bytes 589832 | tf_op jit(solution)/shard_map/ppermute | solution.py:731
  394.7 12.4 %collective-permute-start.35 = (bf16[2,200,768]{2,1,0:T(8,128)(2,1)S(1)}, bf16[2,200,768]{2,1,0:T(8,128)(2,1)S(1)}, u32[]{:S(2)}, u32[]{:S(2)}) collective-permute-start(bf16[2,200,768]{2,1,0:T(8,128)(2,1)S(1)} %pad_maximum_fusion.9), channel_id=1, source_target_pairs={{0,8},{4,12},{8,0},{12,4},{16,24},{20,28},{24,16},{28,20},{1,9},{5... | collective-permute-start | bytes 1843208 | tf_op jit(solution)/shard_map/ppermute | solution.py:731
  410.1 12.7 %copy-start.42 = (bf16[1,200,768]{2,1,0:T(8,128)(2,1)S(1)}, bf16[1,200,768]{2,1,0:T(8,128)(2,1)}, u32[]{:S(2)}) copy-start(bf16[1,200,768]{2,1,0:T(8,128)(2,1)} %get-tuple-element.340) | copy-start | bytes 921604
  410.1 12.6 %collective-permute-start.36 = (bf16[200,768]{1,0:T(8,128)(2,1)}, bf16[200,768]{1,0:T(8,128)(2,1)S(1)}, u32[]{:S(2)}, u32[]{:S(2)}) collective-permute-start(bf16[200,768]{1,0:T(8,128)(2,1)} %bitcast.385), channel_id=1, source_target_pairs={{0,16},{4,20},{8,24},{12,28},{16,0},{20,4},{24,8},{28,12},{1,17},{... | collective-permute-start | bytes 921608 | tf_op jit(solution)/shard_map/ppermute | solution.py:731
  (57 other events, 171.9 us)
Sparse Core Ops, SparseCore 0:
  16.8 133.9 all-gather.2
  320.0 28.4 reduce-scatter.1

commit v2 on v1

--- a/solution.py
+++ b/solution.py
@@ -456,67 +456,82 @@
     return call.run(kernel)
 
 
-def feed_backward(
-    ids, upstream, third_pre, second_pre, second_low, active, slope, cross_mixed, feed, out_weight, vecs,
+def outer_backward(ids, upstream, third_pre, active, vecs, chunks, owned_rows):
+    rows, width = third_pre.shape
+    owners = width // owned_rows
+    call = Call("outer_backward", (chunks,))
+    call.scalars(ids)
+    call.whole(upstream)
+    call.whole(third_pre)
+    call.blocked(active, (rows, width), lambda i: (0, i))
+    call.whole(vecs)
+    call.out((rows, width), jnp.float32)
+    call.out((rows, width), jnp.bfloat16)
+    call.out((24, width), jnp.float32)
+    half = Halves(
+        call, 1, owners, chunks * owned_rows, width, owners // 2 // chunks, lambda i: (i, 0)
+    )
+    call.flops = 2 * rows * chunks * width * width
+
+    def kernel(ids_ref, up_ref, third_ref, active_ref, vecs_ref, grad_ref, low_ref, sums_ref, *grads):
+        @pl.when(pl.program_id(0) == 0)
+        def _():
+            grad, gain_sum, shift_sum = norm_backward(
+                third_ref[...], row(vecs_ref, GAIN_THREE), widen(up_ref[...])
+            )
+            grad_ref[...] = grad
+            low_ref[...] = low(grad)
+            sums_ref[...] = jnp.zeros_like(sums_ref)
+            sums_ref[GAIN_THREE : GAIN_THREE + 1, :] = gain_sum
+            sums_ref[SHIFT_THREE : SHIFT_THREE + 1, :] = shift_sum
+            sums_ref[OUTER_B : OUTER_B + 1, :] = jnp.sum(widen(low(grad)), axis=0, keepdims=True)
+
+        half.store(grads, 0, contract_rows(active_ref[...], low_ref[...]), ids_ref[5])
+
+    results = call.run(kernel)
+    return tuple(results[:3]) + (half.pair(results[3:], ids[5]),)
+
+
+def inner_backward(
+    ids, third_grad, third_low, sums, second_pre, second_low, slope, cross_mixed, feed, out_weight, vecs,
     chunks, owned_rows,
 ):
     rows, width = second_low.shape
-    hidden = chunks * width
     owners = width // owned_rows
-    call = Call("feed_backward", (chunks,))
+    call = Call("inner_backward", (chunks,))
     call.scalars(ids)
-    call.whole(upstream)
-    call.whole(third_pre)
-    call.whole(second_pre)
-    call.whole(second_low)
-    call.blocked(active, (rows, width), lambda i: (0, i))
+    for array in (third_grad, third_low, sums, second_pre, second_low):
+        call.whole(array)
     call.blocked(slope, (rows, width), lambda i: (0, i))
     call.whole(cross_mixed)
     feed_blocks(call, feed, width, chunks, owned_rows)
     call.weight(out_weight)
     call.whole(vecs)
-    inner_half = Halves(
-        call, chunks, owners, owned_rows, width, owners // 2, lambda i: (0, i)
-    )
-    outer_half = Halves(
-        call, 1, owners, chunks * owned_rows, width, owners // 2 // chunks, lambda i: (i, 0)
-    )
-    out_half = Halves(call, 1, owners, owned_rows, width)
     call.out((rows, width), jnp.float32)
     call.out((rows, width), jnp.bfloat16)
-    call.out((16, width), jnp.float32)
-    n_in, n_half, n_outer = len(call.ins), inner_half.outs, outer_half.outs
-    call.flops = 8 * rows * hidden * width + 4 * rows * width * width
-
-    def kernel(*refs):
-        (
-            ids_ref, up_ref, third_ref, second_ref, low_ref, active_ref, slope_ref, mixed_ref, inner_ref,
-            outer_ref, wo_ref, vecs_ref,
-        ) = refs[:n_in]
-        inner_grads = refs[n_in : n_in + n_half]
-        outer_grads = refs[n_in + n_half : n_in + n_half + n_outer]
-        out_grads = refs[n_in + n_half + n_outer : -5]
-        second_grad_ref, mix_ref, sums_ref, third_low_ref, total_ref = refs[-5:]
+    call.out((24, width), jnp.float32)
+    inner_half = Halves(call, chunks, owners, owned_rows, width, owners // 2, lambda i: (0, i))
+    out_half = Halves(call, 1, owners, owned_rows, width)
+    call.flops = 6 * rows * chunks * width * width + 4 * rows * width * width
+    outs = inner_half.outs
+
+    def kernel(
+        ids_ref, third_ref, third_low_ref, sums_in_ref, second_ref, low_ref, slope_ref, mixed_ref, inner_ref, outer_ref,
+        wo_ref, vecs_ref, second_grad_ref, mix_ref, sums_ref, *rest,
+    ):
+        inner_grads, out_grads, total_ref = rest[:outs], rest[outs:-1], rest[-1]
         step = pl.program_id(0)
         mine = ids_ref[5]
 
         @pl.when(step == 0)
         def _():
-            grad, gain_sum, shift_sum = norm_backward(
-                third_ref[...], row(vecs_ref, GAIN_THREE), widen(up_ref[...])
-            )
-            total_ref[...] = grad
-            third_low_ref[...] = low(grad)
-            sums_ref[0:1, :] = gain_sum
-            sums_ref[1:2, :] = shift_sum
-            sums_ref[2:3, :] = jnp.sum(widen(low(grad)), axis=0, keepdims=True)
-
-        third_low = third_low_ref[...]
-        inner_low = low(times_transpose(third_low, load(outer_ref)) * widen(slope_ref[...]))
+            total_ref[...] = third_ref[...]
+            sums_ref[...] = sums_in_ref[...]
+
+        inner_low = low(times_transpose(third_low_ref[...], load(outer_ref)) * widen(slope_ref[...]))
         total_ref[...] += times_transpose(inner_low, load(inner_ref))
-        outer_half.store(outer_grads, 0, contract_rows(active_ref[...], third_low), mine)
         inner_half.store(inner_grads, 0, contract_rows(low_ref[...], inner_low), mine)
-        sums_ref[pl.ds(8 + step, 1), :] = jnp.sum(widen(inner_low), axis=0, keepdims=True)
+        sums_ref[pl.ds(INNER_B + step, 1), :] = jnp.sum(widen(inner_low), axis=0, keepdims=True)
 
         @pl.when(step == chunks - 1)
         def _():
@@ -525,25 +540,22 @@
             )
             second_grad_ref[...] = grad
             cross_low = low(grad)
-            sums_ref[3:4, :] = gain_sum
-            sums_ref[4:5, :] = shift_sum
-            sums_ref[5:6, :] = jnp.sum(widen(cross_low), axis=0, keepdims=True)
+            sums_ref[GAIN_TWO : GAIN_TWO + 1, :] = gain_sum
+            sums_ref[SHIFT_TWO : SHIFT_TWO + 1, :] = shift_sum
+            sums_ref[CROSS_O : CROSS_O + 1, :] = jnp.sum(widen(cross_low), axis=0, keepdims=True)
             mix_ref[...] = low(times_transpose(cross_low, load(wo_ref)))
             out_half.store(out_grads, 0, contract_rows(mixed_ref[...], cross_low), mine)
 
-    results = call.run(
-        kernel, [pltpu.VMEM((rows, width), jnp.bfloat16), pltpu.VMEM((rows, width), jnp.float32)]
-    )
+    results = call.run(kernel, [pltpu.VMEM((rows, width), jnp.float32)])
     core = ids[5]
-    return (
-        inner_half.pair(results[:n_half], core),
-        outer_half.pair(results[n_half : n_half + n_outer], core),
-        out_half.pair(results[n_half + n_outer : -3], core),
-    ) + tuple(results[-3:])
+    return tuple(results[:3]) + (
+        inner_half.pair(results[3 : 3 + outs], core),
+        out_half.pair(results[3 + outs :], core),
+    )
 
 
 def cross_backward(
-    ids, queries, own, other, mixed, upstream, logsum, first_low, first_pre, second_grad, self_mixed,
+    ids, queries, own, other, mixed, upstream, logsum, first_low, first_pre, second_grad, self_mixed, sums,
     query_weight, out_weight, vecs, owned_rows,
 ):
     rows, width = queries.shape
@@ -557,7 +569,7 @@
     call.blocked(logsum, (1, 2, rows), lambda h: (h, 0, 0))
     for array in (own, other):
         call.blocked(array, (2, key_rows, lanes), lambda h: (0, 0, h))
-    for array in (first_low, first_pre, second_grad, self_mixed):
+    for array in (first_low, first_pre, second_grad, self_mixed, sums):
         call.whole(array)
     call.weight(query_weight)
     call.weight(out_weight)
@@ -566,18 +578,23 @@
         call.out((2, key_rows, width), jnp.bfloat16, (2, key_rows, lanes), lambda h: (0, 0, h))
     call.out((rows, width), jnp.float32)
     call.out((rows, width), jnp.bfloat16)
-    call.out((8, width), jnp.float32)
+    call.out((24, width), jnp.float32)
     half = Halves(call, 2, width // owned_rows, owned_rows, width)
     call.flops = 40 * rows * key_rows * width + 8 * rows * width * width
     call.exps = 2 * rows * key_rows * HEADS
 
     def kernel(
         ids_ref, q_ref, mixed_ref, up_ref, log_ref, own_ref, other_ref, low_ref, pre_ref, grad_ref,
-        self_mixed_ref, wq_ref, wo_ref, vecs_ref, own_out_ref, other_out_ref, first_ref, mix_ref,
+        self_mixed_ref, sums_in_ref, wq_ref, wo_ref, vecs_ref, own_out_ref, other_out_ref, first_ref, mix_ref,
         sums_ref, *rest,
     ):
         step = pl.program_id(0)
         weights_refs, dq_ref = rest[:-1], rest[-1]
+
+        @pl.when(step == 0)
+        def _():
+            sums_ref[...] = sums_in_ref[...]
+
         keys, values = (own_ref[0], other_ref[0]), (own_ref[1], other_ref[1])
         dq, dk, dv = attend_pair_backward(
             q_ref[...], keys, values, None, log_ref, mixed_ref[...], up_ref[...]
@@ -586,6 +603,7 @@
         for chunk, out in enumerate((own_out_ref, other_out_ref)):
             out[0] = low(dk[chunk])
             out[1] = low(dv[chunk])
+        sums_ref[CROSS_V : CROSS_V + 1, at(step)] = sum(jnp.sum(v, axis=0, keepdims=True) for v in dv)
 
         @pl.when(step == pairs - 1)
         def _():
@@ -597,47 +615,40 @@
             self_low = low(grad)
             mix_ref[...] = low(times_transpose(self_low, load(wo_ref)))
             half.store(weights_refs, 1, contract_rows(self_mixed_ref[...], self_low), ids_ref[5])
-            sums_ref[0:1, :] = gain_sum
-            sums_ref[1:2, :] = shift_sum
-            sums_ref[2:3, :] = jnp.sum(widen(self_low), axis=0, keepdims=True)
-            sums_ref[3:4, :] = jnp.sum(widen(query_low), axis=0, keepdims=True) * 0.125
+            sums_ref[GAIN_ONE : GAIN_ONE + 1, :] = gain_sum
+            sums_ref[SHIFT_ONE : SHIFT_ONE + 1, :] = shift_sum
+            sums_ref[SELF_O : SELF_O + 1, :] = jnp.sum(widen(self_low), axis=0, keepdims=True)
+            sums_ref[CROSS_Q : CROSS_Q + 1, :] = jnp.sum(widen(query_low), axis=0, keepdims=True) * 0.125
 
     results = call.run(kernel, [pltpu.VMEM((rows, width), jnp.bfloat16)])
     return tuple(results[:5]) + (half.pair(results[5:], ids[5]),)
 
 
-def self_backward(
-    ids, queries, own, other, mixed, upstream, logsum, tokens, first_grad, query_weight, owned_rows
-):
+def self_backward(ids, queries, own, other, mixed, upstream, logsum, first, last):
     rows, width = queries.shape
-    pairs = HEADS // 2
-    lanes, at = lanes_of(width)
-    call = Call("self_backward", (pairs,))
+    lanes, _ = lanes_of(width)
+    count = last - first
+    call = Call("self_backward", (count,))
     call.scalars(ids)
     for array in (queries, mixed, upstream):
-        call.blocked(array, (rows, lanes), lambda h: (0, h))
-    call.blocked(logsum, (1, 2, rows), lambda h: (h, 0, 0))
+        call.blocked(array, (rows, lanes), lambda h: (0, first + h))
+    call.blocked(logsum, (1, 2, rows), lambda h: (first + h, 0, 0))
     for array in (own, other):
-        call.blocked(array, (2, rows, lanes), lambda h: (0, 0, h))
-    for array in (tokens, first_grad):
-        call.whole(array)
-    call.weight(query_weight)
+        call.blocked(array, (2, rows, lanes), lambda h: (0, 0, first + h))
+    call.out((rows, count * lanes), jnp.bfloat16, (rows, lanes), lambda h: (0, h))
     for _ in range(2):
-        call.out((2, rows, width), jnp.bfloat16, (2, rows, lanes), lambda h: (0, 0, h))
-    call.out((rows, width), jnp.float32)
-    call.out((8, width), jnp.float32)
-    half = Halves(call, 1, width // owned_rows, owned_rows, width)
-    call.flops = 40 * rows * rows * width + 4 * rows * width * width
-    call.exps = 2 * rows * rows * HEADS
+        call.out(
+            (2, rows, count * lanes), jnp.bfloat16, (2, rows, lanes), lambda h: (0, 0, h)
+        )
+    call.out((8, count * lanes), jnp.float32, (8, lanes), lambda h: (0, h))
+    call.flops = 40 * rows * rows * count * lanes
+    call.exps = 4 * rows * rows * count
 
     def kernel(
-        ids_ref, q_ref, mixed_ref, up_ref, log_ref, own_ref, other_ref, x_ref, grad_ref, wq_ref,
-        own_out_ref, other_out_ref, part_ref, sums_ref, *rest,
+        ids_ref, q_ref, mixed_ref, up_ref, log_ref, own_ref, other_ref, dq_ref, own_out_ref,
+        other_out_ref, sums_ref, bias_ref,
     ):
-        weights_refs, (bias_ref, dq_ref) = rest[:-2], rest[-2:]
-        step = pl.program_id(0)
-
-        @pl.when(step == 0)
+        @pl.when(pl.program_id(0) == 0)
         def _():
             for chunk in range(2):
                 fill_bias(bias_ref, chunk, rows, ids_ref)
@@ -646,57 +657,118 @@
         dq, dk, dv = attend_pair_backward(
             q_ref[...], keys, values, bias_ref, log_ref, mixed_ref[...], up_ref[...]
         )
-        dq_ref[:, at(step)] = dq
+        dq_ref[...] = dq
         for chunk, out in enumerate((own_out_ref, other_out_ref)):
             out[0] = low(dk[chunk])
             out[1] = low(dv[chunk])
-
-        @pl.when(step == pairs - 1)
-        def _():
-            query_low = dq_ref[...]
-            half.store(weights_refs, 0, contract_rows(x_ref[...], query_low) * 0.125, ids_ref[5])
-            part_ref[...] = grad_ref[...] + times_transpose(query_low, load(wq_ref)) * 0.125
-            sums_ref[0:1, :] = jnp.sum(widen(query_low), axis=0, keepdims=True) * 0.125
-
-    results = call.run(
-        kernel,
-        [pltpu.VMEM((2, rows, rows), jnp.float32), pltpu.VMEM((rows, width), jnp.bfloat16)],
-    )
-    return tuple(results[:4]) + (half.pair(results[4:], ids[5]),)
-
-
-def key_backward(ids, tokens, mine, got, part, key_weight, value_weight, owned_rows):
+        sums_ref[0:1, :] = sum(jnp.sum(v, axis=0, keepdims=True) for v in dv)
+        sums_ref[1:2, :] = jnp.sum(widen(dq), axis=0, keepdims=True) * 0.125
+
+    return call.run(kernel, [pltpu.VMEM((2, rows, rows), jnp.float32)])
+
+
+def query_backward(ids, tokens, query_low, half_sums, sums, first_grad, query_weight, owned_rows):
+    rows, width = tokens.shape
+    call = Call("query_backward", (1,))
+    call.scalars(ids)
+    for array in (tokens, first_grad, sums) + tuple(query_low) + tuple(half_sums):
+        call.whole(array)
+    call.weight(query_weight)
+    call.out((rows, width), jnp.float32)
+    call.out((24, width), jnp.float32)
+    half = Halves(call, 1, width // owned_rows, owned_rows, width)
+    call.flops = 4 * rows * width * width
+
+    def kernel(
+        ids_ref, x_ref, grad_ref, sums_in_ref, first_ref, second_ref, first_sums_ref, second_sums_ref,
+        wq_ref, part_ref, sums_ref, *weights_refs,
+    ):
+        sums_ref[...] = sums_in_ref[...]
+        cut = first_ref.shape[1]
+        for lanes, ref in ((slice(0, cut), first_sums_ref), (slice(cut, width), second_sums_ref)):
+            sums_ref[SELF_V : SELF_V + 1, lanes] = ref[0:1, :]
+            sums_ref[SELF_Q : SELF_Q + 1, lanes] = ref[1:2, :]
+        query = jnp.concatenate([first_ref[...], second_ref[...]], axis=1)
+        half.store(weights_refs, 0, contract_rows(x_ref[...], query) * 0.125, ids_ref[5])
+        part_ref[...] = grad_ref[...] + times_transpose(query, load(wq_ref)) * 0.125
+
+    results = call.run(kernel)
+    return results[0], results[1], half.pair(results[2:], ids[5])
+
+
+def key_weights(ids, tokens, mine, got, owned_rows):
+    rows, width = tokens.shape
+    call = Call("key_weights", (1,))
+    call.scalars(ids)
+    for array in (tokens,) + tuple(mine) + tuple(got):
+        call.whole(array)
+    call.out((2, rows, width), jnp.bfloat16)
+    halves = [Halves(call, 1, width // owned_rows, owned_rows, width) for _ in range(2)]
+    outs = halves[0].outs
+    call.flops = 4 * rows * width * width
+
+    def kernel(ids_ref, x_ref, mine_a, mine_b, got_a, got_b, total_ref, *weights_refs):
+        values = x_ref[...]
+        for i in range(2):
+            total = low(
+                jnp.concatenate(
+                    [widen(m[i]) + widen(g[i]) for m, g in ((mine_a, got_a), (mine_b, got_b))], axis=1
+                )
+            )
+            total_ref[i] = total
+            refs = weights_refs[i * outs : (i + 1) * outs]
+            halves[i].store(refs, 0, contract_rows(values, total), ids_ref[5])
+
+    results = call.run(kernel)
+    return (results[0],) + tuple(
+        halves[i].pair(results[1 + i * outs : 1 + (i + 1) * outs], ids[5]) for i in range(2)
+    )
+
+
+def token_backward(total, part, key_weight, value_weight):
+    rows, width = part.shape
+    call = Call("token_backward", (1,))
+    call.whole(total)
+    call.whole(part)
+    call.weight(key_weight)
+    call.weight(value_weight)
+    call.out((rows, width), jnp.bfloat16)
+    call.flops = 4 * rows * width * width
+
+    def kernel(total_ref, part_ref, wk_ref, wv_ref, out_ref):
+        out_ref[...] = low(
+            part_ref[...]
+            + times_transpose(total_ref[0], load(wk_ref))
+            + times_transpose(total_ref[1], load(wv_ref))
+        )
+
+    return call.run(kernel)[0]
+
+
+def key_backward(ids, tokens, mine, got, key_weight, value_weight, owned_rows):
     rows, width = tokens.shape
     call = Call("key_backward", (1,))
     call.scalars(ids)
-    for array in (tokens, mine, got) + (() if part is None else (part,)):
+    for array in (tokens, mine, got):
         call.whole(array)
     call.weight(key_weight)
     call.weight(value_weight)
     call.out((rows, width), jnp.bfloat16)
-    call.out((8, width), jnp.float32)
     half = Halves(call, 2, width // owned_rows, owned_rows, width)
     call.flops = 8 * rows * width * width
 
-    def kernel(ids_ref, x_ref, mine_ref, got_ref, *refs):
-        if part is not None:
-            total, refs = refs[0][...], refs[1:]
-        else:
-            total = 0.0
-        wk_ref, wv_ref, out_ref, sums_ref = refs[:4]
-        weights_refs = refs[4:]
+    def kernel(ids_ref, x_ref, mine_ref, got_ref, wk_ref, wv_ref, out_ref, *weights_refs):
         values = x_ref[...]
         dk = low(widen(mine_ref[0]) + widen(got_ref[0]))
         dv = low(widen(mine_ref[1]) + widen(got_ref[1]))
         half.store(weights_refs, 0, contract_rows(values, dk), ids_ref[5])
         half.store(weights_refs, 1, contract_rows(values, dv), ids_ref[5])
         out_ref[...] = low(
-            total + times_transpose(dk, load(wk_ref)) + times_transpose(dv, load(wv_ref))
+            times_transpose(dk, load(wk_ref)) + times_transpose(dv, load(wv_ref))
         )
-        sums_ref[0:1, :] = jnp.sum(widen(dv), axis=0, keepdims=True)
 
     results = call.run(kernel)
-    return tuple(results[:2]) + (half.pair(results[2:], ids[5]),)
+    return results[0], half.pair(results[1:], ids[5])
 
 
 def flip(size, bit):
@@ -728,62 +800,18 @@
 
     def send(self, values, step):
         name, bit = step
-        return lax.ppermute(values, name, flip(self.sizes[name], 1 << bit))
+        flat = values.reshape(-1, values.shape[-1])
+        return lax.ppermute(flat, name, flip(self.sizes[name], 1 << bit)).reshape(values.shape)
 
 
 def split_sum(keep, got, at, mine):
-    total = low(widen(keep) + widen(got))
-    return [
-        lax.dynamic_index_in_dim(total, which, at, keepdims=False) for which in (mine, 1 - mine)
-    ]
-
-
-def merge(keep, got, at, mine):
-    shape = keep.shape
-    before, after = 1, shape[-2]
-    for n in shape[:at]:
-        before *= n
-    for n in shape[at + 1 : -2]:
-        after *= n
-    width = shape[-1]
-    left = tuple(shape[:at] + shape[at + 1 :])
-    if shape[-2] % 8:
-        return split_sum(keep, got, at, mine)
-    view = (before, 2, after, width)
-    rows, heads = after, 1
-    while rows > 256 and rows % 16 == 0:
-        rows //= 2
-    while heads * rows < 128 and before % (2 * heads) == 0:
-        heads *= 2
-    block = (heads, None, rows, width)
-
-    def stay(i, j, mine_ref):
-        return (i, mine_ref[0], j, 0)
-
-    def go(i, j, mine_ref):
-        return (i, 1 - mine_ref[0], j, 0)
-
-    def kernel(mine_ref, keep_a, keep_b, got_a, got_b, stay_ref, go_ref):
-        stay_ref[...] = low(widen(keep_a[...]) + widen(got_a[...]))
-        go_ref[...] = low(widen(keep_b[...]) + widen(got_b[...]))
-
-    size = before * after * width
-    out = pl.BlockSpec((heads, rows, width), lambda i, j, mine_ref: (i, j, 0))
-    keep, got = keep.reshape(view), got.reshape(view)
-    results = pl.pallas_call(
-        kernel,
-        grid_spec=pltpu.PrefetchScalarGridSpec(
-            num_scalar_prefetch=1,
-            grid=(before // heads, after // rows),
-            in_specs=[pl.BlockSpec(block, m) for m in (stay, go, stay, go)],
-            out_specs=[out, out],
-        ),
-        out_shape=[jax.ShapeDtypeStruct((before, after, width), jnp.bfloat16)] * 2,
-        compiler_params=pltpu.CompilerParams(vmem_limit_bytes=VMEM_LIMIT),
-        cost_estimate=pl.CostEstimate(flops=2 * size, bytes_accessed=12 * size, transcendentals=0),
-        name="merge",
-    )(mine.reshape(1).astype(jnp.int32), keep, keep, got, got)
-    return [r.reshape(left) for r in results]
+    def side(which):
+        first, second = [
+            lax.dynamic_index_in_dim(v, which, at, keepdims=False) for v in (keep, got)
+        ]
+        return low(widen(first) + widen(second))
+
+    return side(mine), side(1 - mine)
 
 
 class Scatter:
@@ -810,11 +838,32 @@
         if self.order:
             step = self.order[0]
             at = self.dims.index(step)
-            split = merge if self.keep.size > 2**18 else split_sum
-            self.keep, self.away = split(self.keep, got, at, self.moves.mine(step))
+            self.keep, self.away = split_sum(self.keep, got, at, self.moves.mine(step))
             self.dims.pop(at)
         else:
             self.held = widen(self.keep) + widen(got)
+
+    def spread(self):
+        steps, self.order = self.order, []
+        name = steps[0][0]
+        assert self.dims == sorted(steps, reverse=True) and self.got is not None
+        self.keep = self.total()
+        count = 1 << len(steps)
+        first = steps[0][1]
+        assert [bit for _, bit in steps] == list(range(first, first + len(steps)))
+        held = self.keep.reshape((count,) + self.keep.shape[-2:])
+        spot = (self.moves.spots[name] >> first) & (count - 1)
+        self.keep = lax.dynamic_index_in_dim(held, spot, 0, keepdims=False)
+        self.spreads = [
+            (i, lax.dynamic_index_in_dim(held, spot ^ i, 0, keepdims=False)) for i in range(1, count)
+        ]
+        size = self.moves.sizes[name]
+        self.gots = [lax.ppermute(v, name, flip(size, i << first)) for i, v in self.spreads]
+
+    def collect(self):
+        self.held = widen(self.keep)
+        for got in self.gots:
+            self.held = self.held + widen(got)
 
     def total(self):
         return low(widen(self.keep) + widen(self.got))
@@ -957,22 +1006,24 @@
     line, near = dp_bits[:-1], dp_bits[-1]
     cut = 2 * owned_rows
     first_part = jnp.concatenate([self_query, self_key, self_value, tail], axis=0)
+    first_part, inner_mat, outer_mat, self_out, prompt_in, cont_in = tie(
+        first_part, inner_mat, outer_mat, self_out, prompt_in, cont_in
+    )
+    one = Gather(moves, first_part, line)
+    one.ship()
+    prompt_got = swap_seq(pick(prompt_in, 1 - group), 3)
+    sent = jnp.concatenate([pick(v, 1 - group) for v in (cont_in, enc_out)], axis=0)
     feed = jnp.concatenate(
         [outer_mat]
         + [inner_mat[:, i * width : (i + 1) * width] for i in range(chunks)]
-        + [self_out, cross_query, cross_key, cross_value, cross_out],
+        + [cross_key, cross_value, cross_out],
         axis=0,
     )
-    one = Gather(moves, first_part, line)
-    one.ship()
-    first_part, feed, sent = tie(
-        first_part,
-        feed,
-        jnp.concatenate([pick(v, 1 - group) for v in (prompt_in, cont_in, enc_out)], axis=0),
-    )
+    second_part = jnp.concatenate([self_out, cross_query], axis=0)
     feed = lax.all_gather(feed, ("dp", "seq"), axis=0, tiled=False)
+    prompt_got, sent, second_part = pump([one], [one], prompt_got, sent, second_part)
+    two = Gather(moves, second_part, line)
     got = swap_seq(sent, 3)
-    pump([one], [one])
     while len(one.order) > 1:
         pump([one], [one])
     got = pump([one], [], got)
@@ -980,15 +1031,21 @@
         one.part(0, cut, [near, hi, lo]),
         one.part(cut, first_part.shape[0], [hi, near, lo]),
     ]
-    got = pump([], one_parts, got)
-    got = pump(one_parts, one_parts, got)
-    got = pump(one_parts, one_parts, got)
-    got = pump(one_parts, [], got)
+    got = pump([], one_parts + [two], got)
+    got = pump(one_parts + [two], one_parts + [two], got)
+    while len(two.order) > 1:
+        got = pump([two], [two], got)
+    got = pump(one_parts + [two], one_parts, got)
+    two_parts = [
+        two.part(0, owned_rows, [near, hi, lo]),
+        two.part(owned_rows, second_part.shape[0], [hi, near, lo]),
+    ]
+    got = pump(one_parts, two_parts, got)
 
     tokens = jnp.concatenate(
-        [pick(prompt_in, group), got[:rows], pick(cont_in, group), got[rows : 2 * rows]], axis=0
-    )
-    encoder = jnp.concatenate([pick(enc_out, group), got[2 * rows :]], axis=0)
+        [pick(prompt_in, group), prompt_got, pick(cont_in, group), got[:rows]], axis=0
+    )
+    encoder = jnp.concatenate([pick(enc_out, group), got[rows:]], axis=0)
 
     def square(array, index):
         if owned_rows % 8 == 0:
@@ -1000,25 +1057,28 @@
     self_query, self_key, self_value = square(front, 0), square(front, 1), square(back, 0)
     tail = back[:, owned_rows:]
     owners = parts * blocks
+    counts = 13 * owned_rows
     slots = tail.reshape(owners, 8, -1, 128)[:, :, :2, :owned_rows]
     vecs = slots.transpose(2, 1, 0, 3).reshape(16, width)[:13]
     biases = tail[:, 5, 128 : 128 + hidden_rows].reshape(chunks, width)
     vecs = widen(jnp.concatenate([vecs, biases], axis=0))
 
     queries, own = project(tokens, [self_query, self_key, self_value], vecs)
+    own = pump(two_parts, two_parts, own)
     other = swap_seq(own, 1)
+    mixed, logsum = self_attend(ids, queries, own, other)
+    mixed = pump(two_parts, two_parts, mixed)
+    mixed = pump(two_parts, [], mixed)
+    front, back = [g.result() for g in two_parts]
+    self_out, cross_query = square(front, 0), square(back, 0)
     cot_sent = jnp.concatenate([pick(v, 1 - group) for v in (prompt_cot, cont_cot)], axis=0)
-    cot_sent, other = tie(cot_sent, other)
+    cot_sent, mixed = tie(cot_sent, mixed)
     cot_got = swap_seq(cot_sent, 3)
-    mixed, logsum = self_attend(ids, queries, own, other)
-    mixed, cot_got = tie(mixed, cot_got)
-    base = 2 * chunks
-    self_out, cross_query, cross_key, cross_value, cross_out = [
-        square(feed, base + i) for i in range(5)
-    ]
+    first_pre, first_low, cross_queries = self_finish(tokens, mixed, self_out, cross_query, vecs)
+    cross_queries, cot_got, feed = tie(cross_queries, cot_got, feed)
+    cross_key, cross_value, cross_out = [square(feed, 2 * chunks + i) for i in range(3)]
     (cross_own,) = project(encoder, [cross_key, cross_value], vecs)
     cross_other = swap_seq(cross_own, 1)
-    first_pre, first_low, cross_queries = self_finish(tokens, mixed, self_out, cross_query, vecs)
     cross_mixed, cross_logsum, second_pre, second_low = cross_attend(
         cross_queries, cross_own, cross_other, first_pre, cross_out, vecs
     )
@@ -1046,35 +1106,45 @@
     bits = dp_bits[::-1]
     x_first = [lo, hi] + bits
     y_first = [lo, bits[0], hi] + bits[1:]
-    inner_pair, outer_pair, cross_out_pair, second_grad, cross_mix, feed_sums = feed_backward(
-        ids, upstream, third_pre, second_pre, second_low, active, slope, cross_mixed, feed, cross_out,
-        vecs, chunks, owned_rows,
-    )
-    cross_mix, result_back = tie(cross_mix, result_back)
+    third_grad, third_low, sums, outer_pair = outer_backward(
+        ids, upstream, third_pre, active, vecs, chunks, owned_rows
+    )
+    third_low, result_back = tie(third_low, result_back)
     prompt_out, cont_out = place(result, result_back)
     outer_chain = Scatter(moves, [outer_pair], x_first)
+    third_low = depart([outer_chain], third_low)
+    second_grad, cross_mix, sums, inner_pair, cross_out_pair = inner_backward(
+        ids, third_grad, third_low, sums, second_pre, second_low, slope, cross_mixed, feed, cross_out,
+        vecs, chunks, owned_rows,
+    )
     inner_chain = Scatter(moves, [inner_pair], y_first)
     feed_chains = [outer_chain, inner_chain]
-    cross_mix = depart(feed_chains, cross_mix)
-    cross_mix = advance(feed_chains, cross_mix)
-    own_back, other_back, first_grad, mix, cross_sums, query_pair = cross_backward(
+    cross_mix = receive([outer_chain], cross_mix)
+    cross_mix = depart([inner_chain], cross_mix)
+    cross_mix = depart([outer_chain], cross_mix)
+    cross_mix = advance([inner_chain], cross_mix)
+    own_back, other_back, first_grad, mix, sums, query_pair = cross_backward(
         ids, cross_queries, cross_own, cross_other, cross_mixed, cross_mix, cross_logsum, first_low,
-        first_pre, second_grad, mixed, cross_query, self_out, vecs, owned_rows,
+        first_pre, second_grad, mixed, sums, cross_query, self_out, vecs, owned_rows,
     )
     mix, other_back = receive(feed_chains, mix, other_back)
     got_back = swap_seq(other_back, 1)
-    got_back = depart(feed_chains, got_back)
-    enc_back, key_sums, key_pair = key_backward(
-        ids, encoder, own_back, got_back, None, cross_key, cross_value, owned_rows
+    enc_back, key_pair = key_backward(
+        ids, encoder, own_back, got_back, cross_key, cross_value, owned_rows
     )
     cross_chains = [
         Scatter(moves, [query_pair, cross_out_pair], x_first),
         Scatter(moves, [key_pair], y_first),
     ]
-    outer_chain.got, inner_chain.got, enc_back, mix = tie(
-        outer_chain.got, inner_chain.got, enc_back, mix
-    )
-    mix = depart(cross_chains, mix)
+    enc_rows = enc_out.shape[1]
+    mix = depart(cross_chains + feed_chains, mix)
+    enc_sent, mix = tie(enc_back[enc_rows:], mix)
+    enc_got = swap_seq(enc_sent, 3)
+    halfway = HEADS // 4
+    one = self_backward(ids, queries, own, other, mixed, mix, logsum, 0, halfway)
+    tied = receive(cross_chains, enc_got, outer_chain.got, inner_chain.got, mix, *one)
+    enc_got, outer_chain.got, inner_chain.got, mix = tied[:4]
+    one = tied[4:]
     rest = jnp.concatenate([c.total() for c in feed_chains], axis=-2)
     rest, mix = tie(rest, mix)
     rest = rest.reshape((-1,) + rest.shape[-2:])
@@ -1082,67 +1152,66 @@
     rest = lax.psum_scatter(
         rest, "dp", scatter_dimension=0, axis_index_groups=lines, tiled=True
     )[0]
-    mix = advance(cross_chains, mix)
-    self_own, self_other, part, self_sums, self_query_pair = self_backward(
-        ids, queries, own, other, mixed, mix, logsum, tokens, first_grad, self_query, owned_rows
-    )
-    self_other = receive(cross_chains, self_other)
-    self_got = swap_seq(self_other, 1)
-    self_got = depart(cross_chains, self_got)
-    token_grad, self_key_sums, self_key_pair = key_backward(
-        ids, tokens, self_own, self_got, part, self_key, self_value, owned_rows
-    )
-    token_grad = receive(cross_chains, token_grad)
-    sums = jnp.concatenate(
-        [
-            self_sums[0:1],
-            self_key_sums[0:1],
-            cross_sums[2:3],
-            cross_sums[0:2],
-            cross_sums[3:4],
-            key_sums[0:1],
-            feed_sums[5:6],
-            feed_sums[3:5],
-            feed_sums[2:3],
-            feed_sums[0:2],
-        ],
-        axis=0,
-    )
-    slots = jnp.pad(sums.reshape(13, owners, owned_rows), ((0, 3), (0, 0), (0, 128 - owned_rows)))
-    slots = slots.reshape(2, 8, owners, 128).transpose(2, 1, 0, 3)
-    bias_sums = feed_sums[8 : 8 + chunks].reshape(owners, hidden_rows)
-    slots = slots.at[:, 5, 1, :hidden_rows].set(bias_sums)
-    sums = jnp.pad(low(slots).reshape(owners, 8, 256), ((0, 0), (0, 0), (0, width - 256)))
+    mix = depart(cross_chains, mix)
+    two = self_backward(ids, queries, own, other, mixed, mix, logsum, halfway, HEADS // 2)
+    two = receive(cross_chains, *two)
+    sent = [tie(h[2], *[c.away for c in cross_chains])[0] for h in (one, two)]
+    got_one, got_two = [swap_seq(v, 1) for v in sent]
+    part, sums, self_query_pair = query_backward(
+        ids, tokens, (one[0], two[0]), (one[3], two[3]), sums, first_grad, self_query, owned_rows
+    )
+    got_one, got_two, part = tie(got_one, got_two, part)
+    bias_sums = sums[INNER_B : INNER_B + chunks].reshape(owners, hidden_rows)
+    sums = sums[:13].reshape(13, owners, owned_rows).transpose(1, 0, 2).reshape(owners, counts)
+    sums = low(jnp.concatenate([sums, bias_sums], axis=1))
+    sums = jnp.pad(sums[:, None, :], ((0, 0), (0, 7), (0, width - counts - hidden_rows)))
     sums = sums.reshape(-1, 2, 8, width)
     sums_pair = (
         lax.dynamic_index_in_dim(sums, seq & 1, 1, keepdims=False),
         lax.dynamic_index_in_dim(sums, 1 - (seq & 1), 1, keepdims=False),
     )
-    even_chain = Scatter(moves, [self_key_pair], x_first)
-    odd_chain = Scatter(moves, [self_query_pair, sums_pair], y_first)
-    last = [even_chain, odd_chain]
-    token_grad, token_back = send_back(token_grad)
-    depart(last)
-    advance(last)
-    advance(last)
-    receive(last)
-    tail_chain = joined(last + cross_chains)
+    query_chain = Scatter(moves, [self_query_pair, sums_pair], y_first)
+    got_one = depart(cross_chains + [query_chain], got_one)
+    total, key_pair, value_pair = key_weights(
+        ids, tokens, (one[1], two[1]), (got_one, got_two), owned_rows
+    )
+    key_chains = [Scatter(moves, [key_pair], x_first), Scatter(moves, [value_pair], y_first)]
+    total = receive(cross_chains + [query_chain], total)
+    cross_last = joined(cross_chains)
+    total = depart(key_chains + [query_chain, cross_last], total)
+    token_grad = token_backward(total, part, self_key, self_value)
+    token_grad = receive(key_chains + [query_chain, cross_last], token_grad)
+    depart(key_chains + [query_chain, cross_last])
+    receive(key_chains + [query_chain])
+    depart(key_chains)
+    last_away = query_chain.away
+    receive(key_chains)
+    tail_chain = joined(key_chains)
+    tail_chain.order = list(tail_chain.order)
+    query_chain.away = last_away
+    tail_chain.keep = jnp.concatenate([tail_chain.keep, query_chain.keep], axis=-2)
+    tail_chain.away = jnp.concatenate([tail_chain.away, query_chain.away], axis=-2)
+    token_grad, token_back, tail_chain.away = send_back(token_grad, tail_chain.away)
     tail_chain.ship()
-    while tail_chain.got is not None:
+    token_back = receive([tail_chain], token_back)
+    while tail_chain.order:
+        tail_chain.ship()
         receive([tail_chain])
-        if tail_chain.order and tail_chain.away is not None:
-            tail_chain.ship()
-    ends, at = [], 0
-    for size, extra in ((2, 0), (1, 8), (3, 0), (2, 0)):
-        ends.append((at, at + size * owned_rows))
-        at += size * owned_rows + extra
-    self_key_grads, self_query_grad, cross_grads, cross_key_grads = [
-        tail_chain.held[a:b].reshape(-1, owned_rows, width) for a, b in ends
-    ]
-    vec = tail_chain.held[ends[1][1] : ends[1][1] + 8].reshape(8, -1, 128)
+    while cross_last.got is not None:
+        receive([cross_last])
+        if cross_last.order:
+            cross_last.ship()
+
+    def cut_rows(held, sizes):
+        ends = [sum(sizes[: i + 1]) for i in range(len(sizes))]
+        return [held[e - n : e] for e, n in zip(ends, sizes)]
+
+    self_key_grad, self_value_grad, self_query_grad, vec = cut_rows(
+        tail_chain.held, [owned_rows, owned_rows, owned_rows, 8]
+    )
+    cross_held = cross_last.held.reshape(-1, owned_rows, width)
+    vec = vec[0]
     prompt_grad, cont_grad = place(token_grad, token_back)
-    enc_rows = enc_out.shape[1]
-    enc_got = swap_seq(enc_back[enc_rows:], 3)
     enc_grad = jnp.where(
         group == 0,
         jnp.stack([enc_back[:enc_rows], enc_got]),
@@ -1155,29 +1224,29 @@
         [rest[hidden_rows + i * owned_rows : hidden_rows + (i + 1) * owned_rows] for i in range(chunks)],
         axis=1,
     )
-    vec_out = [vec[i % 8, i // 8, :owned_rows] for i in range(13)]
-    inner_bias_out = vec[5, 1, :hidden_rows]
+    vec_out = [vec[i * owned_rows : (i + 1) * owned_rows] for i in range(13)]
+    inner_bias_out = vec[counts : counts + hidden_rows]
     return (
         prompt_out,
         cont_out,
         prompt_grad,
         cont_grad,
         enc_grad,
-        self_query_grad[0],
+        self_query_grad,
         vec_out[0],
-        self_key_grads[0],
-        self_key_grads[1],
+        self_key_grad,
+        self_value_grad,
         vec_out[1],
-        cross_grads[1],
+        cross_held[1],
         vec_out[2],
         vec_out[3],
         vec_out[4],
-        cross_grads[0],
+        cross_held[0],
         vec_out[5],
-        cross_key_grads[0],
-        cross_key_grads[1],
+        cross_held[3],
+        cross_held[4],
         vec_out[6],
-        cross_grads[2],
+        cross_held[2],
         vec_out[7],
         vec_out[8],
         vec_out[9],

time: 438 us -> 391 us (0.89)
  waiting for transfers between devices: 158 us -> 107 us
  other arithmetic: 23.4 us -> 47.6 us
  Pallas kernels: 164 us -> 141 us
  starting transfers between devices: 34.6 us -> 45.3 us
  local copies, waits for them, and re-layouts: 36.2 us -> 28.4 us
    pallas_call x12 -> x0, Pallas kernels: 34.9 us -> none  [merge(): pl.pallas_call(kernel, grid_spec=pltpu.PrefetchScalarGridSpec(num_scalar_...]
    all_gather x1, waiting for transfers between devices: 37 us -> 6.97 us  [body(): feed = lax.all_gather(feed, ('dp', 'seq'), axis=0, tiled=False)]
    convert_element_type x7 -> x30, other arithmetic: 1.71 us -> 26.6 us  [low(): return values.astype(jnp.bfloat16)]
    ppermute x28 -> x41, waiting for transfers between devices: 113 us -> 89.1 us  [send(): lax.ppermute(flat, name, flip(self.sizes[name], 1 << bit))]
    pallas_call x11 -> x15, Pallas kernels: 128 us -> 139 us  [run(): pl.pallas_call(kernel, grid=self.grid, in_specs=self.in_specs, out_specs=...]
    ppermute x28 -> x41, starting transfers between devices: 29.4 us -> 40.2 us  [send(): lax.ppermute(flat, name, flip(self.sizes[name], 1 << bit))]
    ppermute x9 -> x11, waiting for transfers between devices: 4.62 us -> 10.9 us  [swap_seq(): return lax.ppermute(values, 'seq', flip(lax.axis_size('seq'), bits))]
    unnamed x140 -> x89, local copies, waits for them, and re-layouts: 15.8 us -> 12.1 us
  transfers between devices with their start and end apart: 39 -> 54, of which waited for: 25 -> 28; matrix products, arithmetic and copies ran while one was open for 8% -> 12% of each run, Pallas kernels for 27% -> 28%
where the time goes in v2:
time: 391 us; the launch traced here: 384 us
  Pallas kernels  141 us (36%)
  waiting for transfers between devices  107 us (27%)
  other arithmetic  47.6 us (12%)
  starting transfers between devices  45.3 us (12%)
  local copies, waits for them, and re-layouts  28.4 us (7%)
  between operations  15.3 us (4%)
    pallas_call x15, Pallas kernels, run(): pl.pallas_call(kernel, grid=self.grid, in_specs=self.in_specs, out_specs=...  139 us
    ppermute x41, waiting for transfers between devices, send(): lax.ppermute(flat, name, flip(self.sizes[name], 1 << bit))  89.1 us
    ppermute x41, starting transfers between devices, send(): lax.ppermute(flat, name, flip(self.sizes[name], 1 << bit))  40.2 us
    convert_element_type x30, other arithmetic, low(): return values.astype(jnp.bfloat16)  26.6 us
    unnamed x89, local copies, waits for them, and re-layouts  12.1 us
    ppermute x11, waiting for transfers between devices, swap_seq(): return lax.ppermute(values, 'seq', flip(lax.axis_size('seq'), bits))  10.9 us
  transfers between devices with their start and end apart: 54, of which 28 were waited for; matrix products, arithmetic and copies ran while one was open for 12% of the time, Pallas kernels for 28%

profile of v2, /device:TPU:0, one launch (start us, length us, event | category | flops | bytes accessed | tf_op | source)
XLA Modules:
  0.0 384.3 jit_solution(12530032829664594900)
XLA Ops:
  16.8 4.1 %collective-permute-start = (bf16[80,768]{1,0:T(8,128)(2,1)S(1)}, bf16[80,768]{1,0:T(8,128)(2,1)S(1)}, u32[]{:S(2)}, u32[]{:S(2)}) collective-permute-start(bf16[80,768]{1,0:T(8,128)(2,1)S(1)} %pad_maximum_fusion.26), channel_id=1, source_target_pairs={{0,16},{4,20},{8,24},{12,28},{16,0},{20,4},{24,8},{28,12},{1,17},{... | collective-permute-start | bytes 368648 | tf_op jit(solution)/shard_map/ppermute | solution.py:804
  23.1 3.8 collective-permute-done
  26.9 1.9 collective-permute-done.1
  31.2 11.8 %collective-permute-done.2 = bf16[160,768]{1,0:T(8,128)(2,1)S(1)} collective-permute-done((bf16[160,768]{1,0:T(8,128)(2,1)S(1)}, bf16[160,768]{1,0:T(8,128)(2,1)S(1)}, u32[]{:S(2)}, u32[]{:S(2)}) %collective-permute-start.2) | collective-permute-done | bytes 245792 | tf_op jit(solution)/shard_map/ppermute | solution.py:804
  47.7 5.0 %collective-permute-done.6 = bf16[48,768]{1,0:T(8,128)(2,1)S(1)} collective-permute-done((bf16[48,768]{1,0:T(8,128)(2,1)S(1)}, bf16[48,768]{1,0:T(8,128)(2,1)S(1)}, u32[]{:S(2)}, u32[]{:S(2)}) %collective-permute-start.6) | collective-permute-done | bytes 73760 | tf_op jit(solution)/shard_map/ppermute | solution.py:804
  56.6 8.6 %collective-permute-done.9 = bf16[96,768]{1,0:T(8,128)(2,1)S(1)} collective-permute-done((bf16[96,768]{1,0:T(8,128)(2,1)S(1)}, bf16[96,768]{1,0:T(8,128)(2,1)S(1)}, u32[]{:S(2)}, u32[]{:S(2)}) %collective-permute-start.9) | collective-permute-done | bytes 147488 | tf_op jit(solution)/shard_map/ppermute | solution.py:804
  65.2 2.3 collective-permute-done.8
  67.6 10.0 %collective-permute-done.7 = bf16[384,768]{1,0:T(8,128)(2,1)S(1)} collective-permute-done((bf16[384,768]{1,0:T(8,128)(2,1)S(1)}, bf16[384,768]{1,0:T(8,128)(2,1)S(1)}, u32[]{:S(2)}, u32[]{:S(2)}) %collective-permute-start.7) | collective-permute-done | bytes 589856 | tf_op jit(solution)/shard_map/ppermute | solution.py:804
  80.3 1.9 collective-permute-done.11
  84.6 1.7 copy.211
  90.7 5.4 %project.2 = (bf16[512,768]{1,0:T(8,128)(2,1)}, bf16[2,512,768]{2,1,0:T(8,128)(2,1)}) custom-call(bf16[512,768]{1,0:T(8,128)(2,1)} %pad_maximum_fusion.4.refs_0_.x_ref, bf16[32,48,768]{2,1,0:T(8,128)(2,1)} %bitcast.431, bf16[32,48,768]{2,1,0:T(8,128)(2,1)} %bitcast.432, bf16[32,32,768]{2,1,0:T(8,128)(2,1)} %bitcast.437, ...), custom_call_target="tpu_custom_call" | custom-call | flops 1811939328 | bytes 6736896 | tf_op jit(solution)/shard_map/project/pallas_call | solution.py:130
  99.7 1.7 collective-permute-start.14
  102.5 14.8 %self_attend.1 = (bf16[512,768]{1,0:T(8,128)(2,1)}, f32[6,2,512]{2,1,0:T(2,128)}) custom-call(s32[6]{0:T(128)} %stack.273.ids_ref, bf16[512,768]{1,0:T(8,128)(2,1)} %get-tuple-element.275.q_ref, bf16[2,512,768]{2,1,0:T(8,128)(2,1)} %get-tuple-element.276.own_ref, bf16[2,512,768]{2,1,0:T(8,128)(2,1)} %collective-permute-done.16.other_ref), custom_call_target="tpu_custom_call" | custom-call | flops 3221225472 | bytes 4743168 | tf_op jit(solution)/shard_map/self_attend/pallas_call | solution.py:130
  123.4 5.1 %self_finish.1 = (f32[512,768]{1,0:T(8,128)}, bf16[512,768]{1,0:T(8,128)(2,1)}, bf16[512,768]{1,0:T(8,128)(2,1)}) custom-call(bf16[512,768]{1,0:T(8,128)(2,1)} %pad_maximum_fusion.4.refs_0_.x_ref, bf16[512,768]{1,0:T(8,128)(2,1)} %get-tuple-element.285.mixed_ref.self_mixed_ref, bf16[32,24,768]{2,1,0:T(8,128)(2,1)} %bitcast.453, ...), custom_call_target="tpu_custom_call" | custom-call | flops 1207959552 | bytes 7130112 | tf_op jit(solution)/shard_map/self_finish/pallas_call | solution.py:130
  128.5 3.1 collective-permute-done.19
  131.6 7.0 %all-gather.3.cloned.1.call-done = bf16[8448,768]{1,0:T(8,128)(2,1)} async-done(((bf16[264,768]{1,0:T(8,128)(2,1)}), bf16[8448,768]{1,0:T(8,128)(2,1)}) %all-gather.3.cloned.1.call-update) | async-done | bytes 12976144 | tf_op jit(solution)/shard_map/all_gather | solution.py:1023
  138.5 3.0 project.3.own_ref
  141.8 1.7 collective-permute-done.20.other_ref
  144.2 11.0 %cross_attend.1 = (bf16[512,768]{1,0:T(8,128)(2,1)}, f32[6,2,512]{2,1,0:T(2,128)}, f32[512,768]{1,0:T(8,128)}, bf16[512,768]{1,0:T(8,128)(2,1)}) custom-call(bf16[512,768]{1,0:T(8,128)(2,1)} %get-tuple-element.292.q_ref, bf16[2,128,768]{2,1,0:T(8,128)(2,1)} %project.3.own_ref, bf16[2,128,768]{2,1,0:T(8,128)(2,1)} %copy-done.27, ...), custom_call_target="tpu_custom_call" | custom-call | flops 1409286144 | bytes 7547904 | tf_op jit(solution)/shard_map/cross_attend/pallas_call | solution.py:130
  155.2 13.1 %feed_forward.1 = (bf16[512,3072]{1,0:T(8,128)(2,1)}, bf16[512,3072]{1,0:T(8,128)(2,1)}, f32[512,768]{1,0:T(8,128)}, bf16[512,768]{1,0:T(8,128)(2,1)}) custom-call(f32[512,768]{1,0:T(8,128)} %get-tuple-element.295.pre_ref.second_ref, bf16[512,768]{1,0:T(8,128)(2,1)} %get-tuple-element.296.low_ref, bf16[32,264,768]{2,1,0:T(8,128)(2,1)} %bitcast.424, ...), custom_call_target="tpu_custom_call" | custom-call | flops 4831838208 | bytes 37014528 | tf_op jit(solution)/shard_map/feed_forward/pallas_call | solution.py:130
  168.3 2.0 slice_bitcast_fusion.7
  172.7 8.8 %outer_backward.1 = (f32[512,768]{1,0:T(8,128)}, bf16[512,768]{1,0:T(8,128)(2,1)}, f32[24,768]{1,0:T(8,128)}, bf16[16,1,96,768]{3,2,1,0:T(8,128)(2,1)}, bf16[16,1,96,768]{3,2,1,0:T(8,128)(2,1)}) custom-call(s32[6]{0:T(128)} %stack.273.ids_ref, bf16[512,768]{1,0:T(8,128)(2,1)} %pad_maximum_fusion.5.up_ref, f32[512,768]{1,0:T(8,128)} %get-tuple-element.300.third_ref, ...), custom_call_target="tpu_custom_call" | custom-call | flops 2415919104 | bytes 12708864 | tf_op jit(solution)/shard_map/outer_backward/pallas_call | solution.py:130
  181.8 17.7 %inner_backward.1 = (f32[512,768]{1,0:T(8,128)}, bf16[512,768]{1,0:T(8,128)(2,1)}, f32[24,768]{1,0:T(8,128)}, bf16[16,4,24,768]{3,2,1,0:T(8,128)(2,1)}, bf16[16,...) custom-call(s32[6]{0:T(128)} %stack.273.ids_ref, ...), custom_call_target="tpu_custom_call" | custom-call | flops 8455716864 | bytes 44239872 | tf_op jit(solution)/shard_map/inner_backward/pallas_call | solution.py:130
  199.8 3.5 add_convert_fusion.1
  204.6 2.6 fusion.1
  208.3 17.8 %cross_backward.1 = (bf16[2,128,768]{2,1,0:T(8,128)(2,1)}, bf16[2,128,768]{2,1,0:T(8,128)(2,1)}, f32[512,768]{1,0:T(8,128)}, bf16[512,768]{1,0:T(8,128)(2,1)}, f...) custom-call(s32[6]{0:T(128)} %stack.273.ids_ref, ...), custom_call_target="tpu_custom_call" | custom-call | flops 4429185024 | bytes 15952896 | tf_op jit(solution)/shard_map/cross_backward/pallas_call | solution.py:130
  226.1 2.9 pad_maximum_fusion
  229.0 1.6 add_convert_fusion
  231.6 3.8 collective-permute-done.25
  236.4 2.0 fusion.15
  239.2 4.5 %key_backward.1 = (bf16[128,768]{1,0:T(8,128)(2,1)}, bf16[16,2,24,768]{3,2,1,0:T(8,128)(2,1)}, bf16[16,2,24,768]{3,2,1,0:T(8,128)(2,1)}) custom-call(s32[6]{0:T(128)} %stack.273.ids_ref, bf16[128,768]{1,0:T(8,128)(2,1)} %pad_maximum_fusion.23.refs_0_.x_ref, bf16[2,128,768]{2,1,0:T(8,128)(2,1)} %get-tuple-element.331.mine_ref, ...), custom_call_target="tpu_custom_call" | custom-call | flops 603979776 | bytes 5898240 | tf_op jit(solution)/shard_map/key_backward/pallas_call | solution.py:130
  248.8 11.5 %self_backward.2 = (bf16[512,384]{1,0:T(8,128)(2,1)}, bf16[2,512,384]{2,1,0:T(8,128)(2,1)}, bf16[2,512,384]{2,1,0:T(8,128)(2,1)}, f32[8,384]{1,0:T(8,128)}) custom-call(s32[6]{0:T(128)} %stack.273.ids_ref, bf16[512,768]{1,0:T(8,128)(2,1)} %get-tuple-element.275.q_ref, bf16[512,768]{1,0:T(8,128)(2,1)} %get-tuple-element.285.mixed_ref.self_mixed_ref, ...), custom_call_target="tpu_custom_call" | custom-call | flops 4026531840 | bytes 7507968 | tf_op jit(solution)/shard_map/self_backward/pallas_call | solution.py:130
  260.3 2.4 collective-permute-done.29
  267.2 2.1 fusion.13
  269.2 2.8 add_convert_fusion.4
  275.3 11.7 %self_backward.3 = (bf16[512,384]{1,0:T(8,128)(2,1)}, bf16[2,512,384]{2,1,0:T(8,128)(2,1)}, bf16[2,512,384]{2,1,0:T(8,128)(2,1)}, f32[8,384]{1,0:T(8,128)}) custom-call(s32[6]{0:T(128)} %stack.273.ids_ref, bf16[512,768]{1,0:T(8,128)(2,1)} %get-tuple-element.275.q_ref, bf16[512,768]{1,0:T(8,128)(2,1)} %get-tuple-element.285.mixed_ref.self_mixed_ref, ...), custom_call_target="tpu_custom_call" | custom-call | flops 4026531840 | bytes 7507968 | tf_op jit(solution)/shard_map/self_backward/pallas_call | solution.py:130
  288.5 5.9 %collective-permute-done.32 = bf16[576,768]{1,0:T(8,128)(2,1)} collective-permute-done((bf16[576,768]{1,0:T(8,128)(2,1)}, bf16[576,768]{1,0:T(8,128)(2,1)}, u32[]{:S(2)}, u32[]{:S(2)}) %collective-permute-start.32) | collective-permute-done | bytes 884768 | tf_op jit(solution)/shard_map/ppermute | solution.py:804
  298.4 5.1 %query_backward.1 = (f32[512,768]{1,0:T(8,128)}, f32[24,768]{1,0:T(8,128)}, bf16[16,1,24,768]{3,2,1,0:T(8,128)(2,1)}, bf16[16,1,24,768]{3,2,1,0:T(8,128)(2,1)}) custom-call(s32[6]{0:T(128)} %stack.273.ids_ref, bf16[512,768]{1,0:T(8,128)(2,1)} %pad_maximum_fusion.4.refs_0_.x_ref, f32[512,768]{1,0:T(8,128)} %get-tuple-element.374.grad_ref, ...), custom_call_target="tpu_custom_call" | custom-call | flops 1207959552 | bytes 7249920 | tf_op jit(solution)/shard_map/query_backward/pallas_call | solution.py:130
  311.1 5.0 %key_weights.1 = (bf16[2,512,768]{2,1,0:T(8,128)(2,1)}, bf16[16,1,24,768]{3,2,1,0:T(8,128)(2,1)}, bf16[16,1,24,768]{3,2,1,0:T(8,128)(2,1)}, bf16[16,1,24,768]{3,2,1,0:T(8,128)(2,1)}, bf16[16,1,24,768]{3,2,1,0:T(8,128)(2,1)}) custom-call(s32[6]{0:T(128)} %stack.273.ids_ref, bf16[512,768]{1,0:T(8,128)(2,1)} %pad_maximum_fusion.4.refs_0_.x_ref, ...), custom_call_target="tpu_custom_call" | custom-call | flops 1207959552 | bytes 7864320 | tf_op jit(solution)/shard_map/key_weights/pallas_call | solution.py:130
  317.1 1.7 collective-permute-done.37
  318.8 1.8 collective-permute-done.36
  326.8 4.9 %token_backward.1 = bf16[512,768]{1,0:T(8,128)(2,1)} custom-call(bf16[2,512,768]{2,1,0:T(8,128)(2,1)} %get-tuple-element.405.total_ref, f32[512,768]{1,0:T(8,128)} %get-tuple-element.406.part_ref, bf16[32,48,768]{2,1,0:T(8,128)(2,1)} %bitcast.434, bf16[32,32,768]{2,1,0:T(8,128)(2,1)} %bitcast.438), custom_call_target="tpu_custom_call" | custom-call | flops 1207959552 | bytes 6291456 | tf_op jit(solution)/shard_map/token_backward/pallas_call | solution.py:130
  331.7 3.1 collective-permute-done.42
  341.4 7.8 %collective-permute-done.51 = bf16[120,768]{1,0:T(8,128)(2,1)S(1)} collective-permute-done((bf16[120,768]{1,0:T(8,128)(2,1)S(1)}, bf16[120,768]{1,0:T(8,128)(2,1)S(1)}, u32[]{:S(2)}, u32[]{:S(2)}) %collective-permute-start.51) | collective-permute-done | bytes 184352 | tf_op jit(solution)/shard_map/ppermute | solution.py:804
  351.6 3.0 collective-permute-done.46
  357.1 7.8 %collective-permute-done.48 = bf16[160,768]{1,0:T(8,128)(2,1)S(1)} collective-permute-done((bf16[160,768]{1,0:T(8,128)(2,1)S(1)}, bf16[160,768]{1,0:T(8,128)(2,1)S(1)}, u32[]{:S(2)}, u32[]{:S(2)}) %collective-permute-start.48) | collective-permute-done | bytes 245792 | tf_op jit(solution)/shard_map/ppermute | solution.py:804
  364.9 1.9 collective-permute-done.49
  369.7 5.6 %collective-permute-done.50 = bf16[80,768]{1,0:T(8,128)(2,1)S(1)} collective-permute-done((bf16[80,768]{1,0:T(8,128)(2,1)S(1)}, bf16[80,768]{1,0:T(8,128)(2,1)S(1)}, u32[]{:S(2)}, u32[]{:S(2)}) %collective-permute-start.50) | collective-permute-done | bytes 122912 | tf_op jit(solution)/shard_map/ppermute | solution.py:804
  (299 shorter events, 100.8 us)
Async XLA Ops:
  7.2 131.3 %all-gather.3.cloned.1.call-start = ((), (), s32[]{:S(2)}) async-start(), calls=%async_computation.2 | async-start | bytes 13381632 | tf_op jit(solution)/shard_map/all_gather | solution.py:1023
  16.8 299.3 %reduce-scatter.2.cloned.1.call-start = ((), (), s32[]{:S(2)}) async-start(), calls=%async_computation.1 | async-start | bytes 1474560 | tf_op jit(solution)/shard_map/reduce_scatter | solution.py:1152
  16.8 10.1 %collective-permute-start = (bf16[80,768]{1,0:T(8,128)(2,1)S(1)}, bf16[80,768]{1,0:T(8,128)(2,1)S(1)}, u32[]{:S(2)}, u32[]{:S(2)}) collective-permute-start(bf16[80,768]{1,0:T(8,128)(2,1)S(1)} %pad_maximum_fusion.26), channel_id=1, source_target_pairs={{0,16},{4,20},{8,24},{12,28},{16,0},{20,4},{24,8},{28,12},{1,17},{... | collective-permute-start | bytes 368648 | tf_op jit(solution)/shard_map/ppermute | solution.py:804
  21.6 7.2 %collective-permute-start.1 = (bf16[128,768]{1,0:T(8,128)(2,1)S(1)}, bf16[128,768]{1,0:T(8,128)(2,1)S(1)}, u32[]{:S(2)}, u32[]{:S(2)}) collective-permute-start(bf16[128,768]{1,0:T(8,128)(2,1)S(1)} %get-tuple-element.492), channel_id=1, source_target_pairs={{0,3},{1,2},{2,1},{3,0},{4,7},{5,6},{6,5},{7,4},{8,11},{9,10},{10,... | collective-permute-start | bytes 589832 | tf_op jit(solution)/shard_map/ppermute | solution.py:779
  28.8 14.2 %collective-permute-start.3 = (bf16[192,768]{1,0:T(8,128)(2,1)S(1)}, bf16[192,768]{1,0:T(8,128)(2,1)S(1)}, u32[]{:S(2)}, u32[]{:S(2)}) collective-permute-start(bf16[192,768]{1,0:T(8,128)(2,1)S(1)} %pad_maximum_fusion.15), channel_id=1, source_target_pairs={{0,3},{1,2},{2,1},{3,0},{4,7},{5,6},{6,5},{7,4},{8,11},{9,10},{10,... | collective-permute-start | bytes 884744 | tf_op jit(solution)/shard_map/ppermute | solution.py:779
  29.6 13.4 %collective-permute-start.2 = (bf16[160,768]{1,0:T(8,128)(2,1)S(1)}, bf16[160,768]{1,0:T(8,128)(2,1)S(1)}, u32[]{:S(2)}, u32[]{:S(2)}) collective-permute-start(bf16[160,768]{1,0:T(8,128)(2,1)S(1)} %bitcast.465), channel_id=1, source_target_pairs={{0,8},{4,12},{8,0},{12,4},{16,24},{20,28},{24,16},{28,20},{1,9},{5... | collective-permute-start | bytes 737288 | tf_op jit(solution)/shard_map/ppermute | solution.py:804
  43.1 9.6 %collective-permute-start.4 = (bf16[192,768]{1,0:T(8,128)(2,1)S(1)}, bf16[192,768]{1,0:T(8,128)(2,1)S(1)}, u32[]{:S(2)}, u32[]{:S(2)}) collective-permute-start(bf16[192,768]{1,0:T(8,128)(2,1)S(1)} %bitcast.461), channel_id=1, source_target_pairs={{0,4},{4,0},{8,12},{12,8},{16,20},{20,16},{24,28},{28,24},{1,5},{5... | collective-permute-start | bytes 884744 | tf_op jit(solution)/shard_map/ppermute | solution.py:804
  44.7 8.0 %collective-permute-start.5 = (bf16[128,768]{1,0:T(8,128)(2,1)S(1)}, bf16[128,768]{1,0:T(8,128)(2,1)S(1)}, u32[]{:S(2)}, u32[]{:S(2)}) collective-permute-start(bf16[128,768]{1,0:T(8,128)(2,1)S(1)} %bitcast.469), channel_id=1, source_target_pairs={{0,2},{1,3},{2,0},{3,1},{4,6},{5,7},{6,4},{7,5},{8,10},{9,11},{10,... | collective-permute-start | bytes 589832 | tf_op jit(solution)/shard_map/ppermute | solution.py:804
  46.1 6.6 %collective-permute-start.6 = (bf16[48,768]{1,0:T(8,128)(2,1)S(1)}, bf16[48,768]{1,0:T(8,128)(2,1)S(1)}, u32[]{:S(2)}, u32[]{:S(2)}) collective-permute-start(bf16[48,768]{1,0:T(8,128)(2,1)S(1)} %pad_maximum_fusion.28), channel_id=1, source_target_pairs={{0,16},{4,20},{8,24},{12,28},{16,0},{20,4},{24,8},{28,12},{1,17},{... | collective-permute-start | bytes 221192 | tf_op jit(solution)/shard_map/ppermute | solution.py:804
  53.0 24.6 %collective-permute-start.7 = (bf16[384,768]{1,0:T(8,128)(2,1)S(1)}, bf16[384,768]{1,0:T(8,128)(2,1)S(1)}, u32[]{:S(2)}, u32[]{:S(2)}) collective-permute-start(bf16[384,768]{1,0:T(8,128)(2,1)S(1)} %bitcast.444), channel_id=1, source_target_pairs={{0,2},{1,3},{2,0},{3,1},{4,6},{5,7},{6,4},{7,5},{8,10},{9,11},{10,... | collective-permute-start | bytes 1769480 | tf_op jit(solution)/shard_map/ppermute | solution.py:804
  53.9 13.7 %collective-permute-start.8 = (bf16[256,768]{1,0:T(8,128)(2,1)S(1)}, bf16[256,768]{1,0:T(8,128)(2,1)S(1)}, u32[]{:S(2)}, u32[]{:S(2)}) collective-permute-start(bf16[256,768]{1,0:T(8,128)(2,1)S(1)} %bitcast.450), channel_id=1, source_target_pairs={{0,4},{4,0},{8,12},{12,8},{16,20},{20,16},{24,28},{28,24},{1,5},{5... | collective-permute-start | bytes 1179656 | tf_op jit(solution)/shard_map/ppermute | solution.py:804
  55.4 9.8 %collective-permute-start.9 = (bf16[96,768]{1,0:T(8,128)(2,1)S(1)}, bf16[96,768]{1,0:T(8,128)(2,1)S(1)}, u32[]{:S(2)}, u32[]{:S(2)}) collective-permute-start(bf16[96,768]{1,0:T(8,128)(2,1)S(1)} %bitcast.483), channel_id=1, source_target_pairs={{0,8},{4,12},{8,0},{12,4},{16,24},{20,28},{24,16},{28,20},{1,9},{5... | collective-permute-start | bytes 442376 | tf_op jit(solution)/shard_map/ppermute | solution.py:804
  82.1 14.0 %collective-permute-start.12 = (bf16[96,768]{1,0:T(8,128)(2,1)}, bf16[96,768]{1,0:T(8,128)(2,1)S(1)}, u32[]{:S(2)}, u32[]{:S(2)}) collective-permute-start(bf16[96,768]{1,0:T(8,128)(2,1)} %bitcast.53), channel_id=1, source_target_pairs={{0,4},{4,0},{8,12},{12,8},{16,20},{20,16},{24,28},{28,24},{1,5},{5... | collective-permute-start | bytes 442376 | tf_op jit(solution)/shard_map/ppermute | solution.py:804
  83.6 12.5 %collective-permute-start.13 = (bf16[96,768]{1,0:T(8,128)(2,1)}, bf16[96,768]{1,0:T(8,128)(2,1)S(1)}, u32[]{:S(2)}, u32[]{:S(2)}) collective-permute-start(bf16[96,768]{1,0:T(8,128)(2,1)} %bitcast.55), channel_id=1, source_target_pairs={{0,2},{1,3},{2,0},{3,1},{4,6},{5,7},{6,4},{7,5},{8,10},{9,11},{10,... | collective-permute-start | bytes 442376 | tf_op jit(solution)/shard_map/ppermute | solution.py:804
  97.7 4.8 %collective-permute-start.16 = (bf16[2,512,768]{2,1,0:T(8,128)(2,1)S(1)}, bf16[2,512,768]{2,1,0:T(8,128)(2,1)}, u32[]{:S(2)}, u32[]{:S(2)}) collective-permute-start(bf16[2,512,768]{2,1,0:T(8,128)(2,1)S(1)} %copy-done.37), channel_id=1, source_target_pairs={{0,1},{1,0},{2,3},{3,2},{4,5},{5,4},{6,7},{7,6},{8,9},{9,8},{10,11... | collective-permute-start | bytes 4718600 | tf_op jit(solution)/shard_map/ppermute | solution.py:779
  99.7 17.6 %collective-permute-start.14 = (bf16[192,768]{1,0:T(8,128)(2,1)S(1)}, bf16[192,768]{1,0:T(8,128)(2,1)S(1)}, u32[]{:S(2)}, u32[]{:S(2)}) collective-permute-start(bf16[192,768]{1,0:T(8,128)(2,1)S(1)} %bitcast.463), channel_id=1, source_target_pairs={{0,2},{1,3},{2,0},{3,1},{4,6},{5,7},{6,4},{7,5},{8,10},{9,11},{10,... | collective-permute-start | bytes 884744 | tf_op jit(solution)/shard_map/ppermute | solution.py:804
  101.4 15.9 %collective-permute-start.15 = (bf16[192,768]{1,0:T(8,128)(2,1)S(1)}, bf16[192,768]{1,0:T(8,128)(2,1)S(1)}, u32[]{:S(2)}, u32[]{:S(2)}) collective-permute-start(bf16[192,768]{1,0:T(8,128)(2,1)S(1)} %bitcast.462), channel_id=1, source_target_pairs={{0,4},{4,0},{8,12},{12,8},{16,20},{20,16},{24,28},{28,24},{1,5},{5... | collective-permute-start | bytes 884744 | tf_op jit(solution)/shard_map/ppermute | solution.py:804
  120.5 11.1 %collective-permute-start.19 = (bf16[256,768]{1,0:T(8,128)(2,1)S(1)}, bf16[256,768]{1,0:T(8,128)(2,1)S(1)}, u32[]{:S(2)}, u32[]{:S(2)}) collective-permute-start(bf16[256,768]{1,0:T(8,128)(2,1)S(1)} %pad_maximum_fusion.11), channel_id=1, source_target_pairs={{0,3},{1,2},{2,1},{3,0},{4,7},{5,6},{6,5},{7,4},{8,11},{9,10},{10,... | collective-permute-start | bytes 1179656 | tf_op jit(solution)/shard_map/ppermute | solution.py:779
  170.3 11.1 %collective-permute-start.21 = (bf16[256,768]{1,0:T(8,128)(2,1)S(1)}, bf16[256,768]{1,0:T(8,128)(2,1)S(1)}, u32[]{:S(2)}, u32[]{:S(2)}) collective-permute-start(bf16[256,768]{1,0:T(8,128)(2,1)S(1)} %pad_maximum_fusion.12), channel_id=1, source_target_pairs={{0,3},{1,2},{2,1},{3,0},{4,7},{5,6},{6,5},{7,4},{8,11},{9,10},{10,... | collective-permute-start | bytes 1179656 | tf_op jit(solution)/shard_map/ppermute | solution.py:779
  181.5 18.0 %collective-permute-start.22 = (bf16[1536,768]{1,0:T(8,128)(2,1)}, bf16[1536,768]{1,0:T(8,128)(2,1)}, u32[]{:S(2)}, u32[]{:S(2)}) collective-permute-start(bf16[1536,768]{1,0:T(8,128)(2,1)} %bitcast.540), channel_id=1, source_target_pairs={{0,1},{1,0},{2,3},{3,2},{4,5},{5,4},{6,7},{7,6},{8,9},{9,8},{10,11... | collective-permute-start | bytes 7077896 | tf_op jit(solution)/shard_map/ppermute | solution.py:804
  199.5 5.2 %collective-permute-start.23 = (bf16[1536,768]{1,0:T(8,128)(2,1)}, bf16[1536,768]{1,0:T(8,128)(2,1)}, u32[]{:S(2)}, u32[]{:S(2)}) collective-permute-start(bf16[1536,768]{1,0:T(8,128)(2,1)} %bitcast.539), channel_id=1, source_target_pairs={{0,1},{1,0},{2,3},{3,2},{4,5},{5,4},{6,7},{7,6},{8,9},{9,8},{10,11... | collective-permute-start | bytes 7077896 | tf_op jit(solution)/shard_map/ppermute | solution.py:804
  203.3 28.3 %collective-permute-start.24 = (bf16[768,768]{1,0:T(8,128)(2,1)}, bf16[768,768]{1,0:T(8,128)(2,1)S(1)}, u32[]{:S(2)}, u32[]{:S(2)}) collective-permute-start(bf16[768,768]{1,0:T(8,128)(2,1)} %bitcast.116), channel_id=1, source_target_pairs={{0,2},{1,3},{2,0},{3,1},{4,6},{5,7},{6,4},{7,5},{8,10},{9,11},{10,... | collective-permute-start | bytes 3538952 | tf_op jit(solution)/shard_map/ppermute | solution.py:804
  207.2 28.2 %collective-permute-start.25 = (bf16[768,768]{1,0:T(8,128)(2,1)}, bf16[768,768]{1,0:T(8,128)(2,1)}, u32[]{:S(2)}, u32[]{:S(2)}) collective-permute-start(bf16[768,768]{1,0:T(8,128)(2,1)} %bitcast.118), channel_id=1, source_target_pairs={{0,4},{4,0},{8,12},{12,8},{16,20},{20,16},{24,28},{28,24},{1,5},{5... | collective-permute-start | bytes 3538952 | tf_op jit(solution)/shard_map/ppermute | solution.py:804
  243.7 19.0 %collective-permute-start.27 = (bf16[1152,768]{1,0:T(8,128)(2,1)}, bf16[1152,768]{1,0:T(8,128)(2,1)}, u32[]{:S(2)}, u32[]{:S(2)}) collective-permute-start(bf16[1152,768]{1,0:T(8,128)(2,1)} %bitcast.448), channel_id=1, source_target_pairs={{0,1},{1,0},{2,3},{3,2},{4,5},{5,4},{6,7},{7,6},{8,9},{9,8},{10,11... | collective-permute-start | bytes 5308424 | tf_op jit(solution)/shard_map/ppermute | solution.py:804
  244.2 18.5 %collective-permute-start.28 = (bf16[768,768]{1,0:T(8,128)(2,1)}, bf16[768,768]{1,0:T(8,128)(2,1)}, u32[]{:S(2)}, u32[]{:S(2)}) collective-permute-start(bf16[768,768]{1,0:T(8,128)(2,1)} %bitcast.541), channel_id=1, source_target_pairs={{0,1},{1,0},{2,3},{3,2},{4,5},{5,4},{6,7},{7,6},{8,9},{9,8},{10,11... | collective-permute-start | bytes 3538952 | tf_op jit(solution)/shard_map/ppermute | solution.py:804
  244.2 18.5 %collective-permute-start.30 = (bf16[384,768]{1,0:T(8,128)(2,1)}, bf16[384,768]{1,0:T(8,128)(2,1)}, u32[]{:S(2)}, u32[]{:S(2)}) collective-permute-start(bf16[384,768]{1,0:T(8,128)(2,1)} %bitcast.487), channel_id=1, source_target_pairs={{0,4},{4,0},{8,12},{12,8},{16,20},{20,16},{24,28},{28,24},{1,5},{5... | collective-permute-start | bytes 1769480 | tf_op jit(solution)/shard_map/ppermute | solution.py:804
  245.6 17.1 %collective-permute-start.31 = (bf16[384,768]{1,0:T(8,128)(2,1)}, bf16[384,768]{1,0:T(8,128)(2,1)}, u32[]{:S(2)}, u32[]{:S(2)}) collective-permute-start(bf16[384,768]{1,0:T(8,128)(2,1)} %bitcast.486), channel_id=1, source_target_pairs={{0,2},{1,3},{2,0},{3,1},{4,6},{5,7},{6,4},{7,5},{8,10},{9,11},{10,... | collective-permute-start | bytes 1769480 | tf_op jit(solution)/shard_map/ppermute | solution.py:804
  247.9 14.8 %collective-permute-start.29 = (bf16[64,768]{1,0:T(8,128)(2,1)S(1)}, bf16[64,768]{1,0:T(8,128)(2,1)S(1)}, u32[]{:S(2)}, u32[]{:S(2)}) collective-permute-start(bf16[64,768]{1,0:T(8,128)(2,1)S(1)} %get-tuple-element.345), channel_id=1, source_target_pairs={{0,3},{1,2},{2,1},{3,0},{4,7},{5,6},{6,5},{7,4},{8,11},{9,10},{10,... | collective-permute-start | bytes 294920 | tf_op jit(solution)/shard_map/ppermute | solution.py:779
  272.1 22.4 %collective-permute-start.32 = (bf16[576,768]{1,0:T(8,128)(2,1)}, bf16[576,768]{1,0:T(8,128)(2,1)}, u32[]{:S(2)}, u32[]{:S(2)}) collective-permute-start(bf16[576,768]{1,0:T(8,128)(2,1)} %bitcast.142), channel_id=1, source_target_pairs={{0,2},{1,3},{2,0},{3,1},{4,6},{5,7},{6,4},{7,5},{8,10},{9,11},{10,... | collective-permute-start | bytes 2654216 | tf_op jit(solution)/shard_map/ppermute | solution.py:804
  272.7 15.8 %collective-permute-start.33 = (bf16[384,768]{1,0:T(8,128)(2,1)}, bf16[384,768]{1,0:T(8,128)(2,1)}, u32[]{:S(2)}, u32[]{:S(2)}) collective-permute-start(bf16[384,768]{1,0:T(8,128)(2,1)} %bitcast.144), channel_id=1, source_target_pairs={{0,4},{4,0},{8,12},{12,8},{16,20},{20,16},{24,28},{28,24},{1,5},{5... | collective-permute-start | bytes 1769480 | tf_op jit(solution)/shard_map/ppermute | solution.py:804
  297.0 9.3 %collective-permute-start.34 = (bf16[2,512,384]{2,1,0:T(8,128)(2,1)}, bf16[2,512,384]{2,1,0:T(8,128)(2,1)}, u32[]{:S(2)}, u32[]{:S(2)}) collective-permute-start(bf16[2,512,384]{2,1,0:T(8,128)(2,1)} %get-tuple-element.383), channel_id=1, source_target_pairs={{0,1},{1,0},{2,3},{3,2},{4,5},{5,4},{6,7},{7,6},{8,9},{9,8},{10,11... | collective-permute-start | bytes 2359304 | tf_op jit(solution)/shard_map/ppermute | solution.py:779
  297.1 9.3 %collective-permute-start.35 = (bf16[2,512,384]{2,1,0:T(8,128)(2,1)}, bf16[2,512,384]{2,1,0:T(8,128)(2,1)}, u32[]{:S(2)}, u32[]{:S(2)}) collective-permute-start(bf16[2,512,384]{2,1,0:T(8,128)(2,1)} %get-tuple-element.385), channel_id=1, source_target_pairs={{0,1},{1,0},{2,3},{3,2},{4,5},{5,4},{6,7},{7,6},{8,9},{9,8},{10,11... | collective-permute-start | bytes 2359304 | tf_op jit(solution)/shard_map/ppermute | solution.py:779
  306.3 14.3 %collective-permute-start.38 = (bf16[512,768]{1,0:T(8,128)(2,1)S(1)}, bf16[512,768]{1,0:T(8,128)(2,1)}, u32[]{:S(2)}, u32[]{:S(2)}) collective-permute-start(bf16[512,768]{1,0:T(8,128)(2,1)S(1)} %bitcast.466), channel_id=1, source_target_pairs={{0,1},{1,0},{2,3},{3,2},{4,5},{5,4},{6,7},{7,6},{8,9},{9,8},{10,11... | collective-permute-start | bytes 2359304 | tf_op jit(solution)/shard_map/ppermute | solution.py:804
  308.0 12.6 %collective-permute-start.36 = (bf16[288,768]{1,0:T(8,128)(2,1)S(1)}, bf16[288,768]{1,0:T(8,128)(2,1)}, u32[]{:S(2)}, u32[]{:S(2)}) collective-permute-start(bf16[288,768]{1,0:T(8,128)(2,1)S(1)} %bitcast.489), channel_id=1, source_target_pairs={{0,4},{4,0},{8,12},{12,8},{16,20},{20,16},{24,28},{28,24},{1,5},{5... | collective-permute-start | bytes 1327112 | tf_op jit(solution)/shard_map/ppermute | solution.py:804
  309.7 9.1 %collective-permute-start.37 = (bf16[192,768]{1,0:T(8,128)(2,1)S(1)}, bf16[192,768]{1,0:T(8,128)(2,1)S(1)}, u32[]{:S(2)}, u32[]{:S(2)}) collective-permute-start(bf16[192,768]{1,0:T(8,128)(2,1)S(1)} %bitcast.500), channel_id=1, source_target_pairs={{0,2},{1,3},{2,0},{3,1},{4,6},{5,7},{6,4},{7,5},{8,10},{9,11},{10,... | collective-permute-start | bytes 884744 | tf_op jit(solution)/shard_map/ppermute | solution.py:804
  323.3 11.7 %collective-permute-start.39 = (bf16[384,768]{1,0:T(8,128)(2,1)}, bf16[384,768]{1,0:T(8,128)(2,1)S(1)}, u32[]{:S(2)}, u32[]{:S(2)}) collective-permute-start(bf16[384,768]{1,0:T(8,128)(2,1)} %bitcast.172), channel_id=1, source_target_pairs={{0,1},{1,0},{2,3},{3,2},{4,5},{5,4},{6,7},{7,6},{8,9},{9,8},{10,11... | collective-permute-start | bytes 1769480 | tf_op jit(solution)/shard_map/ppermute | solution.py:804
  323.4 11.6 %collective-permute-start.40 = (bf16[384,768]{1,0:T(8,128)(2,1)}, bf16[384,768]{1,0:T(8,128)(2,1)S(1)}, u32[]{:S(2)}, u32[]{:S(2)}) collective-permute-start(bf16[384,768]{1,0:T(8,128)(2,1)} %bitcast.174), channel_id=1, source_target_pairs={{0,1},{1,0},{2,3},{3,2},{4,5},{5,4},{6,7},{7,6},{8,9},{9,8},{10,11... | collective-permute-start | bytes 1769480 | tf_op jit(solution)/shard_map/ppermute | solution.py:804
  323.9 11.1 %collective-permute-start.41 = (bf16[256,768]{1,0:T(8,128)(2,1)S(1)}, bf16[256,768]{1,0:T(8,128)(2,1)S(1)}, u32[]{:S(2)}, u32[]{:S(2)}) collective-permute-start(bf16[256,768]{1,0:T(8,128)(2,1)S(1)} %bitcast.493), channel_id=1, source_target_pairs={{0,4},{4,0},{8,12},{12,8},{16,20},{20,16},{24,28},{28,24},{1,5},{5... | collective-permute-start | bytes 1179656 | tf_op jit(solution)/shard_map/ppermute | solution.py:804
  324.5 10.3 %collective-permute-start.42 = (bf16[240,768]{1,0:T(8,128)(2,1)S(1)}, bf16[240,768]{1,0:T(8,128)(2,1)S(1)}, u32[]{:S(2)}, u32[]{:S(2)}) collective-permute-start(bf16[240,768]{1,0:T(8,128)(2,1)S(1)} %bitcast.496), channel_id=1, source_target_pairs={{0,8},{4,12},{8,0},{12,4},{16,24},{20,28},{24,16},{28,20},{1,9},{5... | collective-permute-start | bytes 1105928 | tf_op jit(solution)/shard_map/ppermute | solution.py:804
  336.4 12.8 %collective-permute-start.43 = (bf16[192,768]{1,0:T(8,128)(2,1)S(1)}, bf16[192,768]{1,0:T(8,128)(2,1)S(1)}, u32[]{:S(2)}, u32[]{:S(2)}) collective-permute-start(bf16[192,768]{1,0:T(8,128)(2,1)S(1)} %bitcast.499), channel_id=1, source_target_pairs={{0,2},{1,3},{2,0},{3,1},{4,6},{5,7},{6,4},{7,5},{8,10},{9,11},{10,... | collective-permute-start | bytes 884744 | tf_op jit(solution)/shard_map/ppermute | solution.py:804
  337.6 11.6 %collective-permute-start.44 = (bf16[192,768]{1,0:T(8,128)(2,1)S(1)}, bf16[192,768]{1,0:T(8,128)(2,1)S(1)}, u32[]{:S(2)}, u32[]{:S(2)}) collective-permute-start(bf16[192,768]{1,0:T(8,128)(2,1)S(1)} %bitcast.498), channel_id=1, source_target_pairs={{0,4},{4,0},{8,12},{12,8},{16,20},{20,16},{24,28},{28,24},{1,5},{5... | collective-permute-start | bytes 884744 | tf_op jit(solution)/shard_map/ppermute | solution.py:804
  338.4 10.8 %collective-permute-start.45 = (bf16[128,768]{1,0:T(8,128)(2,1)S(1)}, bf16[128,768]{1,0:T(8,128)(2,1)S(1)}, u32[]{:S(2)}, u32[]{:S(2)}) collective-permute-start(bf16[128,768]{1,0:T(8,128)(2,1)S(1)} %bitcast.515), channel_id=1, source_target_pairs={{0,2},{1,3},{2,0},{3,1},{4,6},{5,7},{6,4},{7,5},{8,10},{9,11},{10,... | collective-permute-start | bytes 589832 | tf_op jit(solution)/shard_map/ppermute | solution.py:804
  339.7 9.5 %collective-permute-start.51 = (bf16[120,768]{1,0:T(8,128)(2,1)S(1)}, bf16[120,768]{1,0:T(8,128)(2,1)S(1)}, u32[]{:S(2)}, u32[]{:S(2)}) collective-permute-start(bf16[120,768]{1,0:T(8,128)(2,1)S(1)} %fusion.43), channel_id=1, source_target_pairs={{0,16},{4,20},{8,24},{12,28},{16,0},{20,4},{24,8},{28,12},{1,17},{... | collective-permute-start | bytes 552968 | tf_op jit(solution)/shard_map/ppermute | solution.py:804
  349.4 5.2 %collective-permute-start.46 = (bf16[96,768]{1,0:T(8,128)(2,1)S(1)}, bf16[96,768]{1,0:T(8,128)(2,1)S(1)}, u32[]{:S(2)}, u32[]{:S(2)}) collective-permute-start(bf16[96,768]{1,0:T(8,128)(2,1)S(1)} %bitcast.518), channel_id=1, source_target_pairs={{0,4},{4,0},{8,12},{12,8},{16,20},{20,16},{24,28},{28,24},{1,5},{5... | collective-permute-start | bytes 442376 | tf_op jit(solution)/shard_map/ppermute | solution.py:804
  350.6 5.2 %collective-permute-start.47 = (bf16[96,768]{1,0:T(8,128)(2,1)S(1)}, bf16[96,768]{1,0:T(8,128)(2,1)S(1)}, u32[]{:S(2)}, u32[]{:S(2)}) collective-permute-start(bf16[96,768]{1,0:T(8,128)(2,1)S(1)} %bitcast.519), channel_id=1, source_target_pairs={{0,2},{1,3},{2,0},{3,1},{4,6},{5,7},{6,4},{7,5},{8,10},{9,11},{10,... | collective-permute-start | bytes 442376 | tf_op jit(solution)/shard_map/ppermute | solution.py:804
  355.9 10.9 %collective-permute-start.49 = (bf16[256,768]{1,0:T(8,128)(2,1)S(1)}, bf16[256,768]{1,0:T(8,128)(2,1)S(1)}, u32[]{:S(2)}, u32[]{:S(2)}) collective-permute-start(bf16[256,768]{1,0:T(8,128)(2,1)S(1)} %pad_maximum_fusion.13), channel_id=1, source_target_pairs={{0,3},{1,2},{2,1},{3,0},{4,7},{5,6},{6,5},{7,4},{8,11},{9,10},{10,... | collective-permute-start | bytes 1179656 | tf_op jit(solution)/shard_map/ppermute | solution.py:779
  356.1 8.9 %collective-permute-start.48 = (bf16[160,768]{1,0:T(8,128)(2,1)S(1)}, bf16[160,768]{1,0:T(8,128)(2,1)S(1)}, u32[]{:S(2)}, u32[]{:S(2)}) collective-permute-start(bf16[160,768]{1,0:T(8,128)(2,1)S(1)} %bitcast.511), channel_id=1, source_target_pairs={{0,8},{4,12},{8,0},{12,4},{16,24},{20,28},{24,16},{28,20},{1,9},{5... | collective-permute-start | bytes 737288 | tf_op jit(solution)/shard_map/ppermute | solution.py:804
  366.9 8.4 %collective-permute-start.50 = (bf16[80,768]{1,0:T(8,128)(2,1)S(1)}, bf16[80,768]{1,0:T(8,128)(2,1)S(1)}, u32[]{:S(2)}, u32[]{:S(2)}) collective-permute-start(bf16[80,768]{1,0:T(8,128)(2,1)S(1)} %fusion.57), channel_id=1, source_target_pairs={{0,16},{4,20},{8,24},{12,28},{16,0},{20,4},{24,8},{28,12},{1,17},{... | collective-permute-start | bytes 368648 | tf_op jit(solution)/shard_map/ppermute | solution.py:804
  (48 other events, 259.0 us)
Sparse Core Ops, SparseCore 0:
  16.9 121.6 all-gather.2
  274.2 27.4 reduce-scatter.1

commit v3 on v2

--- a/solution.py
+++ b/solution.py
@@ -75,20 +75,54 @@
 ) = range(14)
 
 
-def pack_vectors(vectors, width):
+def pack_vectors(vectors, out_ref, base):
+    out_ref[base : base + 8, :] = jnp.zeros((8, out_ref.shape[1]), out_ref.dtype)
+    for i, ref in enumerate(vectors):
+        at = 128 * (i // 8)
+        out_ref[base + i % 8 : base + i % 8 + 1, at : at + ref.shape[1]] = ref[...]
+
+
+def pack(first, vectors, second, outer, inner, rest):
+    rows, width = first[0].shape
+    chunks = inner.shape[1] // width
+    counts = (len(first), len(vectors), len(second), 1, 1, len(rest))
+
     def kernel(*refs):
-        out_ref = refs[-1]
-        out_ref[...] = jnp.zeros_like(out_ref)
-        for i, ref in enumerate(refs[:-1]):
-            size = ref.shape[1]
-            at = 128 * (i // 8)
-            out_ref[i % 8 : i % 8 + 1, at : at + size] = ref[...]
-
-    return pl.pallas_call(
+        groups, at = [], 0
+        for count in counts:
+            groups.append(refs[at : at + count])
+            at += count
+        outs = refs[at:]
+        if rows % 8 == 0:
+            for i, ref in enumerate(groups[0]):
+                outs[0][i * rows : (i + 1) * rows, :] = ref[...]
+            for i, ref in enumerate(groups[2]):
+                outs[1][i * rows : (i + 1) * rows, :] = ref[...]
+            outs[2][: chunks * rows, :] = groups[3][0][...]
+            for i in range(chunks):
+                at = (chunks + i) * rows
+                outs[2][at : at + rows, :] = groups[4][0][:, i * width : (i + 1) * width]
+            for i, ref in enumerate(groups[5]):
+                at = (2 * chunks + i) * rows
+                outs[2][at : at + rows, :] = ref[...]
+        pack_vectors(groups[1], outs[0], len(first) * rows if rows % 8 == 0 else 0)
+
+    shapes = [len(first) * rows + 8, len(second) * rows, (2 * chunks + len(rest)) * rows]
+    if rows % 8:
+        shapes = [8, 8, 8]
+    outs = pl.pallas_call(
         kernel,
-        out_shape=jax.ShapeDtypeStruct((8, width), vectors[0].dtype),
-        name="pack_vectors",
-    )(*[v[None, :] for v in vectors])
+        out_shape=[jax.ShapeDtypeStruct((n, width), outer.dtype) for n in shapes],
+        name="pack",
+    )(*first, *[v[None, :] for v in vectors], *second, outer, inner, *rest)
+    if rows % 8 == 0:
+        return outs
+    inner = [inner[:, i * width : (i + 1) * width] for i in range(chunks)]
+    return [
+        jnp.concatenate(list(first) + [outs[0]], axis=0),
+        jnp.concatenate(second, axis=0),
+        jnp.concatenate([outer] + inner + list(rest), axis=0),
+    ]
 
 
 class Call:
@@ -96,6 +130,7 @@
         self.name, self.grid = name, grid
         self.ins, self.in_specs, self.out_shapes, self.out_specs = [], [], [], []
         self.flops, self.bytes, self.exps = 0, 0, 0
+        self.lates = []
 
     def whole(self, array):
         zeros = (0,) * array.ndim
@@ -110,6 +145,54 @@
     def scalars(self, array):
         self.ins.append(array)
         self.in_specs.append(pl.BlockSpec(memory_space=pltpu.SMEM))
+
+    def late(self, array, block=None, index=None):
+        self.ins.append(array)
+        self.in_specs.append(pl.BlockSpec(memory_space=pl.ANY))
+        block = block or array.shape
+        self.bytes += array.dtype.itemsize * array.size
+        self.lates.append((len(self.ins) - 1, block, index, array.dtype))
+
+    def late_weight(self, weight):
+        array, block, index = weight
+        self.late(array, block, tuple(i * n for i, n in zip(index, block)))
+
+    def late_copies(self, refs, late_refs):
+        count = len(self.lates)
+        copies = []
+        for i, (place, block, start, _) in enumerate(self.lates):
+            source = refs[place]
+            if start is not None:
+                source = source.at[tuple(pl.ds(a, n) for a, n in zip(start, block))]
+            copies.append(pltpu.make_async_copy(source, late_refs[i], late_refs[count].at[i]))
+        return copies
+
+    def run_late(self, kernel, scratch=()):
+        count = len(self.lates)
+        steps = self.grid[0]
+
+        def wrapped(*refs):
+            refs, late_refs = refs[: -count - 1], refs[-count - 1 :]
+            copies = self.late_copies(refs, late_refs)
+
+            @pl.when(pl.program_id(0) == 0)
+            def _():
+                for copy in copies:
+                    copy.start()
+
+            def fetch():
+                for copy in copies:
+                    copy.wait()
+
+            refs = list(refs)
+            for i, (place, _, _, _) in enumerate(self.lates):
+                refs[place] = late_refs[i]
+            kernel(fetch, *refs)
+
+        buffers = [pltpu.VMEM(block, dtype) for _, block, _, dtype in self.lates]
+        return self.run(
+            wrapped, list(scratch) + buffers + [pltpu.SemaphoreType.DMA((count,))]
+        )
 
     def weight(self, weight):
         array, block, index = weight
@@ -217,22 +300,46 @@
     return jnp.where(first, values, zero), jnp.where(first, zero, values)
 
 
+def key_parts(key_rows, masked):
+    if not masked:
+        return [(0, key_rows, 0)]
+    half = key_rows // 2
+    return [(0, half, 0), (half, key_rows, half)]
+
+
+def widened(values, first, rows, fill):
+    if first == 0:
+        return values
+    blank = jnp.full(values.shape[:-1] + (first,), fill, values.dtype)
+    return jnp.concatenate([blank, values], axis=-1)
+
+
 def attend_pair(queries, keys, values, bias_ref, log_ref):
+    rows = queries.shape[0]
     queries = lane_masks(queries)
+    parts = [
+        (chunk,) + part
+        for part in key_parts(keys[0].shape[0], bias_ref is not None)
+        for chunk in range(len(keys))
+    ]
     outs = []
     for head in range(2):
         scores = []
-        for chunk in range(2):
-            part = times_transpose(keys[chunk], queries[head])
-            scores.append(part if bias_ref is None else part + bias_ref[chunk])
-        top = jnp.maximum(
-            scores[0].max(axis=0, keepdims=True), scores[1].max(axis=0, keepdims=True)
-        )
+        for chunk, low_key, high_key, first in parts:
+            part = times_transpose(keys[chunk][low_key:high_key], queries[head][first:])
+            if bias_ref is not None:
+                part = part + bias_ref[chunk, low_key:high_key, first:]
+            scores.append(part)
+        top = None
+        for part, (_, _, _, first) in zip(scores, parts):
+            most = widened(part.max(axis=0, keepdims=True), first, rows, NEG)
+            top = most if top is None else jnp.maximum(top, most)
         total, mixed = 0.0, 0.0
-        for chunk in range(2):
-            weights = jnp.exp(scores[chunk] - top)
-            total = total + weights.sum(axis=0, keepdims=True)
-            mixed = mixed + contract_rows(values[chunk], low(weights))
+        for part, (chunk, low_key, high_key, first) in zip(scores, parts):
+            weights = jnp.exp(part - top[:, first:])
+            total = total + widened(weights.sum(axis=0, keepdims=True), first, rows, 0.0)
+            out = contract_rows(values[chunk][low_key:high_key], low(weights))
+            mixed = mixed + widened(out, first, rows, 0.0)
         outs.append(mixed * (1.0 / total))
         log_ref[0, head : head + 1, :] = top + jnp.log(total)
     lane = lax.broadcasted_iota(jnp.int32, outs[0].shape, 0)
@@ -240,6 +347,7 @@
 
 
 def attend_pair_backward(queries, keys, values, bias_ref, log_ref, mixed, upstream):
+    rows = queries.shape[0]
     queries = lane_masks(queries)
     ups = lane_masks(upstream)
     product = widen(mixed) * widen(upstream)
@@ -253,20 +361,28 @@
     ).astype(jnp.bfloat16)
     delta = times_transpose(pick, high) + times_transpose(pick, rest)
     dq = 0.0
-    dk = [0.0, 0.0]
-    dv = [0.0, 0.0]
+    parts = key_parts(keys[0].shape[0], bias_ref is not None)
+    dk = [[0.0] * len(parts) for _ in keys]
+    dv = [[0.0] * len(parts) for _ in keys]
     for head in range(2):
-        for chunk in range(2):
-            part = times_transpose(keys[chunk], queries[head])
-            if bias_ref is not None:
-                part = part + bias_ref[chunk]
-            probs = jnp.exp(part - log_ref[0, head : head + 1, :])
-            prob_grad = times_transpose(values[chunk], ups[head])
-            score_grad = low(probs * (prob_grad - delta[head : head + 1, :]))
-            dv[chunk] = dv[chunk] + matmul(low(probs), ups[head])
-            dk[chunk] = dk[chunk] + matmul(score_grad, queries[head])
-            dq = dq + contract_rows(lane_masks(keys[chunk])[head], score_grad)
-    return low(dq.T), dk, dv
+        for chunk in range(len(keys)):
+            masked_keys = lane_masks(keys[chunk])[head]
+            for i, (low_key, high_key, first) in enumerate(parts):
+                part = times_transpose(keys[chunk][low_key:high_key], queries[head][first:])
+                if bias_ref is not None:
+                    part = part + bias_ref[chunk, low_key:high_key, first:]
+                probs = jnp.exp(part - log_ref[0, head : head + 1, first:])
+                up = ups[head][first:]
+                prob_grad = times_transpose(values[chunk][low_key:high_key], up)
+                score_grad = low(probs * (prob_grad - delta[head : head + 1, first:]))
+                dv[chunk][i] = dv[chunk][i] + matmul(low(probs), up)
+                dk[chunk][i] = dk[chunk][i] + matmul(score_grad, queries[head][first:])
+                out = contract_rows(masked_keys[low_key:high_key], score_grad)
+                dq = dq + widened(out, first, rows, 0.0)
+    join = [
+        [v[0] if len(v) == 1 else jnp.concatenate(v, axis=0) for v in side] for side in (dk, dv)
+    ]
+    return low(dq.T), join[0], join[1]
 
 
 def project_kernel(scaled, x_ref, *refs):
@@ -362,76 +478,98 @@
     return call.run(kernel)
 
 
-def cross_attend(queries, own, other, first_pre, out_weight, vecs):
+def cross_attend(queries, keys, first_pre, out_weight, vecs):
     rows, width = queries.shape
-    key_rows = own.shape[1]
+    key_rows = keys.shape[1]
     pairs = HEADS // 2
     lanes, at = lanes_of(width)
     call = Call("cross_attend", (pairs,))
     call.blocked(queries, (rows, lanes), lambda h: (0, h))
-    for array in (own, other):
-        call.blocked(array, (2, key_rows, lanes), lambda h: (0, 0, h))
-    call.whole(first_pre)
-    call.weight(out_weight)
+    call.blocked(keys, (2, key_rows, lanes), lambda h: (0, 0, h))
+    call.late(first_pre)
+    call.late_weight(out_weight)
     call.whole(vecs)
     call.out((rows, width), jnp.bfloat16)
     call.out((pairs, 2, rows), jnp.float32, (1, 2, rows), lambda h: (h, 0, 0))
     call.out((rows, width), jnp.float32)
     call.out((rows, width), jnp.bfloat16)
-    call.flops = 16 * rows * key_rows * width + 2 * rows * width * width
+    call.flops = 8 * rows * key_rows * width + 2 * rows * width * width
     call.exps = 2 * rows * key_rows * HEADS
 
     def kernel(
-        q_ref, own_ref, other_ref, first_ref, wo_ref, vecs_ref, mixed_ref, log_ref, pre_ref, low_ref
+        fetch, q_ref, keys_ref, first_ref, wo_ref, vecs_ref, mixed_ref, log_ref, pre_ref, low_ref
     ):
         step = pl.program_id(0)
-        keys, values = (own_ref[0], other_ref[0]), (own_ref[1], other_ref[1])
-        mixed_ref[:, at(step)] = attend_pair(q_ref[...], keys, values, None, log_ref)
+        mixed_ref[:, at(step)] = attend_pair(
+            q_ref[...], (keys_ref[0],), (keys_ref[1],), None, log_ref
+        )
 
         @pl.when(step == pairs - 1)
         def _():
+            fetch()
             first = normalize(first_ref[...], row(vecs_ref, GAIN_ONE), row(vecs_ref, SHIFT_ONE))
             pre = first + matmul(mixed_ref[...], load(wo_ref)) + row(vecs_ref, CROSS_O)
             pre_ref[...] = pre
             low_ref[...] = low(normalize(pre, row(vecs_ref, GAIN_TWO), row(vecs_ref, SHIFT_TWO)))
 
-    return call.run(kernel)
+    return call.run_late(kernel)
 
 
 def feed_blocks(call, feed, width, chunks, owned_rows):
     owners = feed.shape[0]
+
+    def at(i):
+        return jnp.minimum(i, chunks - 1)
+
     hidden_rows = chunks * owned_rows
     if owned_rows % 8 == 0:
-        call.blocked(feed, (owners, owned_rows, width), lambda i: (0, chunks + i, 0))
-        call.blocked(feed, (owners // chunks, hidden_rows, width), lambda i: (i, 0, 0))
+        call.blocked(feed, (owners, owned_rows, width), lambda i: (0, chunks + at(i), 0))
+        call.blocked(feed, (owners // chunks, hidden_rows, width), lambda i: (at(i), 0, 0))
     else:
         parts = [
             feed[:, hidden_rows + i * owned_rows : hidden_rows + (i + 1) * owned_rows]
             for i in range(chunks)
         ]
         parts = [p.reshape(-1, width) for p in parts]
-        call.blocked(jnp.concatenate(parts, axis=1), (width, width), lambda i: (0, i))
-        call.blocked(feed[:, :hidden_rows].reshape(-1, width), (width, width), lambda i: (i, 0))
-
-
-def feed_forward(second_pre, second_low, feed, vecs, chunks, owned_rows):
+        call.blocked(jnp.concatenate(parts, axis=1), (width, width), lambda i: (0, at(i)))
+        call.blocked(feed[:, :hidden_rows].reshape(-1, width), (width, width), lambda i: (at(i), 0))
+
+
+def feed_forward(ids, second_pre, second_low, upstream, feed, vecs, chunks, owned_rows):
     rows, width = second_low.shape
     hidden = chunks * width
-    call = Call("feed_forward", (chunks,))
+    owners = width // owned_rows
+    call = Call("feed_forward", (2 * chunks,))
+    call.scalars(ids)
     call.whole(second_pre)
     call.whole(second_low)
+    call.late(upstream)
     feed_blocks(call, feed, width, chunks, owned_rows)
     call.whole(vecs)
-    call.out((rows, hidden), jnp.bfloat16, (rows, width), lambda i: (0, i))
-    call.out((rows, hidden), jnp.bfloat16, (rows, width), lambda i: (0, i))
+    call.out(
+        (rows, hidden), jnp.bfloat16, (rows, width), lambda i: (0, jnp.minimum(i, chunks - 1))
+    )
+    call.out((rows, width), jnp.bfloat16)
     call.out((rows, width), jnp.float32)
     call.out((rows, width), jnp.bfloat16)
-    call.flops = 4 * rows * hidden * width
+    call.out((24, width), jnp.float32)
+    half = Halves(
+        call,
+        1,
+        owners,
+        chunks * owned_rows,
+        width,
+        owners // 2 // chunks,
+        lambda i: (jnp.maximum(i - chunks, 0), 0),
+    )
+    call.flops = 6 * rows * hidden * width
     call.exps = 2 * rows * hidden
 
     def kernel(
-        pre_ref, low_ref, inner_ref, outer_ref, vecs_ref, active_ref, slope_ref, third_ref, out_ref
+        fetch, ids_ref, pre_ref, low_ref, up_ref, inner_ref, outer_ref, vecs_ref, slope_ref, out_ref,
+        grad_ref, third_low_ref, sums_ref, *rest,
     ):
+        grads, (active_ref, third_ref) = rest[:-2], rest[-2:]
         step = pl.program_id(0)
 
         @pl.when(step == 0)
@@ -439,57 +577,40 @@
             second = normalize(pre_ref[...], row(vecs_ref, GAIN_TWO), row(vecs_ref, SHIFT_TWO))
             third_ref[...] = second + row(vecs_ref, OUTER_B)
 
-        inner = matmul(low_ref[...], load(inner_ref)) + vecs_ref[pl.ds(INNER_B + step, 1), :]
-        bell = 0.5 * (1.0 + lax.erf(inner * 0.7071067811865476))
-        active = low(inner * bell)
-        active_ref[...] = active
-        density = jnp.exp(-0.5 * inner * inner) * 0.3989422804014327
-        slope_ref[...] = low(bell + inner * density)
-        third_ref[...] += matmul(active, load(outer_ref))
+        @pl.when(step < chunks)
+        def _():
+            inner = matmul(low_ref[...], load(inner_ref)) + vecs_ref[pl.ds(INNER_B + step, 1), :]
+            bell = 0.5 * (1.0 + lax.erf(inner * 0.7071067811865476))
+            active = low(inner * bell)
+            active_ref[step] = active
+            density = jnp.exp(-0.5 * inner * inner) * 0.3989422804014327
+            slope_ref[...] = low(bell + inner * density)
+            third_ref[...] += matmul(active, load(outer_ref))
 
         @pl.when(step == chunks - 1)
         def _():
-            out_ref[...] = low(
-                normalize(third_ref[...], row(vecs_ref, GAIN_THREE), row(vecs_ref, SHIFT_THREE))
-            )
-
-    return call.run(kernel)
-
-
-def outer_backward(ids, upstream, third_pre, active, vecs, chunks, owned_rows):
-    rows, width = third_pre.shape
-    owners = width // owned_rows
-    call = Call("outer_backward", (chunks,))
-    call.scalars(ids)
-    call.whole(upstream)
-    call.whole(third_pre)
-    call.blocked(active, (rows, width), lambda i: (0, i))
-    call.whole(vecs)
-    call.out((rows, width), jnp.float32)
-    call.out((rows, width), jnp.bfloat16)
-    call.out((24, width), jnp.float32)
-    half = Halves(
-        call, 1, owners, chunks * owned_rows, width, owners // 2 // chunks, lambda i: (i, 0)
-    )
-    call.flops = 2 * rows * chunks * width * width
-
-    def kernel(ids_ref, up_ref, third_ref, active_ref, vecs_ref, grad_ref, low_ref, sums_ref, *grads):
-        @pl.when(pl.program_id(0) == 0)
-        def _():
-            grad, gain_sum, shift_sum = norm_backward(
-                third_ref[...], row(vecs_ref, GAIN_THREE), widen(up_ref[...])
-            )
+            fetch()
+            third = third_ref[...]
+            gain = row(vecs_ref, GAIN_THREE)
+            out_ref[...] = low(normalize(third, gain, row(vecs_ref, SHIFT_THREE)))
+            grad, gain_sum, shift_sum = norm_backward(third, gain, widen(up_ref[...]))
             grad_ref[...] = grad
-            low_ref[...] = low(grad)
+            third_low_ref[...] = low(grad)
             sums_ref[...] = jnp.zeros_like(sums_ref)
             sums_ref[GAIN_THREE : GAIN_THREE + 1, :] = gain_sum
             sums_ref[SHIFT_THREE : SHIFT_THREE + 1, :] = shift_sum
             sums_ref[OUTER_B : OUTER_B + 1, :] = jnp.sum(widen(low(grad)), axis=0, keepdims=True)
 
-        half.store(grads, 0, contract_rows(active_ref[...], low_ref[...]), ids_ref[5])
-
-    results = call.run(kernel)
-    return tuple(results[:3]) + (half.pair(results[3:], ids[5]),)
+        @pl.when(step >= chunks)
+        def _():
+            active = active_ref[jnp.maximum(step - chunks, 0)]
+            half.store(grads, 0, contract_rows(active, third_low_ref[...]), ids_ref[5])
+
+    results = call.run_late(
+        kernel,
+        [pltpu.VMEM((chunks, rows, width), jnp.bfloat16), pltpu.VMEM((rows, width), jnp.float32)],
+    )
+    return tuple(results[:5]) + (half.pair(results[5:], ids[5]),)
 
 
 def inner_backward(
@@ -500,12 +621,14 @@
     owners = width // owned_rows
     call = Call("inner_backward", (chunks,))
     call.scalars(ids)
-    for array in (third_grad, third_low, sums, second_pre, second_low):
+    for array in (third_grad, third_low, sums):
         call.whole(array)
+    call.late(second_pre)
+    call.whole(second_low)
     call.blocked(slope, (rows, width), lambda i: (0, i))
-    call.whole(cross_mixed)
+    call.late(cross_mixed)
     feed_blocks(call, feed, width, chunks, owned_rows)
-    call.weight(out_weight)
+    call.late_weight(out_weight)
     call.whole(vecs)
     call.out((rows, width), jnp.float32)
     call.out((rows, width), jnp.bfloat16)
@@ -516,7 +639,7 @@
     outs = inner_half.outs
 
     def kernel(
-        ids_ref, third_ref, third_low_ref, sums_in_ref, second_ref, low_ref, slope_ref, mixed_ref, inner_ref, outer_ref,
+        fetch, ids_ref, third_ref, third_low_ref, sums_in_ref, second_ref, low_ref, slope_ref, mixed_ref, inner_ref, outer_ref,
         wo_ref, vecs_ref, second_grad_ref, mix_ref, sums_ref, *rest,
     ):
         inner_grads, out_grads, total_ref = rest[:outs], rest[outs:-1], rest[-1]
@@ -535,6 +658,7 @@
 
         @pl.when(step == chunks - 1)
         def _():
+            fetch()
             grad, gain_sum, shift_sum = norm_backward(
                 second_ref[...], row(vecs_ref, GAIN_TWO), total_ref[...]
             )
@@ -546,7 +670,7 @@
             mix_ref[...] = low(times_transpose(cross_low, load(wo_ref)))
             out_half.store(out_grads, 0, contract_rows(mixed_ref[...], cross_low), mine)
 
-    results = call.run(kernel, [pltpu.VMEM((rows, width), jnp.float32)])
+    results = call.run_late(kernel, [pltpu.VMEM((rows, width), jnp.float32)])
     core = ids[5]
     return tuple(results[:3]) + (
         inner_half.pair(results[3 : 3 + outs], core),
@@ -555,11 +679,11 @@
 
 
 def cross_backward(
-    ids, queries, own, other, mixed, upstream, logsum, first_low, first_pre, second_grad, self_mixed, sums,
-    query_weight, out_weight, vecs, owned_rows,
+    ids, queries, keys, mixed, upstream, logsum, first_low, first_pre, second_grad, self_mixed, sums,
+    encoder, query_weight, out_weight, key_weight, value_weight, vecs, owned_rows,
 ):
     rows, width = queries.shape
-    key_rows = own.shape[1]
+    key_rows = keys.shape[1]
     pairs = HEADS // 2
     lanes, at = lanes_of(width)
     call = Call("cross_backward", (pairs,))
@@ -567,61 +691,75 @@
     for array in (queries, mixed, upstream):
         call.blocked(array, (rows, lanes), lambda h: (0, h))
     call.blocked(logsum, (1, 2, rows), lambda h: (h, 0, 0))
-    for array in (own, other):
-        call.blocked(array, (2, key_rows, lanes), lambda h: (0, 0, h))
-    for array in (first_low, first_pre, second_grad, self_mixed, sums):
-        call.whole(array)
-    call.weight(query_weight)
-    call.weight(out_weight)
+    call.blocked(keys, (2, key_rows, lanes), lambda h: (0, 0, h))
+    for array in (first_low, first_pre, second_grad, self_mixed):
+        call.late(array)
+    call.whole(sums)
+    call.late_weight(query_weight)
+    call.late_weight(out_weight)
+    call.late(encoder)
+    call.late_weight(key_weight)
+    call.late_weight(value_weight)
     call.whole(vecs)
-    for _ in range(2):
-        call.out((2, key_rows, width), jnp.bfloat16, (2, key_rows, lanes), lambda h: (0, 0, h))
+    call.out((key_rows, width), jnp.bfloat16)
     call.out((rows, width), jnp.float32)
     call.out((rows, width), jnp.bfloat16)
     call.out((24, width), jnp.float32)
-    half = Halves(call, 2, width // owned_rows, owned_rows, width)
-    call.flops = 40 * rows * key_rows * width + 8 * rows * width * width
+    halves = [Halves(call, 2, width // owned_rows, owned_rows, width) for _ in range(2)]
+    outs = halves[0].outs
+    call.flops = 20 * rows * key_rows * width + 8 * (rows + key_rows) * width * width
     call.exps = 2 * rows * key_rows * HEADS
 
     def kernel(
-        ids_ref, q_ref, mixed_ref, up_ref, log_ref, own_ref, other_ref, low_ref, pre_ref, grad_ref,
-        self_mixed_ref, sums_in_ref, wq_ref, wo_ref, vecs_ref, own_out_ref, other_out_ref, first_ref, mix_ref,
+        fetch, ids_ref, q_ref, mixed_ref, up_ref, log_ref, keys_ref, low_ref, pre_ref, grad_ref,
+        self_mixed_ref, sums_in_ref, wq_ref, wo_ref, enc_ref, wk_ref, wv_ref, vecs_ref, enc_back_ref, first_ref, mix_ref,
         sums_ref, *rest,
     ):
         step = pl.program_id(0)
-        weights_refs, dq_ref = rest[:-1], rest[-1]
+        weights_refs, (dq_ref, dkv_ref) = rest[:-2], rest[-2:]
 
         @pl.when(step == 0)
         def _():
             sums_ref[...] = sums_in_ref[...]
 
-        keys, values = (own_ref[0], other_ref[0]), (own_ref[1], other_ref[1])
         dq, dk, dv = attend_pair_backward(
-            q_ref[...], keys, values, None, log_ref, mixed_ref[...], up_ref[...]
+            q_ref[...], (keys_ref[0],), (keys_ref[1],), None, log_ref, mixed_ref[...], up_ref[...]
         )
         dq_ref[:, at(step)] = dq
-        for chunk, out in enumerate((own_out_ref, other_out_ref)):
-            out[0] = low(dk[chunk])
-            out[1] = low(dv[chunk])
+        dkv_ref[0, :, at(step)] = low(dk[0])
+        dkv_ref[1, :, at(step)] = low(dv[0])
         sums_ref[CROSS_V : CROSS_V + 1, at(step)] = sum(jnp.sum(v, axis=0, keepdims=True) for v in dv)
 
         @pl.when(step == pairs - 1)
         def _():
+            fetch()
             query_low = dq_ref[...]
-            half.store(weights_refs, 0, contract_rows(low_ref[...], query_low) * 0.125, ids_ref[5])
+            halves[0].store(weights_refs[:outs], 0, contract_rows(low_ref[...], query_low) * 0.125, ids_ref[5])
+            for i in range(2):
+                value = contract_rows(enc_ref[...], dkv_ref[i])
+                halves[1].store(weights_refs[outs:], i, value, ids_ref[5])
+            enc_back_ref[...] = low(
+                times_transpose(dkv_ref[0], load(wk_ref)) + times_transpose(dkv_ref[1], load(wv_ref))
+            )
             total = grad_ref[...] + times_transpose(query_low, load(wq_ref)) * 0.125
             grad, gain_sum, shift_sum = norm_backward(pre_ref[...], row(vecs_ref, GAIN_ONE), total)
             first_ref[...] = grad
             self_low = low(grad)
             mix_ref[...] = low(times_transpose(self_low, load(wo_ref)))
-            half.store(weights_refs, 1, contract_rows(self_mixed_ref[...], self_low), ids_ref[5])
+            halves[0].store(weights_refs[:outs], 1, contract_rows(self_mixed_ref[...], self_low), ids_ref[5])
             sums_ref[GAIN_ONE : GAIN_ONE + 1, :] = gain_sum
             sums_ref[SHIFT_ONE : SHIFT_ONE + 1, :] = shift_sum
             sums_ref[SELF_O : SELF_O + 1, :] = jnp.sum(widen(self_low), axis=0, keepdims=True)
             sums_ref[CROSS_Q : CROSS_Q + 1, :] = jnp.sum(widen(query_low), axis=0, keepdims=True) * 0.125
 
-    results = call.run(kernel, [pltpu.VMEM((rows, width), jnp.bfloat16)])
-    return tuple(results[:5]) + (half.pair(results[5:], ids[5]),)
+    results = call.run_late(
+        kernel,
+        [pltpu.VMEM((rows, width), jnp.bfloat16), pltpu.VMEM((2, key_rows, width), jnp.bfloat16)],
+    )
+    return tuple(results[:4]) + (
+        halves[0].pair(results[4 : 4 + outs], ids[5]),
+        halves[1].pair(results[4 + outs :], ids[5]),
+    )
 
 
 def self_backward(ids, queries, own, other, mixed, upstream, logsum, first, last):
@@ -745,32 +883,6 @@
     return call.run(kernel)[0]
 
 
-def key_backward(ids, tokens, mine, got, key_weight, value_weight, owned_rows):
-    rows, width = tokens.shape
-    call = Call("key_backward", (1,))
-    call.scalars(ids)
-    for array in (tokens, mine, got):
-        call.whole(array)
-    call.weight(key_weight)
-    call.weight(value_weight)
-    call.out((rows, width), jnp.bfloat16)
-    half = Halves(call, 2, width // owned_rows, owned_rows, width)
-    call.flops = 8 * rows * width * width
-
-    def kernel(ids_ref, x_ref, mine_ref, got_ref, wk_ref, wv_ref, out_ref, *weights_refs):
-        values = x_ref[...]
-        dk = low(widen(mine_ref[0]) + widen(got_ref[0]))
-        dv = low(widen(mine_ref[1]) + widen(got_ref[1]))
-        half.store(weights_refs, 0, contract_rows(values, dk), ids_ref[5])
-        half.store(weights_refs, 1, contract_rows(values, dv), ids_ref[5])
-        out_ref[...] = low(
-            times_transpose(dk, load(wk_ref)) + times_transpose(dv, load(wv_ref))
-        )
-
-    results = call.run(kernel)
-    return results[0], half.pair(results[1:], ids[5])
-
-
 def flip(size, bit):
     return [(i, i ^ bit) for i in range(size)]
 
@@ -843,28 +955,6 @@
         else:
             self.held = widen(self.keep) + widen(got)
 
-    def spread(self):
-        steps, self.order = self.order, []
-        name = steps[0][0]
-        assert self.dims == sorted(steps, reverse=True) and self.got is not None
-        self.keep = self.total()
-        count = 1 << len(steps)
-        first = steps[0][1]
-        assert [bit for _, bit in steps] == list(range(first, first + len(steps)))
-        held = self.keep.reshape((count,) + self.keep.shape[-2:])
-        spot = (self.moves.spots[name] >> first) & (count - 1)
-        self.keep = lax.dynamic_index_in_dim(held, spot, 0, keepdims=False)
-        self.spreads = [
-            (i, lax.dynamic_index_in_dim(held, spot ^ i, 0, keepdims=False)) for i in range(1, count)
-        ]
-        size = self.moves.sizes[name]
-        self.gots = [lax.ppermute(v, name, flip(size, i << first)) for i, v in self.spreads]
-
-    def collect(self):
-        self.held = widen(self.keep)
-        for got in self.gots:
-            self.held = self.held + widen(got)
-
     def total(self):
         return low(widen(self.keep) + widen(self.got))
 
@@ -899,6 +989,18 @@
 def advance(chains, *values):
     values = receive(chains, *values)
     return depart(chains, *(values if isinstance(values, (list, tuple)) else (values,)))
+
+
+def line_sends(moves, totals, first):
+    count = totals.shape[0]
+    spot = moves.spots["dp"] >> first
+    keep = lax.dynamic_index_in_dim(totals, spot, 0, keepdims=False)
+    away = [
+        lax.dynamic_index_in_dim(totals, spot ^ i, 0, keepdims=False) for i in range(1, count)
+    ]
+    away = tie(*away)
+    size = moves.sizes["dp"]
+    return keep, [lax.ppermute(v, "dp", flip(size, i << first)) for i, v in enumerate(away, 1)]
 
 
 class Gather:
@@ -999,27 +1101,23 @@
     ]
     hidden_rows = outer_mat.shape[0]
     chunks = hidden_rows // owned_rows
-    tail = pack_vectors(vectors + [inner_bias], width)
+    first_part, second_part, feed = pack(
+        [self_query, self_key, self_value],
+        vectors + [inner_bias],
+        [self_out, cross_query],
+        outer_mat,
+        inner_mat,
+        [cross_key, cross_value, cross_out],
+    )
     moves = Moves()
     bits = moves.canonical
     dp_bits, hi, lo = bits[:-2], bits[-2], bits[-1]
     line, near = dp_bits[:-1], dp_bits[-1]
     cut = 2 * owned_rows
-    first_part = jnp.concatenate([self_query, self_key, self_value, tail], axis=0)
-    first_part, inner_mat, outer_mat, self_out, prompt_in, cont_in = tie(
-        first_part, inner_mat, outer_mat, self_out, prompt_in, cont_in
-    )
     one = Gather(moves, first_part, line)
     one.ship()
     prompt_got = swap_seq(pick(prompt_in, 1 - group), 3)
     sent = jnp.concatenate([pick(v, 1 - group) for v in (cont_in, enc_out)], axis=0)
-    feed = jnp.concatenate(
-        [outer_mat]
-        + [inner_mat[:, i * width : (i + 1) * width] for i in range(chunks)]
-        + [cross_key, cross_value, cross_out],
-        axis=0,
-    )
-    second_part = jnp.concatenate([self_out, cross_query], axis=0)
     feed = lax.all_gather(feed, ("dp", "seq"), axis=0, tiled=False)
     prompt_got, sent, second_part = pump([one], [one], prompt_got, sent, second_part)
     two = Gather(moves, second_part, line)
@@ -1046,6 +1144,7 @@
         [pick(prompt_in, group), prompt_got, pick(cont_in, group), got[:rows]], axis=0
     )
     encoder = jnp.concatenate([pick(enc_out, group), got[rows:]], axis=0)
+    enc_other = swap_seq(encoder, 1)
 
     def square(array, index):
         if owned_rows % 8 == 0:
@@ -1077,16 +1176,16 @@
     first_pre, first_low, cross_queries = self_finish(tokens, mixed, self_out, cross_query, vecs)
     cross_queries, cot_got, feed = tie(cross_queries, cot_got, feed)
     cross_key, cross_value, cross_out = [square(feed, 2 * chunks + i) for i in range(3)]
-    (cross_own,) = project(encoder, [cross_key, cross_value], vecs)
-    cross_other = swap_seq(cross_own, 1)
+    both = jnp.concatenate([encoder, enc_other], axis=0)
+    (cross_keys,) = project(both, [cross_key, cross_value], vecs)
     cross_mixed, cross_logsum, second_pre, second_low = cross_attend(
-        cross_queries, cross_own, cross_other, first_pre, cross_out, vecs
+        cross_queries, cross_keys, first_pre, cross_out, vecs
     )
     upstream = jnp.concatenate(
         [pick(prompt_cot, group), cot_got[:rows], pick(cont_cot, group), cot_got[rows:]], axis=0
     )
-    active, slope, third_pre, result = feed_forward(
-        second_pre, second_low, feed, vecs, chunks, owned_rows
+    slope, result, third_grad, third_low, sums, outer_pair = feed_forward(
+        ids, second_pre, second_low, upstream, feed, vecs, chunks, owned_rows
     )
 
     def send_back(own, *values):
@@ -1101,50 +1200,45 @@
             jnp.where(group == 0, jnp.stack([a, b]), jnp.stack([b, a])) for a, b in zip(kept, back)
         ]
 
-    result, result_back, third_pre = send_back(result, third_pre)
-
     bits = dp_bits[::-1]
     x_first = [lo, hi] + bits
     y_first = [lo, bits[0], hi] + bits[1:]
-    third_grad, third_low, sums, outer_pair = outer_backward(
-        ids, upstream, third_pre, active, vecs, chunks, owned_rows
-    )
-    third_low, result_back = tie(third_low, result_back)
-    prompt_out, cont_out = place(result, result_back)
     outer_chain = Scatter(moves, [outer_pair], x_first)
     third_low = depart([outer_chain], third_low)
+    result, result_back, third_low = send_back(result, third_low)
     second_grad, cross_mix, sums, inner_pair, cross_out_pair = inner_backward(
         ids, third_grad, third_low, sums, second_pre, second_low, slope, cross_mixed, feed, cross_out,
         vecs, chunks, owned_rows,
     )
+    cross_mix, result_back = tie(cross_mix, result_back)
+    prompt_out, cont_out = place(result, result_back)
     inner_chain = Scatter(moves, [inner_pair], y_first)
     feed_chains = [outer_chain, inner_chain]
     cross_mix = receive([outer_chain], cross_mix)
     cross_mix = depart([inner_chain], cross_mix)
     cross_mix = depart([outer_chain], cross_mix)
     cross_mix = advance([inner_chain], cross_mix)
-    own_back, other_back, first_grad, mix, sums, query_pair = cross_backward(
-        ids, cross_queries, cross_own, cross_other, cross_mixed, cross_mix, cross_logsum, first_low,
-        first_pre, second_grad, mixed, sums, cross_query, self_out, vecs, owned_rows,
-    )
-    mix, other_back = receive(feed_chains, mix, other_back)
-    got_back = swap_seq(other_back, 1)
-    enc_back, key_pair = key_backward(
-        ids, encoder, own_back, got_back, cross_key, cross_value, owned_rows
-    )
+    enc_part, first_grad, mix, sums, query_pair, key_pair = cross_backward(
+        ids, cross_queries, cross_keys, cross_mixed, cross_mix, cross_logsum, first_low, first_pre,
+        second_grad, mixed, sums, both, cross_query, self_out, cross_key, cross_value, vecs, owned_rows,
+    )
+    mix, enc_part = receive(feed_chains, mix, enc_part)
     cross_chains = [
-        Scatter(moves, [query_pair, cross_out_pair], x_first),
-        Scatter(moves, [key_pair], y_first),
+        Scatter(moves, [query_pair], x_first),
+        Scatter(moves, [key_pair, cross_out_pair], y_first),
     ]
+    enc_half = encoder.shape[0]
+    enc_there = swap_seq(enc_part[enc_half:], 1)
     enc_rows = enc_out.shape[1]
     mix = depart(cross_chains + feed_chains, mix)
+    halfway = HEADS // 4
+    one = self_backward(ids, queries, own, other, mixed, mix, logsum, 0, halfway)
+    tied = receive(cross_chains, enc_there, outer_chain.got, inner_chain.got, mix, *one)
+    enc_there, outer_chain.got, inner_chain.got, mix = tied[:4]
+    one = tied[4:]
+    enc_back = low(widen(enc_part[:enc_half]) + widen(enc_there))
     enc_sent, mix = tie(enc_back[enc_rows:], mix)
     enc_got = swap_seq(enc_sent, 3)
-    halfway = HEADS // 4
-    one = self_backward(ids, queries, own, other, mixed, mix, logsum, 0, halfway)
-    tied = receive(cross_chains, enc_got, outer_chain.got, inner_chain.got, mix, *one)
-    enc_got, outer_chain.got, inner_chain.got, mix = tied[:4]
-    one = tied[4:]
     rest = jnp.concatenate([c.total() for c in feed_chains], axis=-2)
     rest, mix = tie(rest, mix)
     rest = rest.reshape((-1,) + rest.shape[-2:])
@@ -1154,7 +1248,8 @@
     )[0]
     mix = depart(cross_chains, mix)
     two = self_backward(ids, queries, own, other, mixed, mix, logsum, halfway, HEADS // 2)
-    two = receive(cross_chains, *two)
+    tied = receive(cross_chains, enc_got, *two)
+    enc_got, two = tied[0], tied[1:]
     sent = [tie(h[2], *[c.away for c in cross_chains])[0] for h in (one, two)]
     got_one, got_two = [swap_seq(v, 1) for v in sent]
     part, sums, self_query_pair = query_backward(
@@ -1170,7 +1265,7 @@
         lax.dynamic_index_in_dim(sums, seq & 1, 1, keepdims=False),
         lax.dynamic_index_in_dim(sums, 1 - (seq & 1), 1, keepdims=False),
     )
-    query_chain = Scatter(moves, [self_query_pair, sums_pair], y_first)
+    query_chain = Scatter(moves, [self_query_pair, sums_pair], x_first)
     got_one = depart(cross_chains + [query_chain], got_one)
     total, key_pair, value_pair = key_weights(
         ids, tokens, (one[1], two[1]), (got_one, got_two), owned_rows
@@ -1181,22 +1276,25 @@
     total = depart(key_chains + [query_chain, cross_last], total)
     token_grad = token_backward(total, part, self_key, self_value)
     token_grad = receive(key_chains + [query_chain, cross_last], token_grad)
+    token_grad, token_back, key_chains[0].away = send_back(token_grad, key_chains[0].away)
     depart(key_chains + [query_chain, cross_last])
-    receive(key_chains + [query_chain])
+    token_back = receive(key_chains, token_back)
     depart(key_chains)
-    last_away = query_chain.away
-    receive(key_chains)
-    tail_chain = joined(key_chains)
-    tail_chain.order = list(tail_chain.order)
-    query_chain.away = last_away
-    tail_chain.keep = jnp.concatenate([tail_chain.keep, query_chain.keep], axis=-2)
-    tail_chain.away = jnp.concatenate([tail_chain.away, query_chain.away], axis=-2)
-    token_grad, token_back, tail_chain.away = send_back(token_grad, tail_chain.away)
-    tail_chain.ship()
-    token_back = receive([tail_chain], token_back)
-    while tail_chain.order:
-        tail_chain.ship()
-        receive([tail_chain])
+    totals = [query_chain.total()]
+    key_chains[0].got, key_chains[1].got, totals[0] = tie(
+        key_chains[0].got, key_chains[1].got, totals[0]
+    )
+    totals = jnp.concatenate([c.total() for c in key_chains] + totals, axis=-2)
+    totals = totals.reshape((-1,) + totals.shape[-2:])
+    if totals.shape[0] <= 4:
+        keep, gots = line_sends(moves, totals, 1)
+        tied = tie(*gots, cross_last.got)
+        gots, cross_last.got = tied[:-1], tied[-1]
+        tail_held = widen(keep) + sum(widen(g) for g in gots)
+    else:
+        tail_held = widen(
+            lax.psum_scatter(totals, "dp", scatter_dimension=0, axis_index_groups=lines, tiled=True)[0]
+        )
     while cross_last.got is not None:
         receive([cross_last])
         if cross_last.order:
@@ -1207,7 +1305,7 @@
         return [held[e - n : e] for e, n in zip(ends, sizes)]
 
     self_key_grad, self_value_grad, self_query_grad, vec = cut_rows(
-        tail_chain.held, [owned_rows, owned_rows, owned_rows, 8]
+        tail_held, [owned_rows, owned_rows, owned_rows, 8]
     )
     cross_held = cross_last.held.reshape(-1, owned_rows, width)
     vec = vec[0]
@@ -1243,10 +1341,10 @@
         vec_out[4],
         cross_held[0],
         vec_out[5],
+        cross_held[2],
         cross_held[3],
+        vec_out[6],
         cross_held[4],
-        vec_out[6],
-        cross_held[2],
         vec_out[7],
         vec_out[8],
         vec_out[9],

time: 391 us -> 369 us (0.944)
  Pallas kernels: 141 us -> 126 us
  local copies, waits for them, and re-layouts: 28.4 us -> 20.2 us
  waiting for transfers between devices: 107 us -> 112 us
    pallas_call x15 -> x13, Pallas kernels: 139 us -> 124 us  [run(): pl.pallas_call(kernel, grid=self.grid, in_specs=self.in_specs, out_specs=...]
    ppermute x0 -> x3, waiting for transfers between devices: none -> 8.04 us  [line_sends(): lax.ppermute(v, 'dp', flip(size, i << first))]
    unnamed x89 -> x80, local copies, waits for them, and re-layouts: 12.1 us -> 4.55 us
    ppermute x41 -> x39, waiting for transfers between devices: 89.1 us -> 84.4 us  [send(): lax.ppermute(flat, name, flip(self.sizes[name], 1 << bit))]
    ppermute x0 -> x3, starting transfers between devices: none -> 4.45 us  [line_sends(): lax.ppermute(v, 'dp', flip(size, i << first))]
    ppermute x41 -> x39, starting transfers between devices: 40.2 us -> 35.8 us  [send(): lax.ppermute(flat, name, flip(self.sizes[name], 1 << bit))]
    convert_element_type x30 -> x26, other arithmetic: 26.6 us -> 23.5 us  [low(): return values.astype(jnp.bfloat16)]
  transfers between devices with their start and end apart: 54 -> 55, of which waited for: 28 -> 32; matrix products, arithmetic and copies ran while one was open for 12% -> 11% of each run, Pallas kernels for 28% -> 26%
where the time goes in v3:
time: 369 us; the launch traced here: 363 us
  Pallas kernels  126 us (34%)
  waiting for transfers between devices  112 us (30%)
  starting transfers between devices  45 us (12%)
  other arithmetic  44.5 us (12%)
  local copies, waits for them, and re-layouts  20.2 us (5%)
  between operations  15.3 us (4%)
    pallas_call x13, Pallas kernels, run(): pl.pallas_call(kernel, grid=self.grid, in_specs=self.in_specs, out_specs=...  124 us
    ppermute x39, waiting for transfers between devices, send(): lax.ppermute(flat, name, flip(self.sizes[name], 1 << bit))  84.4 us
    ppermute x39, starting transfers between devices, send(): lax.ppermute(flat, name, flip(self.sizes[name], 1 << bit))  35.8 us
    convert_element_type x26, other arithmetic, low(): return values.astype(jnp.bfloat16)  23.5 us
    ppermute x11, waiting for transfers between devices, swap_seq(): return lax.ppermute(values, 'seq', flip(lax.axis_size('seq'), bits))  12.3 us
    ppermute x3, waiting for transfers between devices, line_sends(): lax.ppermute(v, 'dp', flip(size, i << first))  8.04 us
  transfers between devices with their start and end apart: 55, of which 32 were waited for; matrix products, arithmetic and copies ran while one was open for 11% of the time, Pallas kernels for 26%

profile of v3, /device:TPU:0, one launch (start us, length us, event | category | flops | bytes accessed | tf_op | source)
XLA Modules:
  0.0 363.0 jit_solution(12010598216026525708)
XLA Ops:
  7.3 2.1 pack.1
  9.6 2.4 collective-permute-start.1
  12.0 2.6 collective-permute-start
  15.4 6.1 %collective-permute-done = bf16[80,768]{1,0:T(8,128)(2,1)S(1)} collective-permute-done((bf16[80,768]{1,0:T(8,128)(2,1)S(1)}, bf16[80,768]{1,0:T(8,128)(2,1)S(1)}, u32[]{:S(2)}, u32[]{:S(2)}) %collective-permute-start) | collective-permute-done | bytes 122912 | tf_op jit(solution)/shard_map/ppermute | solution.py:916
  22.8 13.2 %collective-permute-done.2 = bf16[160,768]{1,0:T(8,128)(2,1)S(1)} collective-permute-done((bf16[160,768]{1,0:T(8,128)(2,1)S(1)}, bf16[160,768]{1,0:T(8,128)(2,1)S(1)}, u32[]{:S(2)}, u32[]{:S(2)}) %collective-permute-start.2) | collective-permute-done | bytes 245792 | tf_op jit(solution)/shard_map/ppermute | solution.py:916
  36.8 2.0 collective-permute-start.4
  40.3 2.1 collective-permute-start.6
  42.4 4.7 %collective-permute-done.6 = bf16[48,768]{1,0:T(8,128)(2,1)S(1)} collective-permute-done((bf16[48,768]{1,0:T(8,128)(2,1)S(1)}, bf16[48,768]{1,0:T(8,128)(2,1)S(1)}, u32[]{:S(2)}, u32[]{:S(2)}) %collective-permute-start.6) | collective-permute-done | bytes 73760 | tf_op jit(solution)/shard_map/ppermute | solution.py:916
  48.9 10.8 %collective-permute-done.9 = bf16[96,768]{1,0:T(8,128)(2,1)S(1)} collective-permute-done((bf16[96,768]{1,0:T(8,128)(2,1)S(1)}, bf16[96,768]{1,0:T(8,128)(2,1)S(1)}, u32[]{:S(2)}, u32[]{:S(2)}) %collective-permute-start.9) | collective-permute-done | bytes 147488 | tf_op jit(solution)/shard_map/ppermute | solution.py:916
  59.8 2.3 collective-permute-done.8
  62.1 8.9 %collective-permute-done.7 = bf16[384,768]{1,0:T(8,128)(2,1)S(1)} collective-permute-done((bf16[384,768]{1,0:T(8,128)(2,1)S(1)}, bf16[384,768]{1,0:T(8,128)(2,1)S(1)}, u32[]{:S(2)}, u32[]{:S(2)}) %collective-permute-start.7) | collective-permute-done | bytes 589856 | tf_op jit(solution)/shard_map/ppermute | solution.py:916
  86.3 5.4 %project.2 = (bf16[512,768]{1,0:T(8,128)(2,1)}, bf16[2,512,768]{2,1,0:T(8,128)(2,1)}) custom-call(bf16[512,768]{1,0:T(8,128)(2,1)} %pad_maximum_fusion.4.refs_0_.x_ref, bf16[32,48,768]{2,1,0:T(8,128)(2,1)} %bitcast.418, bf16[32,48,768]{2,1,0:T(8,128)(2,1)} %bitcast.419, bf16[32,32,768]{2,1,0:T(8,128)(2,1)} %bitcast.424, ...), custom_call_target="tpu_custom_call" | custom-call | flops 1811939328 | bytes 6736896 | tf_op jit(solution)/shard_map/project/pallas_call | solution.py:213
  95.1 2.2 collective-permute-start.14
  97.3 12.4 %self_attend.1 = (bf16[512,768]{1,0:T(8,128)(2,1)}, f32[6,2,512]{2,1,0:T(2,128)}) custom-call(s32[6]{0:T(128)} %stack.237.ids_ref.refs_0_, bf16[512,768]{1,0:T(8,128)(2,1)} %get-tuple-element.273.q_ref, bf16[2,512,768]{2,1,0:T(8,128)(2,1)} %get-tuple-element.274.own_ref, bf16[2,512,768]{2,1,0:T(8,128)(2,1)} %collective-permute-done.16.other_ref), custom_call_target="tpu_custom_call" | custom-call | flops 3221225472 | bytes 4743168 | tf_op jit(solution)/shard_map/self_attend/pallas_call | solution.py:213
  114.6 2.1 collective-permute-done.20
  120.1 5.2 %self_finish.1 = (f32[512,768]{1,0:T(8,128)}, bf16[512,768]{1,0:T(8,128)(2,1)}, bf16[512,768]{1,0:T(8,128)(2,1)}) custom-call(bf16[512,768]{1,0:T(8,128)(2,1)} %pad_maximum_fusion.4.refs_0_.x_ref, bf16[512,768]{1,0:T(8,128)(2,1)} %get-tuple-element.283.mixed_ref.refs_9_, bf16[32,24,768]{2,1,0:T(8,128)(2,1)} %bitcast.428, bf16[32,24,768]{2,1,0:T(8,128)(2,1)} %bitcast.426, ...), custom_call_target="tpu_custom_call" | custom-call | flops 1207959552 | bytes 7130112 | tf_op jit(solution)/shard_map/self_finish/pallas_call | solution.py:213
  125.2 3.3 collective-permute-done.19
  128.5 7.0 %all-gather.3.cloned.1.call-done = bf16[8448,768]{1,0:T(8,128)(2,1)} async-done(((bf16[264,768]{1,0:T(8,128)(2,1)}), bf16[8448,768]{1,0:T(8,128)(2,1)}) %all-gather.3.cloned.1.call-update) | async-done | bytes 12976144 | tf_op jit(solution)/shard_map/all_gather | solution.py:1121
  135.5 3.5 project.3.refs_1_.refs_5_
  139.0 10.0 %cross_attend.1 = (bf16[512,768]{1,0:T(8,128)(2,1)}, f32[6,2,512]{2,1,0:T(2,128)}, f32[512,768]{1,0:T(8,128)}, bf16[512,768]{1,0:T(8,128)(2,1)}) custom-call(bf16[512,768]{1,0:T(8,128)(2,1)} %get-tuple-element.289.refs_0_.refs_1_, bf16[2,256,768]{2,1,0:T(8,128)(2,1)} %project.3.refs_1_.refs_5_, f32[512,768]{1,0:T(8,128)} %get-tuple-element.291.refs_2_.refs_7_, ...), custom_call_target="tpu_custom_call" | custom-call | flops 1409286144 | bytes 19344384 | tf_op jit(solution)/shard_map/cross_attend/pallas_call | solution.py:213
  149.9 17.9 %feed_forward.1 = (bf16[512,3072]{1,0:T(8,128)(2,1)}, bf16[512,768]{1,0:T(8,128)(2,1)}, f32[512,768]{1,0:T(8,128)}, bf16[512,768]{1,0:T(8,128)(2,1)}, f32[24,768...) custom-call(s32[6]{0:T(128)} %stack.237.ids_ref.refs_0_, ...), custom_call_target="tpu_custom_call" | custom-call | flops 7247757312 | bytes 40233984 | tf_op jit(solution)/shard_map/feed_forward/pallas_call | solution.py:213
  168.1 2.0 slice_bitcast_fusion.7
  171.5 16.9 %inner_backward.1 = (f32[512,768]{1,0:T(8,128)}, bf16[512,768]{1,0:T(8,128)(2,1)}, f32[24,768]{1,0:T(8,128)}, bf16[16,4,24,768]{3,2,1,0:T(8,128)(2,1)}, bf16[16,...) custom-call(s32[6]{0:T(128)} %stack.237.ids_ref.refs_0_, ...), custom_call_target="tpu_custom_call" | custom-call | flops 8455716864 | bytes 56036352 | tf_op jit(solution)/shard_map/inner_backward/pallas_call | solution.py:213
  188.8 3.5 add_convert_fusion.1
  193.4 2.6 fusion.1
  196.7 17.1 %cross_backward.1 = (bf16[256,768]{1,0:T(8,128)(2,1)}, f32[512,768]{1,0:T(8,128)}, bf16[512,768]{1,0:T(8,128)(2,1)}, f32[24,768]{1,0:T(8,128)}, bf16[16,2,24,768...) custom-call(s32[6]{0:T(128)} %stack.237.ids_ref.refs_0_, ...), custom_call_target="tpu_custom_call" | custom-call | flops 5637144576 | bytes 44264448 | tf_op jit(solution)/shard_map/cross_backward/pallas_call | solution.py:213
  213.8 2.8 pad_maximum_fusion
  218.2 2.4 collective-permute-done.24
  220.6 3.9 %collective-permute-done.25 = bf16[768,768]{1,0:T(8,128)(2,1)} collective-permute-done((bf16[768,768]{1,0:T(8,128)(2,1)}, bf16[768,768]{1,0:T(8,128)(2,1)}, u32[]{:S(2)}, u32[]{:S(2)}) %collective-permute-start.25) | collective-permute-done | bytes 1179680 | tf_op jit(solution)/shard_map/ppermute | solution.py:916
  224.5 2.0 fusion.15
  230.3 10.5 %self_backward.2 = (bf16[512,384]{1,0:T(8,128)(2,1)}, bf16[2,512,384]{2,1,0:T(8,128)(2,1)}, bf16[2,512,384]{2,1,0:T(8,128)(2,1)}, f32[8,384]{1,0:T(8,128)}) custom-call(s32[6]{0:T(128)} %stack.237.ids_ref.refs_0_, bf16[512,768]{1,0:T(8,128)(2,1)} %get-tuple-element.273.q_ref, bf16[512,768]{1,0:T(8,128)(2,1)} %get-tuple-element.283.mixed_ref.refs_9_, ...), custom_call_target="tpu_custom_call" | custom-call | flops 4026531840 | bytes 7507968 | tf_op jit(solution)/shard_map/self_backward/pallas_call | solution.py:213
  240.9 2.7 collective-permute-done.29
  250.0 2.5 add_convert_fusion.6
  252.5 1.9 add_convert_fusion.4
  256.7 10.3 %self_backward.3 = (bf16[512,384]{1,0:T(8,128)(2,1)}, bf16[2,512,384]{2,1,0:T(8,128)(2,1)}, bf16[2,512,384]{2,1,0:T(8,128)(2,1)}, f32[8,384]{1,0:T(8,128)}) custom-call(s32[6]{0:T(128)} %stack.237.ids_ref.refs_0_, bf16[512,768]{1,0:T(8,128)(2,1)} %get-tuple-element.273.q_ref, bf16[512,768]{1,0:T(8,128)(2,1)} %get-tuple-element.283.mixed_ref.refs_9_, ...), custom_call_target="tpu_custom_call" | custom-call | flops 4026531840 | bytes 7507968 | tf_op jit(solution)/shard_map/self_backward/pallas_call | solution.py:213
  267.0 3.2 collective-permute-done.33
  271.1 3.8 %collective-permute-done.32 = bf16[576,768]{1,0:T(8,128)(2,1)S(1)} collective-permute-done((bf16[576,768]{1,0:T(8,128)(2,1)S(1)}, bf16[576,768]{1,0:T(8,128)(2,1)S(1)}, u32[]{:S(2)}, u32[]{:S(2)}) %collective-permute-start.32) | collective-permute-done | bytes 884768 | tf_op jit(solution)/shard_map/ppermute | solution.py:916
  277.0 5.1 %query_backward.1 = (f32[512,768]{1,0:T(8,128)}, f32[24,768]{1,0:T(8,128)}, bf16[16,1,24,768]{3,2,1,0:T(8,128)(2,1)}, bf16[16,1,24,768]{3,2,1,0:T(8,128)(2,1)}) custom-call(s32[6]{0:T(128)} %stack.237.ids_ref.refs_0_, bf16[512,768]{1,0:T(8,128)(2,1)} %pad_maximum_fusion.4.refs_0_.x_ref, f32[512,768]{1,0:T(8,128)} %get-tuple-element.368.grad_ref, ...), custom_call_target="tpu_custom_call" | custom-call | flops 1207959552 | bytes 7249920 | tf_op jit(solution)/shard_map/query_backward/pallas_call | solution.py:213
  289.5 5.1 %key_weights.1 = (bf16[2,512,768]{2,1,0:T(8,128)(2,1)}, bf16[16,1,24,768]{3,2,1,0:T(8,128)(2,1)}, bf16[16,1,24,768]{3,2,1,0:T(8,128)(2,1)}, bf16[16,1,24,768]{3,2,1,0:T(8,128)(2,1)}, bf16[16,1,24,768]{3,2,1,0:T(8,128)(2,1)}) custom-call(s32[6]{0:T(128)} %stack.237.ids_ref.refs_0_, bf16[512,768]{1,0:T(8,128)(2,1)} %pad_maximum_fusion.4.refs_0_.x_ref, ...), custom_call_target="tpu_custom_call" | custom-call | flops 1207959552 | bytes 7864320 | tf_op jit(solution)/shard_map/key_weights/pallas_call | solution.py:213
  295.6 2.1 collective-permute-done.36
  306.7 4.9 %token_backward.1 = bf16[512,768]{1,0:T(8,128)(2,1)} custom-call(bf16[2,512,768]{2,1,0:T(8,128)(2,1)} %get-tuple-element.399.total_ref, f32[512,768]{1,0:T(8,128)} %get-tuple-element.400.part_ref, bf16[32,48,768]{2,1,0:T(8,128)(2,1)} %bitcast.421, bf16[32,32,768]{2,1,0:T(8,128)(2,1)} %bitcast.425), custom_call_target="tpu_custom_call" | custom-call | flops 1207959552 | bytes 6291456 | tf_op jit(solution)/shard_map/token_backward/pallas_call | solution.py:213
  311.6 2.2 collective-permute-done.42
  318.5 2.4 collective-permute-start.52
  320.9 2.3 collective-permute-done.48
  323.3 3.2 collective-permute-done.43
  327.5 3.8 %collective-permute-done.45 = bf16[256,768]{1,0:T(8,128)(2,1)S(1)} collective-permute-done((bf16[256,768]{1,0:T(8,128)(2,1)S(1)}, bf16[256,768]{1,0:T(8,128)(2,1)S(1)}, u32[]{:S(2)}, u32[]{:S(2)}) %collective-permute-start.45) | collective-permute-done | bytes 393248 | tf_op jit(solution)/shard_map/ppermute | solution.py:891
  333.2 4.6 %collective-permute-done.46 = bf16[96,768]{1,0:T(8,128)(2,1)S(1)} collective-permute-done((bf16[96,768]{1,0:T(8,128)(2,1)S(1)}, bf16[96,768]{1,0:T(8,128)(2,1)S(1)}, u32[]{:S(2)}, u32[]{:S(2)}) %collective-permute-start.46) | collective-permute-done | bytes 147488 | tf_op jit(solution)/shard_map/ppermute | solution.py:916
  346.1 7.1 %collective-permute-done.50 = bf16[80,768]{1,0:T(8,128)(2,1)S(1)} collective-permute-done((bf16[80,768]{1,0:T(8,128)(2,1)S(1)}, bf16[80,768]{1,0:T(8,128)(2,1)S(1)}, u32[]{:S(2)}, u32[]{:S(2)}) %collective-permute-start.50) | collective-permute-done | bytes 122912 | tf_op jit(solution)/shard_map/ppermute | solution.py:1003
  (280 shorter events, 90.7 us)
Async XLA Ops:
  7.2 128.3 %all-gather.3.cloned.1.call-start = ((), (), s32[]{:S(2)}) async-start(), calls=%async_computation.2 | async-start | bytes 13381632 | tf_op jit(solution)/shard_map/all_gather | solution.py:1121
  9.5 285.1 %reduce-scatter.2.cloned.1.call-start = ((), (), s32[]{:S(2)}) async-start(), calls=%async_computation.1 | async-start | bytes 1474560 | tf_op jit(solution)/shard_map/reduce_scatter | solution.py:1246
  9.6 11.9 %collective-permute-start.1 = (bf16[128,768]{1,0:T(8,128)(2,1)S(1)}, bf16[128,768]{1,0:T(8,128)(2,1)S(1)}, u32[]{:S(2)}, u32[]{:S(2)}) collective-permute-start(bf16[128,768]{1,0:T(8,128)(2,1)S(1)} %get-tuple-element.495), channel_id=1, source_target_pairs={{0,3},{1,2},{2,1},{3,0},{4,7},{5,6},{6,5},{7,4},{8,11},{9,10},{10,... | collective-permute-start | bytes 589832 | tf_op jit(solution)/shard_map/ppermute | solution.py:891
  12.0 9.4 %collective-permute-start = (bf16[80,768]{1,0:T(8,128)(2,1)S(1)}, bf16[80,768]{1,0:T(8,128)(2,1)S(1)}, u32[]{:S(2)}, u32[]{:S(2)}) collective-permute-start(bf16[80,768]{1,0:T(8,128)(2,1)S(1)} %copy-done.32), channel_id=1, source_target_pairs={{0,16},{4,20},{8,24},{12,28},{16,0},{20,4},{24,8},{28,12},{1,17},{... | collective-permute-start | bytes 368648 | tf_op jit(solution)/shard_map/ppermute | solution.py:916
  21.5 14.5 %collective-permute-start.3 = (bf16[192,768]{1,0:T(8,128)(2,1)S(1)}, bf16[192,768]{1,0:T(8,128)(2,1)S(1)}, u32[]{:S(2)}, u32[]{:S(2)}) collective-permute-start(bf16[192,768]{1,0:T(8,128)(2,1)S(1)} %pad_maximum_fusion.17), channel_id=1, source_target_pairs={{0,3},{1,2},{2,1},{3,0},{4,7},{5,6},{6,5},{7,4},{8,11},{9,10},{10,... | collective-permute-start | bytes 884744 | tf_op jit(solution)/shard_map/ppermute | solution.py:891
  22.1 13.9 %collective-permute-start.2 = (bf16[160,768]{1,0:T(8,128)(2,1)S(1)}, bf16[160,768]{1,0:T(8,128)(2,1)S(1)}, u32[]{:S(2)}, u32[]{:S(2)}) collective-permute-start(bf16[160,768]{1,0:T(8,128)(2,1)S(1)} %bitcast.452), channel_id=1, source_target_pairs={{0,8},{4,12},{8,0},{12,4},{16,24},{20,28},{24,16},{28,20},{1,9},{5... | collective-permute-start | bytes 737288 | tf_op jit(solution)/shard_map/ppermute | solution.py:916
  36.8 10.3 %collective-permute-start.4 = (bf16[192,768]{1,0:T(8,128)(2,1)S(1)}, bf16[192,768]{1,0:T(8,128)(2,1)S(1)}, u32[]{:S(2)}, u32[]{:S(2)}) collective-permute-start(bf16[192,768]{1,0:T(8,128)(2,1)S(1)} %bitcast.447), channel_id=1, source_target_pairs={{0,4},{4,0},{8,12},{12,8},{16,20},{20,16},{24,28},{28,24},{1,5},{5... | collective-permute-start | bytes 884744 | tf_op jit(solution)/shard_map/ppermute | solution.py:916
  38.8 8.3 %collective-permute-start.5 = (bf16[128,768]{1,0:T(8,128)(2,1)S(1)}, bf16[128,768]{1,0:T(8,128)(2,1)S(1)}, u32[]{:S(2)}, u32[]{:S(2)}) collective-permute-start(bf16[128,768]{1,0:T(8,128)(2,1)S(1)} %bitcast.459), channel_id=1, source_target_pairs={{0,2},{1,3},{2,0},{3,1},{4,6},{5,7},{6,4},{7,5},{8,10},{9,11},{10,... | collective-permute-start | bytes 589832 | tf_op jit(solution)/shard_map/ppermute | solution.py:916
  40.3 6.8 %collective-permute-start.6 = (bf16[48,768]{1,0:T(8,128)(2,1)S(1)}, bf16[48,768]{1,0:T(8,128)(2,1)S(1)}, u32[]{:S(2)}, u32[]{:S(2)}) collective-permute-start(bf16[48,768]{1,0:T(8,128)(2,1)S(1)} %copy-done.36), channel_id=1, source_target_pairs={{0,16},{4,20},{8,24},{12,28},{16,0},{20,4},{24,8},{28,12},{1,17},{... | collective-permute-start | bytes 221192 | tf_op jit(solution)/shard_map/ppermute | solution.py:916
  47.4 23.6 %collective-permute-start.7 = (bf16[384,768]{1,0:T(8,128)(2,1)S(1)}, bf16[384,768]{1,0:T(8,128)(2,1)S(1)}, u32[]{:S(2)}, u32[]{:S(2)}) collective-permute-start(bf16[384,768]{1,0:T(8,128)(2,1)S(1)} %bitcast.435), channel_id=1, source_target_pairs={{0,2},{1,3},{2,0},{3,1},{4,6},{5,7},{6,4},{7,5},{8,10},{9,11},{10,... | collective-permute-start | bytes 1769480 | tf_op jit(solution)/shard_map/ppermute | solution.py:916
  48.0 14.1 %collective-permute-start.8 = (bf16[256,768]{1,0:T(8,128)(2,1)S(1)}, bf16[256,768]{1,0:T(8,128)(2,1)S(1)}, u32[]{:S(2)}, u32[]{:S(2)}) collective-permute-start(bf16[256,768]{1,0:T(8,128)(2,1)S(1)} %bitcast.442), channel_id=1, source_target_pairs={{0,4},{4,0},{8,12},{12,8},{16,20},{20,16},{24,28},{28,24},{1,5},{5... | collective-permute-start | bytes 1179656 | tf_op jit(solution)/shard_map/ppermute | solution.py:916
  48.9 10.8 %collective-permute-start.9 = (bf16[96,768]{1,0:T(8,128)(2,1)S(1)}, bf16[96,768]{1,0:T(8,128)(2,1)S(1)}, u32[]{:S(2)}, u32[]{:S(2)}) collective-permute-start(bf16[96,768]{1,0:T(8,128)(2,1)S(1)} %bitcast.473), channel_id=1, source_target_pairs={{0,8},{4,12},{8,0},{12,4},{16,24},{20,28},{24,16},{28,20},{1,9},{5... | collective-permute-start | bytes 442376 | tf_op jit(solution)/shard_map/ppermute | solution.py:916
  81.4 10.3 %collective-permute-start.12 = (bf16[96,768]{1,0:T(8,128)(2,1)S(1)}, bf16[96,768]{1,0:T(8,128)(2,1)S(1)}, u32[]{:S(2)}, u32[]{:S(2)}) collective-permute-start(bf16[96,768]{1,0:T(8,128)(2,1)S(1)} %bitcast.477), channel_id=1, source_target_pairs={{0,4},{4,0},{8,12},{12,8},{16,20},{20,16},{24,28},{28,24},{1,5},{5... | collective-permute-start | bytes 442376 | tf_op jit(solution)/shard_map/ppermute | solution.py:916
  83.0 8.9 %collective-permute-start.13 = (bf16[96,768]{1,0:T(8,128)(2,1)S(1)}, bf16[96,768]{1,0:T(8,128)(2,1)S(1)}, u32[]{:S(2)}, u32[]{:S(2)}) collective-permute-start(bf16[96,768]{1,0:T(8,128)(2,1)S(1)} %bitcast.476), channel_id=1, source_target_pairs={{0,2},{1,3},{2,0},{3,1},{4,6},{5,7},{6,4},{7,5},{8,10},{9,11},{10,... | collective-permute-start | bytes 442376 | tf_op jit(solution)/shard_map/ppermute | solution.py:916
  95.1 16.2 %collective-permute-start.14 = (bf16[192,768]{1,0:T(8,128)(2,1)S(1)}, bf16[192,768]{1,0:T(8,128)(2,1)S(1)}, u32[]{:S(2)}, u32[]{:S(2)}) collective-permute-start(bf16[192,768]{1,0:T(8,128)(2,1)S(1)} %bitcast.448), channel_id=1, source_target_pairs={{0,2},{1,3},{2,0},{3,1},{4,6},{5,7},{6,4},{7,5},{8,10},{9,11},{10,... | collective-permute-start | bytes 884744 | tf_op jit(solution)/shard_map/ppermute | solution.py:916
  97.3 15.9 %collective-permute-start.15 = (bf16[192,768]{1,0:T(8,128)(2,1)S(1)}, bf16[192,768]{1,0:T(8,128)(2,1)S(1)}, u32[]{:S(2)}, u32[]{:S(2)}) collective-permute-start(bf16[192,768]{1,0:T(8,128)(2,1)S(1)} %bitcast.449), channel_id=1, source_target_pairs={{0,4},{4,0},{8,12},{12,8},{16,20},{20,16},{24,28},{28,24},{1,5},{5... | collective-permute-start | bytes 884744 | tf_op jit(solution)/shard_map/ppermute | solution.py:916
  117.4 11.1 %collective-permute-start.19 = (bf16[256,768]{1,0:T(8,128)(2,1)S(1)}, bf16[256,768]{1,0:T(8,128)(2,1)S(1)}, u32[]{:S(2)}, u32[]{:S(2)}) collective-permute-start(bf16[256,768]{1,0:T(8,128)(2,1)S(1)} %pad_maximum_fusion.12), channel_id=1, source_target_pairs={{0,3},{1,2},{2,1},{3,0},{4,7},{5,6},{6,5},{7,4},{8,11},{9,10},{10,... | collective-permute-start | bytes 1179656 | tf_op jit(solution)/shard_map/ppermute | solution.py:891
  167.8 20.6 %collective-permute-start.22 = (bf16[1536,768]{1,0:T(8,128)(2,1)}, bf16[1536,768]{1,0:T(8,128)(2,1)}, u32[]{:S(2)}, u32[]{:S(2)}) collective-permute-start(bf16[1536,768]{1,0:T(8,128)(2,1)} %bitcast.527), channel_id=1, source_target_pairs={{0,1},{1,0},{2,3},{3,2},{4,5},{5,4},{6,7},{7,6},{8,9},{9,8},{10,11... | collective-permute-start | bytes 7077896 | tf_op jit(solution)/shard_map/ppermute | solution.py:916
  170.2 18.3 %collective-permute-start.21 = (bf16[256,768]{1,0:T(8,128)(2,1)S(1)}, bf16[256,768]{1,0:T(8,128)(2,1)}, u32[]{:S(2)}, u32[]{:S(2)}) collective-permute-start(bf16[256,768]{1,0:T(8,128)(2,1)S(1)} %pad_maximum_fusion.14), channel_id=1, source_target_pairs={{0,3},{1,2},{2,1},{3,0},{4,7},{5,6},{6,5},{7,4},{8,11},{9,10},{10,... | collective-permute-start | bytes 1179656 | tf_op jit(solution)/shard_map/ppermute | solution.py:891
  192.3 28.3 %collective-permute-start.24 = (bf16[768,768]{1,0:T(8,128)(2,1)}, bf16[768,768]{1,0:T(8,128)(2,1)S(1)}, u32[]{:S(2)}, u32[]{:S(2)}) collective-permute-start(bf16[768,768]{1,0:T(8,128)(2,1)} %bitcast.118), channel_id=1, source_target_pairs={{0,2},{1,3},{2,0},{3,1},{4,6},{5,7},{6,4},{7,5},{8,10},{9,11},{10,... | collective-permute-start | bytes 3538952 | tf_op jit(solution)/shard_map/ppermute | solution.py:916
  196.0 28.4 %collective-permute-start.25 = (bf16[768,768]{1,0:T(8,128)(2,1)}, bf16[768,768]{1,0:T(8,128)(2,1)}, u32[]{:S(2)}, u32[]{:S(2)}) collective-permute-start(bf16[768,768]{1,0:T(8,128)(2,1)} %bitcast.120), channel_id=1, source_target_pairs={{0,4},{4,0},{8,12},{12,8},{16,20},{20,16},{24,28},{28,24},{1,5},{5... | collective-permute-start | bytes 3538952 | tf_op jit(solution)/shard_map/ppermute | solution.py:916
  227.5 16.4 %collective-permute-start.27 = (bf16[1152,768]{1,0:T(8,128)(2,1)}, bf16[1152,768]{1,0:T(8,128)(2,1)}, u32[]{:S(2)}, u32[]{:S(2)}) collective-permute-start(bf16[1152,768]{1,0:T(8,128)(2,1)} %bitcast.127), channel_id=1, source_target_pairs={{0,1},{1,0},{2,3},{3,2},{4,5},{5,4},{6,7},{7,6},{8,9},{9,8},{10,11... | collective-permute-start | bytes 5308424 | tf_op jit(solution)/shard_map/ppermute | solution.py:916
  227.5 16.4 %collective-permute-start.26 = (bf16[768,768]{1,0:T(8,128)(2,1)}, bf16[768,768]{1,0:T(8,128)(2,1)}, u32[]{:S(2)}, u32[]{:S(2)}) collective-permute-start(bf16[768,768]{1,0:T(8,128)(2,1)} %bitcast.125), channel_id=1, source_target_pairs={{0,1},{1,0},{2,3},{3,2},{4,5},{5,4},{6,7},{7,6},{8,9},{9,8},{10,11... | collective-permute-start | bytes 3538952 | tf_op jit(solution)/shard_map/ppermute | solution.py:916
  228.0 15.6 %collective-permute-start.29 = (bf16[384,768]{1,0:T(8,128)(2,1)}, bf16[384,768]{1,0:T(8,128)(2,1)}, u32[]{:S(2)}, u32[]{:S(2)}) collective-permute-start(bf16[384,768]{1,0:T(8,128)(2,1)} %bitcast.129), channel_id=1, source_target_pairs={{0,4},{4,0},{8,12},{12,8},{16,20},{20,16},{24,28},{28,24},{1,5},{5... | collective-permute-start | bytes 1769480 | tf_op jit(solution)/shard_map/ppermute | solution.py:916
  228.6 15.3 %collective-permute-start.30 = (bf16[384,768]{1,0:T(8,128)(2,1)}, bf16[384,768]{1,0:T(8,128)(2,1)}, u32[]{:S(2)}, u32[]{:S(2)}) collective-permute-start(bf16[384,768]{1,0:T(8,128)(2,1)} %bitcast.131), channel_id=1, source_target_pairs={{0,2},{1,3},{2,0},{3,1},{4,6},{5,7},{6,4},{7,5},{8,10},{9,11},{10,... | collective-permute-start | bytes 1769480 | tf_op jit(solution)/shard_map/ppermute | solution.py:916
  230.3 10.6 %collective-permute-start.28 = (bf16[128,768]{1,0:T(8,128)(2,1)}, bf16[128,768]{1,0:T(8,128)(2,1)}, u32[]{:S(2)}, u32[]{:S(2)}) collective-permute-start(bf16[128,768]{1,0:T(8,128)(2,1)} %slice.272), channel_id=1, source_target_pairs={{0,1},{1,0},{2,3},{3,2},{4,5},{5,4},{6,7},{7,6},{8,9},{9,8},{10,11... | collective-permute-start | bytes 589832 | tf_op jit(solution)/shard_map/ppermute | solution.py:891
  254.5 20.4 %collective-permute-start.32 = (bf16[576,768]{1,0:T(8,128)(2,1)S(1)}, bf16[576,768]{1,0:T(8,128)(2,1)S(1)}, u32[]{:S(2)}, u32[]{:S(2)}) collective-permute-start(bf16[576,768]{1,0:T(8,128)(2,1)S(1)} %bitcast.454), channel_id=1, source_target_pairs={{0,4},{4,0},{8,12},{12,8},{16,20},{20,16},{24,28},{28,24},{1,5},{5... | collective-permute-start | bytes 2654216 | tf_op jit(solution)/shard_map/ppermute | solution.py:916
  255.9 15.2 %collective-permute-start.31 = (bf16[384,768]{1,0:T(8,128)(2,1)}, bf16[384,768]{1,0:T(8,128)(2,1)}, u32[]{:S(2)}, u32[]{:S(2)}) collective-permute-start(bf16[384,768]{1,0:T(8,128)(2,1)} %bitcast.142), channel_id=1, source_target_pairs={{0,2},{1,3},{2,0},{3,1},{4,6},{5,7},{6,4},{7,5},{8,10},{9,11},{10,... | collective-permute-start | bytes 1769480 | tf_op jit(solution)/shard_map/ppermute | solution.py:916
  256.6 13.6 %collective-permute-start.33 = (bf16[64,768]{1,0:T(8,128)(2,1)S(1)}, bf16[64,768]{1,0:T(8,128)(2,1)S(1)}, u32[]{:S(2)}, u32[]{:S(2)}) collective-permute-start(bf16[64,768]{1,0:T(8,128)(2,1)S(1)} %copy-done.35), channel_id=1, source_target_pairs={{0,3},{1,2},{2,1},{3,0},{4,7},{5,6},{6,5},{7,4},{8,11},{9,10},{10,... | collective-permute-start | bytes 294920 | tf_op jit(solution)/shard_map/ppermute | solution.py:891
  276.4 7.6 %collective-permute-start.35 = (bf16[2,512,384]{2,1,0:T(8,128)(2,1)}, bf16[2,512,384]{2,1,0:T(8,128)(2,1)}, u32[]{:S(2)}, u32[]{:S(2)}) collective-permute-start(bf16[2,512,384]{2,1,0:T(8,128)(2,1)} %get-tuple-element.379), channel_id=1, source_target_pairs={{0,1},{1,0},{2,3},{3,2},{4,5},{5,4},{6,7},{7,6},{8,9},{9,8},{10,11... | collective-permute-start | bytes 2359304 | tf_op jit(solution)/shard_map/ppermute | solution.py:891
  276.5 7.5 %collective-permute-start.34 = (bf16[2,512,384]{2,1,0:T(8,128)(2,1)}, bf16[2,512,384]{2,1,0:T(8,128)(2,1)}, u32[]{:S(2)}, u32[]{:S(2)}) collective-permute-start(bf16[2,512,384]{2,1,0:T(8,128)(2,1)} %get-tuple-element.377), channel_id=1, source_target_pairs={{0,1},{1,0},{2,3},{3,2},{4,5},{5,4},{6,7},{7,6},{8,9},{9,8},{10,11... | collective-permute-start | bytes 2359304 | tf_op jit(solution)/shard_map/ppermute | solution.py:891
  284.0 15.4 %collective-permute-start.38 = (bf16[512,768]{1,0:T(8,128)(2,1)S(1)}, bf16[512,768]{1,0:T(8,128)(2,1)S(1)}, u32[]{:S(2)}, u32[]{:S(2)}) collective-permute-start(bf16[512,768]{1,0:T(8,128)(2,1)S(1)} %bitcast.455), channel_id=1, source_target_pairs={{0,1},{1,0},{2,3},{3,2},{4,5},{5,4},{6,7},{7,6},{8,9},{9,8},{10,11... | collective-permute-start | bytes 2359304 | tf_op jit(solution)/shard_map/ppermute | solution.py:916
  286.8 12.6 %collective-permute-start.37 = (bf16[288,768]{1,0:T(8,128)(2,1)S(1)}, bf16[288,768]{1,0:T(8,128)(2,1)}, u32[]{:S(2)}, u32[]{:S(2)}) collective-permute-start(bf16[288,768]{1,0:T(8,128)(2,1)S(1)} %bitcast.479), channel_id=1, source_target_pairs={{0,2},{1,3},{2,0},{3,1},{4,6},{5,7},{6,4},{7,5},{8,10},{9,11},{10,... | collective-permute-start | bytes 1327112 | tf_op jit(solution)/shard_map/ppermute | solution.py:916
  288.5 9.2 %collective-permute-start.36 = (bf16[192,768]{1,0:T(8,128)(2,1)S(1)}, bf16[192,768]{1,0:T(8,128)(2,1)}, u32[]{:S(2)}, u32[]{:S(2)}) collective-permute-start(bf16[192,768]{1,0:T(8,128)(2,1)S(1)} %bitcast.491), channel_id=1, source_target_pairs={{0,4},{4,0},{8,12},{12,8},{16,20},{20,16},{24,28},{28,24},{1,5},{5... | collective-permute-start | bytes 884744 | tf_op jit(solution)/shard_map/ppermute | solution.py:916
  302.0 11.9 %collective-permute-start.39 = (bf16[384,768]{1,0:T(8,128)(2,1)}, bf16[384,768]{1,0:T(8,128)(2,1)S(1)}, u32[]{:S(2)}, u32[]{:S(2)}) collective-permute-start(bf16[384,768]{1,0:T(8,128)(2,1)} %bitcast.172), channel_id=1, source_target_pairs={{0,1},{1,0},{2,3},{3,2},{4,5},{5,4},{6,7},{7,6},{8,9},{9,8},{10,11... | collective-permute-start | bytes 1769480 | tf_op jit(solution)/shard_map/ppermute | solution.py:916
  302.1 11.8 %collective-permute-start.40 = (bf16[384,768]{1,0:T(8,128)(2,1)}, bf16[384,768]{1,0:T(8,128)(2,1)S(1)}, u32[]{:S(2)}, u32[]{:S(2)}) collective-permute-start(bf16[384,768]{1,0:T(8,128)(2,1)} %bitcast.174), channel_id=1, source_target_pairs={{0,1},{1,0},{2,3},{3,2},{4,5},{5,4},{6,7},{7,6},{8,9},{9,8},{10,11... | collective-permute-start | bytes 1769480 | tf_op jit(solution)/shard_map/ppermute | solution.py:916
  302.6 11.3 %collective-permute-start.41 = (bf16[256,768]{1,0:T(8,128)(2,1)S(1)}, bf16[256,768]{1,0:T(8,128)(2,1)S(1)}, u32[]{:S(2)}, u32[]{:S(2)}) collective-permute-start(bf16[256,768]{1,0:T(8,128)(2,1)S(1)} %bitcast.484), channel_id=1, source_target_pairs={{0,2},{1,3},{2,0},{3,1},{4,6},{5,7},{6,4},{7,5},{8,10},{9,11},{10,... | collective-permute-start | bytes 1179656 | tf_op jit(solution)/shard_map/ppermute | solution.py:916
  303.6 10.3 %collective-permute-start.42 = (bf16[240,768]{1,0:T(8,128)(2,1)S(1)}, bf16[240,768]{1,0:T(8,128)(2,1)S(1)}, u32[]{:S(2)}, u32[]{:S(2)}) collective-permute-start(bf16[240,768]{1,0:T(8,128)(2,1)S(1)} %bitcast.487), channel_id=1, source_target_pairs={{0,8},{4,12},{8,0},{12,4},{16,24},{20,28},{24,16},{28,20},{1,9},{5... | collective-permute-start | bytes 1105928 | tf_op jit(solution)/shard_map/ppermute | solution.py:916
  315.3 7.9 %collective-permute-start.48 = (bf16[128,768]{1,0:T(8,128)(2,1)S(1)}, bf16[128,768]{1,0:T(8,128)(2,1)S(1)}, u32[]{:S(2)}, u32[]{:S(2)}) collective-permute-start(bf16[128,768]{1,0:T(8,128)(2,1)S(1)} %bitcast.501), channel_id=1, source_target_pairs={{0,4},{4,0},{8,12},{12,8},{16,20},{20,16},{24,28},{28,24},{1,5},{5... | collective-permute-start | bytes 589832 | tf_op jit(solution)/shard_map/ppermute | solution.py:916
  316.5 9.9 %collective-permute-start.43 = (bf16[192,768]{1,0:T(8,128)(2,1)S(1)}, bf16[192,768]{1,0:T(8,128)(2,1)S(1)}, u32[]{:S(2)}, u32[]{:S(2)}) collective-permute-start(bf16[192,768]{1,0:T(8,128)(2,1)S(1)} %bitcast.490), channel_id=1, source_target_pairs={{0,2},{1,3},{2,0},{3,1},{4,6},{5,7},{6,4},{7,5},{8,10},{9,11},{10,... | collective-permute-start | bytes 884744 | tf_op jit(solution)/shard_map/ppermute | solution.py:916
  317.8 9.7 %collective-permute-start.44 = (bf16[192,768]{1,0:T(8,128)(2,1)S(1)}, bf16[192,768]{1,0:T(8,128)(2,1)S(1)}, u32[]{:S(2)}, u32[]{:S(2)}) collective-permute-start(bf16[192,768]{1,0:T(8,128)(2,1)S(1)} %bitcast.489), channel_id=1, source_target_pairs={{0,4},{4,0},{8,12},{12,8},{16,20},{20,16},{24,28},{28,24},{1,5},{5... | collective-permute-start | bytes 884744 | tf_op jit(solution)/shard_map/ppermute | solution.py:916
  318.4 12.9 %collective-permute-start.45 = (bf16[256,768]{1,0:T(8,128)(2,1)S(1)}, bf16[256,768]{1,0:T(8,128)(2,1)S(1)}, u32[]{:S(2)}, u32[]{:S(2)}) collective-permute-start(bf16[256,768]{1,0:T(8,128)(2,1)S(1)} %pad_maximum_fusion.15), channel_id=1, source_target_pairs={{0,3},{1,2},{2,1},{3,0},{4,7},{5,6},{6,5},{7,4},{8,11},{9,10},{10,... | collective-permute-start | bytes 1179656 | tf_op jit(solution)/shard_map/ppermute | solution.py:891
  318.5 26.6 %collective-permute-start.52 = (bf16[120,768]{1,0:T(8,128)(2,1)S(1)}, bf16[120,768]{1,0:T(8,128)(2,1)S(1)}, u32[]{:S(2)}, u32[]{:S(2)}) collective-permute-start(bf16[120,768]{1,0:T(8,128)(2,1)S(1)} %fusion.45), channel_id=1, source_target_pairs={{0,16},{4,20},{8,24},{12,28},{16,0},{20,4},{24,8},{28,12},{1,17},{... | collective-permute-start | bytes 552968 | tf_op jit(solution)/shard_map/ppermute | solution.py:916
  331.4 6.4 %collective-permute-start.46 = (bf16[96,768]{1,0:T(8,128)(2,1)S(1)}, bf16[96,768]{1,0:T(8,128)(2,1)S(1)}, u32[]{:S(2)}, u32[]{:S(2)}) collective-permute-start(bf16[96,768]{1,0:T(8,128)(2,1)S(1)} %bitcast.509), channel_id=1, source_target_pairs={{0,4},{4,0},{8,12},{12,8},{16,20},{20,16},{24,28},{28,24},{1,5},{5... | collective-permute-start | bytes 442376 | tf_op jit(solution)/shard_map/ppermute | solution.py:916
  332.2 6.7 %collective-permute-start.47 = (bf16[96,768]{1,0:T(8,128)(2,1)S(1)}, bf16[96,768]{1,0:T(8,128)(2,1)S(1)}, u32[]{:S(2)}, u32[]{:S(2)}) collective-permute-start(bf16[96,768]{1,0:T(8,128)(2,1)S(1)} %bitcast.508), channel_id=1, source_target_pairs={{0,2},{1,3},{2,0},{3,1},{4,6},{5,7},{6,4},{7,5},{8,10},{9,11},{10,... | collective-permute-start | bytes 442376 | tf_op jit(solution)/shard_map/ppermute | solution.py:916
  339.1 7.0 %collective-permute-start.49 = (bf16[80,768]{1,0:T(8,128)(2,1)S(1)}, bf16[80,768]{1,0:T(8,128)(2,1)S(1)}, u32[]{:S(2)}, u32[]{:S(2)}) collective-permute-start(bf16[80,768]{1,0:T(8,128)(2,1)S(1)} %get-tuple-element.422), channel_id=1, source_target_pairs={{0,8},{4,12},{8,0},{12,4},{16,24},{20,28},{24,16},{28,20},{1,9},{5... | collective-permute-start | bytes 368648 | tf_op jit(solution)/shard_map/ppermute | solution.py:1003
  340.8 12.4 %collective-permute-start.50 = (bf16[80,768]{1,0:T(8,128)(2,1)S(1)}, bf16[80,768]{1,0:T(8,128)(2,1)S(1)}, u32[]{:S(2)}, u32[]{:S(2)}) collective-permute-start(bf16[80,768]{1,0:T(8,128)(2,1)S(1)} %get-tuple-element.423), channel_id=1, source_target_pairs={{0,16},{4,20},{8,24},{12,28},{16,0},{20,4},{24,8},{28,12},{1,17},{... | collective-permute-start | bytes 368648 | tf_op jit(solution)/shard_map/ppermute | solution.py:1003
  341.8 11.4 %collective-permute-start.51 = (bf16[80,768]{1,0:T(8,128)(2,1)S(1)}, bf16[80,768]{1,0:T(8,128)(2,1)S(1)}, u32[]{:S(2)}, u32[]{:S(2)}) collective-permute-start(bf16[80,768]{1,0:T(8,128)(2,1)S(1)} %get-tuple-element.424), channel_id=1, source_target_pairs={{0,24},{4,28},{8,16},{12,20},{16,8},{20,12},{24,0},{28,4},{1,25},{... | collective-permute-start | bytes 368648 | tf_op jit(solution)/shard_map/ppermute | solution.py:1003
  (46 other events, 198.6 us)
Sparse Core Ops, SparseCore 0:
  11.0 124.4 all-gather.2
  256.7 28.0 reduce-scatter.1
